TPU v7x, 256 devices: a whole 4x4x8 slice. The times are simulated.
256 devices in a mesh: dp: 8 (over z), expert: 32 (over y, x, core).
Axes of the slice: x: 4, y: 4, z: 8, core: 2. Of those that a mesh axis runs over, the one named last changes fastest.
Arguments:
- tokens: bfloat16 [32768, 2048], P(('dp', 'expert')), may hold values from -6 to 6
- out_grad: bfloat16 [32768, 2048], P(('dp', 'expert')), may hold values from -6 to 6
- expert_ids: int32 [32768, 6], P(('dp', 'expert')), may hold values from 0 to 31, all different within a row; in each aligned block of 128 rows (0 to 127, 128 to 255, ...) at most 25 rows name the same one
- gate_weights: float32 [32768, 6], P(('dp', 'expert')), may hold values from 0.05 to 1
- trained: int32 [8], replicated, may hold values from 0 to 31, as said below
- w_in: bfloat16 [32, 2048, 1408], P('expert'), may hold values from -0.125 to 0.125
- w_down: bfloat16 [32, 704, 2048], P('expert'), may hold values from -0.21875 to 0.21875
- saved: bfloat16 [8, 32, 800, 1408], P('dp', 'expert'), may hold values from -6 to 6
Outputs:
- in_grad: bfloat16 [32768, 2048], P(('dp', 'expert'))
- weight_grad: bfloat16 [32, 2048, 2112], P('expert', 'dp')
Inputs may be any that keep to these rules, and one draw needn't show every extreme that they name: `expert_ids`: among the 128 tokens of one device no expert is named more than 25 times, a bound that some block reaches; a token names 6 different experts. `trained`: 8 different expert ids; the ids 0 and 31 are always among them.
All inputs are finite; a program needn't handle non-finite values.
Results may differ from a plain program's by a relative error of at most 0.017.
Values may be sent and summed in bfloat16 or wider, within the bound.
A program may use at most 128 MiB of HBM per device.

v0:
```python
import jax
import jax.numpy as jnp
from jax import lax
from jax.sharding import PartitionSpec as P


def per_device(tokens, out_grad, expert_ids, gate_weights, trained, w_in, w_down, saved):
    groups = lax.axis_size("expert")
    local_count = w_in.shape[0]
    experts = local_count * groups
    tok_count = tokens.shape[0]
    fanout = expert_ids.shape[1]
    slot_total = saved.shape[2]
    capacity = slot_total // groups
    hidden_units = w_down.shape[1]
    f32, bf16 = jnp.float32, jnp.bfloat16

    flat_ids = expert_ids.reshape(-1)
    onehot = (flat_ids[:, None] == jnp.arange(experts, dtype=jnp.int32)[None, :]).astype(jnp.int32)
    slot_rank = jnp.sum(jnp.cumsum(onehot, axis=0) * onehot, axis=1) - 1
    ids4 = flat_ids.reshape(1, 1, tok_count, fanout)
    rank4 = slot_rank.reshape(1, 1, tok_count, fanout)
    sel = (ids4 == jnp.arange(experts, dtype=jnp.int32)[:, None, None, None]) & (
        rank4 == jnp.arange(capacity, dtype=jnp.int32)[None, :, None, None]
    )
    tok_sel = jnp.any(sel, axis=3)
    tok_sel_b = tok_sel.astype(bf16)
    gate_slot = jnp.sum(jnp.where(sel, gate_weights[None, None, :, :], 0.0), axis=(2, 3))

    pick = (((2,), (0,)), ((), ()))
    og_slot = lax.dot_general(tok_sel_b, out_grad, pick, preferred_element_type=f32)
    s_send = (gate_slot[:, :, None] * og_slot).astype(bf16)
    x_send = lax.dot_general(tok_sel_b, tokens, pick, preferred_element_type=f32).astype(bf16)

    s_recv = lax.all_to_all(s_send, "expert", 0, 0, tiled=True)
    x_send, s_recv = lax.optimization_barrier((x_send, s_recv))
    x_recv = lax.all_to_all(x_send, "expert", 0, 0, tiled=True)

    saved3 = saved.reshape(groups, capacity, 2 * hidden_units)
    gate_pre = saved3[:, :, :hidden_units].astype(f32)
    up_pre = saved3[:, :, hidden_units:].astype(f32)
    hidden_grad = lax.dot_general(
        s_recv, w_down[0], (((2,), (1,)), ((), ())), preferred_element_type=f32
    )
    sigmoid_gate = jax.nn.sigmoid(gate_pre)
    activated = gate_pre * sigmoid_gate
    pre_grad = jnp.concatenate(
        [
            hidden_grad * up_pre * sigmoid_gate * (1.0 + gate_pre * (1.0 - sigmoid_gate)),
            hidden_grad * activated,
        ],
        axis=2,
    ).astype(bf16)
    hidden = (activated * up_pre).astype(bf16)
    slot_grads = lax.dot_general(
        pre_grad, w_in[0], (((2,), (1,)), ((), ())), preferred_element_type=f32
    ).astype(bf16)

    trained_flag = jnp.any(trained == lax.axis_index("expert")).astype(f32)
    over_slots = (((0, 1), (0, 1)), ((), ()))
    grad_down = lax.dot_general(s_recv, hidden, over_slots, preferred_element_type=f32)
    down_block = lax.psum_scatter(
        (grad_down * trained_flag).astype(bf16), "dp", scatter_dimension=0, tiled=True
    )

    slot_grads, x_recv = lax.optimization_barrier((slot_grads, x_recv))
    arrived = lax.all_to_all(slot_grads, "expert", 0, 0, tiled=True)

    grad_in = lax.dot_general(x_recv, pre_grad, over_slots, preferred_element_type=f32)
    in_block = lax.psum_scatter(
        (grad_in * trained_flag).astype(bf16), "dp", scatter_dimension=0, tiled=True
    )

    in_grad = lax.dot_general(
        tok_sel_b, arrived, (((0, 1), (0, 1)), ((), ())), preferred_element_type=f32
    ).astype(bf16)
    weight_block = jnp.concatenate([in_block, down_block], axis=1)
    return (in_grad, weight_block[None])


def solution(mesh):
    return jax.shard_map(
        per_device,
        mesh=mesh,
        in_specs=(
            P(("dp", "expert"), None),
            P(("dp", "expert"), None),
            P(("dp", "expert"), None),
            P(("dp", "expert"), None),
            P(),
            P("expert", None, None),
            P("expert", None, None),
            P("dp", "expert", None, None),
        ),
        out_specs=(P(("dp", "expert"), None), P("expert", "dp", None)),
        check_vma=False,
    )
```

profile of v0, /device:TPU:1, one launch (start us, length us, event | category | flops | bytes accessed | tf_op | source)
XLA Modules:
  0.0 242.3 jit_solution(7086879945517812808)
XLA Ops:
  9.1 1.7 reduce-window.6
  12.9 2.1 multiply_convert_fusion
  15.0 3.9 %copy.58 = bf16[32,25,2048]{2,1,0:T(8,128)(2,1)} copy(bf16[32,25,2048]{2,0,1:T(8,128)(2,1)S(1)} %multiply_convert_fusion) | data formatting | bytes 6553600 | tf_op jit(solution)/shard_map/convert_element_type | solution.py:32
  18.8 8.8 %all-to-all-start = ((bf16[32,25,2048]{2,1,0:T(8,128)(2,1)}), bf16[32,25,2048]{2,1,0:T(8,128)(2,1)}, u32[]{:S(2)}, u32[]{:S(2)}) async-start(bf16[32,25,2048]{2,1,0:T(8,128)(2,1)} %copy.58), calls=%async_computation | async-start | bytes 8388608 | tf_op jit(solution)/shard_map/all_to_all | solution.py:35
  28.9 4.3 %reshape.50 = bf16[32,25,1408]{2,1,0:T(8,128)(2,1)} reshape(bf16[1,1,800,1408]{3,2,1,0:T(8,128)(2,1)} %param.15) | data formatting | bytes 4505600 | tf_op jit(solution)/shard_map/reshape | solution.py:39
  33.2 3.8 %convolution_convert_fusion = bf16[32,25,2048]{2,0,1:T(8,128)(2,1)} fusion(pred[32,25,128]{2,0,1:T(8,128)(4,1)S(1)} %and_reduce_fusion, bf16[128,2048]{1,0:T(8,128)(2,1)} %param.8), kind=kOutput, calls=%fused_computation.11 | convolution fusion | flops 421068800 | bytes 3903488 | tf_op jit(solution)/shard_map/dot_general | solution.py:33
  37.1 2.5 %fusion.34 = (bf16[32,25,704]{2,1,0:T(8,128)(2,1)}, bf16[32,25,704]{2,1,0:T(8,128)(2,1)}) fusion(bf16[32,25,1408]{2,1,0:T(8,128)(2,1)S(1)} %copy-done.2), kind=kLoop, calls=%fused_computation.51 | loop fusion | bytes 4505600 | tf_op jit(solution)/shard_map/slice | solution.py:41
  39.6 38.3 %all-to-all-done = bf16[32,25,2048]{2,1,0:T(8,128)(2,1)} async-done(((bf16[32,25,2048]{2,1,0:T(8,128)(2,1)}), bf16[32,25,2048]{2,1,0:T(8,128)(2,1)}, u32[]{:S(2)}, u32[]{:S(2)}) %all-to-all-start) | async-done | bytes 3276832 | tf_op jit(solution)/shard_map/all_to_all | solution.py:35
  77.9 5.9 %copy.62 = bf16[32,25,2048]{2,1,0:T(8,128)(2,1)} copy(bf16[32,25,2048]{2,0,1:T(8,128)(2,1)} %convolution_convert_fusion) | data formatting | bytes 6553600 | tf_op jit(solution)/shard_map/optimization_barrier | solution.py:36
  83.8 8.0 %all-to-all-start.1 = ((bf16[32,25,2048]{2,1,0:T(8,128)(2,1)}), bf16[32,25,2048]{2,1,0:T(8,128)(2,1)}, u32[]{:S(2)}, u32[]{:S(2)}) async-start(bf16[32,25,2048]{2,1,0:T(8,128)(2,1)} %copy.62), calls=%async_computation.1 | async-start | bytes 8388608 | tf_op jit(solution)/shard_map/all_to_all | solution.py:37
  92.0 11.6 %fusion.18 = (bf16[32,25,704]{2,0,1:T(8,128)(2,1)}, bf16[32,25,704]{2,0,1:T(8,128)(2,1)}, bf16[32,25,704]{2,0,1:T(8,128)(2,1)S(1)}) fusion(bf16[32,25,704]{2,1,0:T(8,128)(2,1)} %get-tuple-element.23, bf16[32,25,704]{2,1,0:T(8,128)(2,1)} %get-tuple-element.24, bf16[1,704,2048]{2,1,0:T(8,128)(2,1)S(1)} %copy-done, bf16[32,25,2048]{2,1,0:T(8,128)(2,1)} %all-to-all-done), kind=kOutput, calls=%fused_computation.25 | convolution fusion | flops 2316441600 | bytes 11792384 | tf_op jit(solution)/shard_map/dot_general | solution.py:42
  103.6 7.2 %fusion.1 = bf16[2048,704]{0,1:T(8,128)(2,1)} fusion(bf16[32,25,2048]{2,1,0:T(8,128)(2,1)} %all-to-all-done, f32[]{:T(128)S(6)} %convert_element_type.44, bf16[32,25,704]{2,0,1:T(8,128)(2,1)S(1)} %get-tuple-element.22), kind=kOutput, calls=%fused_computation.4 | convolution fusion | flops 2309750784 | bytes 7286788 | tf_op jit(solution)/shard_map/dot_general | solution.py:61
  111.1 2.4 pad_maximum_fusion
  113.4 9.3 %fusion.4 = bf16[32,25,2048]{2,0,1:T(8,128)(2,1)} fusion(bf16[32,25,1408]{2,0,1:T(8,128)(2,1)S(1)} %pad_maximum_fusion, bf16[1,2048,1408]{2,1,0:T(8,128)(2,1)} %param.13), kind=kOutput, calls=%fused_computation.10 | convolution fusion | flops 4615372800 | bytes 11296768 | tf_op jit(solution)/shard_map/dot_general | solution.py:55
  122.7 19.4 %all-to-all-done.1 = bf16[32,25,2048]{2,1,0:T(8,128)(2,1)} async-done(((bf16[32,25,2048]{2,1,0:T(8,128)(2,1)}), bf16[32,25,2048]{2,1,0:T(8,128)(2,1)}, u32[]{:S(2)}, u32[]{:S(2)}) %all-to-all-start.1) | async-done | bytes 3276832 | tf_op jit(solution)/shard_map/all_to_all | solution.py:37
  142.2 11.4 %fusion = bf16[2048,1408]{1,0:T(8,128)(2,1)} fusion(bf16[32,25,2048]{2,1,0:T(8,128)(2,1)} %all-to-all-done.1, f32[]{:T(128)S(6)} %convert_element_type.44, bf16[32,25,1408]{2,0,1:T(8,128)(2,1)S(1)} %pad_maximum_fusion), kind=kOutput, calls=%fused_computation.1 | convolution fusion | flops 4619501568 | bytes 11296772 | tf_op jit(solution)/shard_map/dot_general | solution.py:69
  153.6 5.9 %copy.63 = bf16[32,25,2048]{2,1,0:T(8,128)(2,1)} copy(bf16[32,25,2048]{2,0,1:T(8,128)(2,1)} %fusion.4) | data formatting | bytes 6553600 | tf_op jit(solution)/shard_map/optimization_barrier | solution.py:66
  159.5 7.9 %all-to-all-start.2 = ((bf16[32,25,2048]{2,1,0:T(8,128)(2,1)}), bf16[32,25,2048]{2,1,0:T(8,128)(2,1)}, u32[]{:S(2)}, u32[]{:S(2)}) async-start(bf16[32,25,2048]{2,1,0:T(8,128)(2,1)} %copy.63), calls=%async_computation.2 | async-start | bytes 8388608 | tf_op jit(solution)/shard_map/all_to_all | solution.py:67
  167.5 1.2 copy.67
  168.6 49.2 %all-to-all-done.2 = bf16[32,25,2048]{2,1,0:T(8,128)(2,1)} async-done(((bf16[32,25,2048]{2,1,0:T(8,128)(2,1)}), bf16[32,25,2048]{2,1,0:T(8,128)(2,1)}, u32[]{:S(2)}, u32[]{:S(2)}) %all-to-all-start.2) | async-done | bytes 3276832 | tf_op jit(solution)/shard_map/all_to_all | solution.py:67
  217.8 5.3 %fusion.25 = bf16[128,2048]{1,0:T(8,128)(2,1)} fusion(pred[32,25,128]{2,0,1:T(8,128)(4,1)S(1)} %and_reduce_fusion, bf16[32,25,2048]{2,1,0:T(8,128)(2,1)} %all-to-all-done.2), kind=kOutput, calls=%fused_computation.33 | convolution fusion | flops 419692544 | bytes 3903488 | tf_op jit(solution)/shard_map/dot_general | solution.py:74
  223.1 7.9 %reduce-scatter.3.cloned.1.call-done = bf16[256,1408]{1,0:T(8,128)(2,1)} async-done(((bf16[2048,1408]{1,0:T(8,128)(2,1)}), bf16[256,1408]{1,0:T(8,128)(2,1)}) %reduce-scatter.3.cloned.1.call-update) | async-done | bytes 720912 | tf_op jit(solution)/shard_map/reduce_scatter | solution.py:70
  231.0 2.2 maximum_bitcast_fusion
  233.2 2.3 copy.68
  (28 shorter events, 5.1 us)
Async XLA Ops:
  7.2 84.8 %copy-start = (bf16[1,704,2048]{2,1,0:T(8,128)(2,1)S(1)}, bf16[1,704,2048]{2,1,0:T(8,128)(2,1)}, u32[]{:S(2)}) copy-start(bf16[1,704,2048]{2,1,0:T(8,128)(2,1)} %param.14) | copy-start | bytes 8650756
  18.8 8.8 %copy-start.3 = (s32[8]{0:T(128)S(1)}, s32[8]{0:T(128)}, u32[]{:S(2)}) copy-start(s32[8]{0:T(128)} %param.12) | copy-start | bytes 100
  18.8 59.0 %all-to-all-start = ((bf16[32,25,2048]{2,1,0:T(8,128)(2,1)}), bf16[32,25,2048]{2,1,0:T(8,128)(2,1)}, u32[]{:S(2)}, u32[]{:S(2)}) async-start(bf16[32,25,2048]{2,1,0:T(8,128)(2,1)} %copy.58), calls=%async_computation | async-start | bytes 8388608 | tf_op jit(solution)/shard_map/all_to_all | solution.py:35
  33.2 3.8 %copy-start.2 = (bf16[32,25,1408]{2,1,0:T(8,128)(2,1)S(1)}, bf16[32,25,1408]{2,1,0:T(8,128)(2,1)}, u32[]{:S(2)}) copy-start(bf16[32,25,1408]{2,1,0:T(8,128)(2,1)} %reshape.50) | copy-start | bytes 6758404
  83.8 58.4 %all-to-all-start.1 = ((bf16[32,25,2048]{2,1,0:T(8,128)(2,1)}), bf16[32,25,2048]{2,1,0:T(8,128)(2,1)}, u32[]{:S(2)}, u32[]{:S(2)}) async-start(bf16[32,25,2048]{2,1,0:T(8,128)(2,1)} %copy.62), calls=%async_computation.1 | async-start | bytes 8388608 | tf_op jit(solution)/shard_map/all_to_all | solution.py:37
  91.8 75.7 %reduce-scatter.5.cloned.1.call-start = ((), (), s32[]{:S(2)}) async-start(), calls=%async_computation.6 | async-start | bytes 3244032 | tf_op jit(solution)/shard_map/reduce_scatter | solution.py:62
  110.8 120.2 %reduce-scatter.3.cloned.1.call-start = ((), (), s32[]{:S(2)}) async-start(), calls=%async_computation.5 | async-start | bytes 6488064 | tf_op jit(solution)/shard_map/reduce_scatter | solution.py:70
  159.5 58.3 %all-to-all-start.2 = ((bf16[32,25,2048]{2,1,0:T(8,128)(2,1)}), bf16[32,25,2048]{2,1,0:T(8,128)(2,1)}, u32[]{:S(2)}, u32[]{:S(2)}) async-start(bf16[32,25,2048]{2,1,0:T(8,128)(2,1)} %copy.63), calls=%async_computation.2 | async-start | bytes 8388608 | tf_op jit(solution)/shard_map/all_to_all | solution.py:67
  217.8 17.7 %copy-start.1 = (bf16[1,704,2048]{2,1,0:T(8,128)(2,1)S(1)}, bf16[1,704,2048]{2,1,0:T(8,128)(2,1)}, u32[]{:S(2)}) copy-start(bf16[1,704,2048]{2,1,0:T(8,128)(2,1)} %param.14) | copy-start | bytes 8650756
Sparse Core Ops, SparseCore 0:
  110.9 44.1 reduce-scatter.4
  157.6 73.2 reduce-scatter.2
where the time goes:
time: 243 us; the launch traced here: 242 us
  waiting for transfers between devices  115 us (47%)
  matrix products  50.7 us (21%)
  local copies, waits for them, and re-layouts  27.5 us (11%)
  starting transfers between devices  25.2 us (10%)
  between operations  14.8 us (6%)
  other arithmetic  9.32 us (4%)
    all_to_all x1, waiting for transfers between devices, per_device(): arrived = lax.all_to_all(slot_grads, 'expert', 0, 0, tiled=True)  49.2 us
    all_to_all x1, waiting for transfers between devices, per_device(): s_recv = lax.all_to_all(s_send, 'expert', 0, 0, tiled=True)  38.3 us
    all_to_all x1, waiting for transfers between devices, per_device(): x_recv = lax.all_to_all(x_send, 'expert', 0, 0, tiled=True)  19.4 us
    dot_general x1, matrix products, per_device(): lax.dot_general(s_recv, w_down[0], (((2,), (1,)), ((), ())), preferred_el...  11.6 us
    dot_general x1, matrix products, per_device(): lax.dot_general(x_recv, pre_grad, over_slots, preferred_element_type=f32)  11.4 us
    dot_general x1, matrix products, per_device(): lax.dot_general(pre_grad, w_in[0], (((2,), (1,)), ((), ())), preferred_el...  9.31 us
    all_to_all x1, starting transfers between devices, per_device(): s_recv = lax.all_to_all(s_send, 'expert', 0, 0, tiled=True)  8.78 us
    all_to_all x1, starting transfers between devices, per_device(): x_recv = lax.all_to_all(x_send, 'expert', 0, 0, tiled=True)  7.96 us
  transfers between devices with their start and end apart: 5, of which 4 were waited for; matrix products, arithmetic and copies ran while one was open for 27% of the time, Pallas kernels for 0%

commit v1 on v0

--- a/solution.py
+++ b/solution.py
@@ -1,7 +1,70 @@
 import jax
 import jax.numpy as jnp
 from jax import lax
+from jax.experimental import pallas as pl
+from jax.experimental.pallas import tpu as pltpu
 from jax.sharding import PartitionSpec as P
+
+MESH = pl.DeviceIdType.MESH
+
+
+def _exchange_kernel(send_ref, recv_ref, send_sems, recv_sems, local_sem):
+    n = send_ref.shape[0]
+    me = lax.axis_index("expert")
+    row = lax.axis_index("dp")
+    barrier = pltpu.get_barrier_semaphore()
+
+    def greet(k, carry):
+        peer = lax.rem(me + k, n)
+        pl.semaphore_signal(barrier, 1, device_id=(row, peer), device_id_type=MESH)
+        return carry
+
+    lax.fori_loop(1, n, greet, 0)
+    pl.semaphore_wait(barrier, n - 1)
+    local = pltpu.make_async_copy(send_ref.at[me], recv_ref.at[me], local_sem)
+    local.start()
+
+    def outgoing(peer):
+        return pltpu.make_async_remote_copy(
+            send_ref.at[peer], recv_ref.at[me], send_sems.at[peer], recv_sems.at[me],
+            device_id=(row, peer), device_id_type=MESH,
+        )
+
+    def incoming(src):
+        return pltpu.make_async_remote_copy(
+            send_ref.at[src], recv_ref.at[src], send_sems.at[src], recv_sems.at[src],
+            device_id=(row, src), device_id_type=MESH,
+        )
+
+    def start(k, carry):
+        outgoing(lax.rem(me + k, n)).start()
+        return carry
+
+    lax.fori_loop(1, n, start, 0)
+
+    def finish(k, carry):
+        outgoing(lax.rem(me + k, n)).wait_send()
+        incoming(lax.rem(me + n - k, n)).wait_recv()
+        return carry
+
+    lax.fori_loop(1, n, finish, 0)
+    local.wait()
+
+
+def exchange(x, collective):
+    n = x.shape[0]
+    return pl.pallas_call(
+        _exchange_kernel,
+        out_shape=jax.ShapeDtypeStruct(x.shape, x.dtype),
+        in_specs=[pl.BlockSpec(memory_space=pl.ANY)],
+        out_specs=pl.BlockSpec(memory_space=pl.ANY),
+        scratch_shapes=[
+            pltpu.SemaphoreType.DMA((n,)),
+            pltpu.SemaphoreType.DMA((n,)),
+            pltpu.SemaphoreType.DMA(()),
+        ],
+        compiler_params=pltpu.CompilerParams(collective_id=collective, has_side_effects=True),
+    )(x)
 
 
 def per_device(tokens, out_grad, expert_ids, gate_weights, trained, w_in, w_down, saved):
@@ -32,9 +95,7 @@
     s_send = (gate_slot[:, :, None] * og_slot).astype(bf16)
     x_send = lax.dot_general(tok_sel_b, tokens, pick, preferred_element_type=f32).astype(bf16)
 
-    s_recv = lax.all_to_all(s_send, "expert", 0, 0, tiled=True)
-    x_send, s_recv = lax.optimization_barrier((x_send, s_recv))
-    x_recv = lax.all_to_all(x_send, "expert", 0, 0, tiled=True)
+    s_recv = exchange(s_send, 0)
 
     saved3 = saved.reshape(groups, capacity, 2 * hidden_units)
     gate_pre = saved3[:, :, :hidden_units].astype(f32)
@@ -59,12 +120,13 @@
     trained_flag = jnp.any(trained == lax.axis_index("expert")).astype(f32)
     over_slots = (((0, 1), (0, 1)), ((), ()))
     grad_down = lax.dot_general(s_recv, hidden, over_slots, preferred_element_type=f32)
-    down_block = lax.psum_scatter(
-        (grad_down * trained_flag).astype(bf16), "dp", scatter_dimension=0, tiled=True
-    )
+    down_part = (grad_down * trained_flag).astype(bf16)
+    x_send, down_part = lax.optimization_barrier((x_send, down_part))
+    down_block = lax.psum_scatter(down_part, "dp", scatter_dimension=0, tiled=True)
+    x_recv = exchange(x_send, 1)
 
     slot_grads, x_recv = lax.optimization_barrier((slot_grads, x_recv))
-    arrived = lax.all_to_all(slot_grads, "expert", 0, 0, tiled=True)
+    arrived = exchange(slot_grads, 2)
 
     grad_in = lax.dot_general(x_recv, pre_grad, over_slots, preferred_element_type=f32)
     in_block = lax.psum_scatter(

time: 243 us -> 307 us (1.26)
  Pallas kernels: 0 us -> 220 us
  waiting for transfers between devices: 115 us -> 0.06 us
  starting transfers between devices: 25.2 us -> 0.26 us
  local copies, waits for them, and re-layouts: 27.5 us -> 14 us
  matrix products: 50.7 us -> 45.3 us
    pallas_call x0 -> x3, Pallas kernels: none -> 220 us  [exchange(): pl.pallas_call(_exchange_kernel, out_shape=jax.ShapeDtypeStruct(x.shape,...]
    all_to_all x3 -> x0, waiting for transfers between devices: 107 us -> none  [the longest x1 49.2 us: per_device(): arrived = lax.all_to_all(slot_grads, 'expert', 0, 0, tiled=True)]
    all_to_all x3 -> x0, starting transfers between devices: 24.7 us -> none  [the longest x1 8.78 us: per_device(): s_recv = lax.all_to_all(s_send, 'expert', 0, 0, tiled=True)]
    optimization_barrier x2 -> x0, local copies, waits for them, and re-layouts: 11.8 us -> none  [the longest x1 5.92 us: per_device(): x_send, s_recv = lax.optimization_barrier((x_send, s_recv))]
    reduce_scatter x1, waiting for transfers between devices: 7.9 us -> 0.02 us  [per_device(): lax.psum_scatter((grad_in * trained_flag).astype(bf16), 'dp', scatter_dim...]
    convert_element_type x1 -> x0, local copies, waits for them, and re-layouts: 3.87 us -> none  [per_device(): s_send = (gate_slot[:, :, None] * og_slot).astype(bf16)]
  transfers between devices with their start and end apart: 5 -> 2, of which waited for: 4 -> 0; matrix products, arithmetic and copies ran while one was open for 27% -> 9% of each run, Pallas kernels for 0% -> 47%
where the time goes in v1:
time: 307 us; the launch traced here: 304 us
  Pallas kernels  220 us (72%)
  matrix products  45.3 us (15%)
  between operations  14.9 us (5%)
  local copies, waits for them, and re-layouts  14 us (5%)
  other arithmetic  9.99 us (3%)
    pallas_call x3, Pallas kernels, exchange(): pl.pallas_call(_exchange_kernel, out_shape=jax.ShapeDtypeStruct(x.shape,...  220 us
    dot_general x1, matrix products, per_device(): lax.dot_general(pre_grad, w_in[0], (((2,), (1,)), ((), ())), preferred_el...  11 us
    dot_general x1, matrix products, per_device(): lax.dot_general(s_recv, w_down[0], (((2,), (1,)), ((), ())), preferred_el...  9.16 us
    dot_general x1, matrix products, per_device(): lax.dot_general(x_recv, pre_grad, over_slots, preferred_element_type=f32)  8.71 us
  transfers between devices with their start and end apart: 2, of which 0 were waited for; matrix products, arithmetic and copies ran while one was open for 9% of the time, Pallas kernels for 47%

profile of v1, /device:TPU:1, one launch (start us, length us, event | category | flops | bytes accessed | tf_op | source)
XLA Modules:
  0.0 304.4 jit_solution(18341053666531972160)
XLA Ops:
  7.2 0.9 iota_compare_fusion.3
  8.1 0.8 copy.37
  9.2 1.3 compare_reduce_fusion
  11.1 1.7 reduce-window.6
  12.9 0.3 slice_reduce_fusion
  13.5 0.2 and_reduce_fusion
  13.8 1.1 fusion.21
  15.0 4.3 %reshape.50 = bf16[32,25,1408]{2,1,0:T(8,128)(2,1)} reshape(bf16[1,1,800,1408]{3,2,1,0:T(8,128)(2,1)} %param.15) | data formatting | bytes 4505600 | tf_op jit(solution)/shard_map/reshape | solution.py:100
  19.2 4.6 %fusion.37 = (bf16[32,25,704]{2,1,0:T(8,128)(2,1)}, bf16[32,25,704]{2,1,0:T(8,128)(2,1)}) fusion(bf16[32,25,1408]{2,1,0:T(8,128)(2,1)} %reshape.50), kind=kLoop, calls=%fused_computation.54 | loop fusion | bytes 4505600 | tf_op jit(solution)/shard_map/slice | solution.py:102
  23.9 3.2 %multiply_convert_fusion.send_ref = bf16[32,25,2048]{2,1,0:T(8,128)(2,1)} fusion(f32[32,25]{1,0:T(8,128)S(1)} %copy.41, bf16[128,2048]{1,0:T(8,128)(2,1)S(1)} %copy-done.3, pred[32,25,128]{2,0,1:T(8,128)(4,1)S(1)} %and_reduce_fusion), kind=kOutput, calls=%fused_computation.2 | convolution fusion | flops 422707200 | bytes 3906688 | tf_op jit(solution)/shard_map/dot_general | solution.py:94
  27.1 75.7 %shard_map.95 = bf16[32,25,2048]{2,1,0:T(8,128)(2,1)} custom-call(bf16[32,25,2048]{2,1,0:T(8,128)(2,1)} %multiply_convert_fusion.send_ref), custom_call_target="tpu_custom_call" | custom-call | tf_op jit(solution)/shard_map/pallas_call | solution.py:56
  102.8 3.2 %convolution_convert_fusion.send_ref = bf16[32,25,2048]{2,1,0:T(8,128)(2,1)} fusion(bf16[128,2048]{1,0:T(8,128)(2,1)S(1)} %copy-done.4, pred[32,25,128]{2,0,1:T(8,128)(4,1)S(1)} %and_reduce_fusion), kind=kOutput, calls=%fused_computation.8 | convolution fusion | flops 421068800 | bytes 3903488 | tf_op jit(solution)/shard_map/dot_general | solution.py:96
  106.0 9.2 %fusion.19 = (bf16[32,25,704]{2,0,1:T(8,128)(2,1)}, bf16[32,25,704]{2,0,1:T(8,128)(2,1)}, bf16[32,25,704]{2,0,1:T(8,128)(2,1)S(1)}) fusion(bf16[32,25,704]{2,1,0:T(8,128)(2,1)} %get-tuple-element.19, bf16[32,25,704]{2,1,0:T(8,128)(2,1)} %get-tuple-element.20, bf16[1,704,2048]{2,1,0:T(8,128)(2,1)S(1)} %copy-done, bf16[32,25,2048]{2,1,0:T(8,128)(2,1)S(1)} %copy-done.1), kind=kOutput, calls=%fused_computation.26 | convolution fusion | flops 2316441600 | bytes 11792384 | tf_op jit(solution)/shard_map/dot_general | solution.py:103
  115.2 4.9 %fusion.1 = bf16[2048,704]{0,1:T(8,128)(2,1)} fusion(bf16[32,25,2048]{2,1,0:T(8,128)(2,1)S(1)} %copy-done.1, f32[]{:T(128)S(6)} %convert_element_type.44, bf16[32,25,704]{2,0,1:T(8,128)(2,1)S(1)} %get-tuple-element.18), kind=kOutput, calls=%fused_computation.4 | convolution fusion | flops 2309750784 | bytes 7286788 | tf_op jit(solution)/shard_map/dot_general | solution.py:122
  120.1 0.2 reduce-scatter.3.cloned.1.call-start
  120.4 71.5 %shard_map.96 = bf16[32,25,2048]{2,1,0:T(8,128)(2,1)} custom-call(bf16[32,25,2048]{2,1,0:T(8,128)(2,1)} %convolution_convert_fusion.send_ref), custom_call_target="tpu_custom_call" | custom-call | tf_op jit(solution)/shard_map/pallas_call | solution.py:56
  191.9 2.4 pad_maximum_fusion
  194.3 11.0 %fusion.4.send_ref = bf16[32,25,2048]{2,1,0:T(8,128)(2,1)} fusion(bf16[1,2048,1408]{2,1,0:T(8,128)(2,1)} %param.13, bf16[32,25,1408]{2,0,1:T(8,128)(2,1)S(1)} %pad_maximum_fusion), kind=kOutput, calls=%fused_computation.7 | convolution fusion | flops 4615372800 | bytes 11296768 | tf_op jit(solution)/shard_map/dot_general | solution.py:116
  205.3 8.7 %fusion = bf16[2048,1408]{1,0:T(8,128)(2,1)} fusion(bf16[32,25,2048]{2,1,0:T(8,128)(2,1)S(1)} %copy-done.2, f32[]{:T(128)S(6)} %convert_element_type.44, bf16[32,25,1408]{2,0,1:T(8,128)(2,1)S(1)} %pad_maximum_fusion), kind=kOutput, calls=%fused_computation.1 | convolution fusion | flops 4619501568 | bytes 11296772 | tf_op jit(solution)/shard_map/dot_general | solution.py:131
  214.0 72.7 %shard_map.97 = bf16[32,25,2048]{2,1,0:T(8,128)(2,1)} custom-call(bf16[32,25,2048]{2,1,0:T(8,128)(2,1)} %fusion.4.send_ref), custom_call_target="tpu_custom_call" | custom-call | tf_op jit(solution)/shard_map/pallas_call | solution.py:56
  286.8 5.1 %fusion.26 = bf16[128,2048]{1,0:T(8,128)(2,1)} fusion(pred[32,25,128]{2,0,1:T(8,128)(4,1)S(1)} %and_reduce_fusion, bf16[32,25,2048]{2,1,0:T(8,128)(2,1)} %shard_map.97), kind=kOutput, calls=%fused_computation.34 | convolution fusion | flops 419692544 | bytes 3903488 | tf_op jit(solution)/shard_map/dot_general | solution.py:136
  291.8 1.2 copy.51
  293.0 2.2 maximum_bitcast_fusion
  295.2 2.3 copy.52
  (25 shorter events, 0.8 us)
Async XLA Ops:
  7.2 98.8 %copy-start = (bf16[1,704,2048]{2,1,0:T(8,128)(2,1)S(1)}, bf16[1,704,2048]{2,1,0:T(8,128)(2,1)}, u32[]{:S(2)}) copy-start(bf16[1,704,2048]{2,1,0:T(8,128)(2,1)} %param.14) | copy-start | bytes 8650756
  7.2 284.7 %reduce-scatter.5.cloned.1.call-start = ((), (), s32[]{:S(2)}) async-start(), calls=%async_computation.3 | async-start | bytes 3244032 | tf_op jit(solution)/shard_map/reduce_scatter | solution.py:125
  19.2 4.6 %copy-start.3 = (bf16[128,2048]{1,0:T(8,128)(2,1)S(1)}, bf16[128,2048]{1,0:T(8,128)(2,1)}, u32[]{:S(2)}) copy-start(bf16[128,2048]{1,0:T(8,128)(2,1)} %param.9) | copy-start | bytes 1572868
  27.1 75.8 %copy-start.4 = (bf16[128,2048]{1,0:T(8,128)(2,1)S(1)}, bf16[128,2048]{1,0:T(8,128)(2,1)}, u32[]{:S(2)}) copy-start(bf16[128,2048]{1,0:T(8,128)(2,1)} %param.8) | copy-start | bytes 1572868
  102.8 3.2 %copy-start.1 = (bf16[32,25,2048]{2,1,0:T(8,128)(2,1)S(1)}, bf16[32,25,2048]{2,1,0:T(8,128)(2,1)}, u32[]{:S(2)}) copy-start(bf16[32,25,2048]{2,1,0:T(8,128)(2,1)} %shard_map.95) | copy-start | bytes 9830404
  120.1 172.9 %reduce-scatter.3.cloned.1.call-start = ((), (), s32[]{:S(2)}) async-start(), calls=%async_computation.2 | async-start | bytes 6488064 | tf_op jit(solution)/shard_map/reduce_scatter | solution.py:132
  194.2 11.0 %copy-start.2 = (bf16[32,25,2048]{2,1,0:T(8,128)(2,1)S(1)}, bf16[32,25,2048]{2,1,0:T(8,128)(2,1)}, u32[]{:S(2)}) copy-start(bf16[32,25,2048]{2,1,0:T(8,128)(2,1)} %shard_map.96) | copy-start | bytes 9830404
Sparse Core Ops, SparseCore 0:
  120.2 41.4 reduce-scatter.4
  214.1 70.1 reduce-scatter.2

commit v2 on v0

--- a/solution.py
+++ b/solution.py
@@ -1,7 +1,16 @@
 import jax
 import jax.numpy as jnp
 from jax import lax
+from jax.experimental.layout import Layout, with_layout_constraint
 from jax.sharding import PartitionSpec as P
+
+
+def row_major(x):
+    return with_layout_constraint(x, Layout(major_to_minor=tuple(range(x.ndim))))
+
+
+def col_major(x):
+    return with_layout_constraint(x, Layout(major_to_minor=(1, 0)))
 
 
 def per_device(tokens, out_grad, expert_ids, gate_weights, trained, w_in, w_down, saved):
@@ -32,18 +41,27 @@
     s_send = (gate_slot[:, :, None] * og_slot).astype(bf16)
     x_send = lax.dot_general(tok_sel_b, tokens, pick, preferred_element_type=f32).astype(bf16)
 
-    s_recv = lax.all_to_all(s_send, "expert", 0, 0, tiled=True)
-    x_send, s_recv = lax.optimization_barrier((x_send, s_recv))
-    x_recv = lax.all_to_all(x_send, "expert", 0, 0, tiled=True)
-
     saved3 = saved.reshape(groups, capacity, 2 * hidden_units)
     gate_pre = saved3[:, :, :hidden_units].astype(f32)
     up_pre = saved3[:, :, hidden_units:].astype(f32)
+    sigmoid_gate = jax.nn.sigmoid(gate_pre)
+    activated = gate_pre * sigmoid_gate
+    hidden = (activated * up_pre).astype(bf16)
+
+    s_recv = lax.all_to_all(row_major(s_send), "expert", 0, 0, tiled=True)
+    x_send, s_recv, hidden = lax.optimization_barrier((x_send, s_recv, hidden))
+    x_recv = lax.all_to_all(row_major(x_send), "expert", 0, 0, tiled=True)
+
+    trained_flag = jnp.any(trained == lax.axis_index("expert")).astype(f32)
+    over_slots = (((0, 1), (0, 1)), ((), ()))
+    grad_down = lax.dot_general(s_recv, hidden, over_slots, preferred_element_type=f32)
+    down_part = col_major((grad_down * trained_flag).astype(bf16))
+    down_part, s_recv = lax.optimization_barrier((down_part, s_recv))
+    down_block = lax.psum_scatter(down_part, "dp", scatter_dimension=0, tiled=True)
+
     hidden_grad = lax.dot_general(
         s_recv, w_down[0], (((2,), (1,)), ((), ())), preferred_element_type=f32
     )
-    sigmoid_gate = jax.nn.sigmoid(gate_pre)
-    activated = gate_pre * sigmoid_gate
     pre_grad = jnp.concatenate(
         [
             hidden_grad * up_pre * sigmoid_gate * (1.0 + gate_pre * (1.0 - sigmoid_gate)),
@@ -51,25 +69,16 @@
         ],
         axis=2,
     ).astype(bf16)
-    hidden = (activated * up_pre).astype(bf16)
     slot_grads = lax.dot_general(
         pre_grad, w_in[0], (((2,), (1,)), ((), ())), preferred_element_type=f32
     ).astype(bf16)
 
-    trained_flag = jnp.any(trained == lax.axis_index("expert")).astype(f32)
-    over_slots = (((0, 1), (0, 1)), ((), ()))
-    grad_down = lax.dot_general(s_recv, hidden, over_slots, preferred_element_type=f32)
-    down_block = lax.psum_scatter(
-        (grad_down * trained_flag).astype(bf16), "dp", scatter_dimension=0, tiled=True
-    )
-
     slot_grads, x_recv = lax.optimization_barrier((slot_grads, x_recv))
-    arrived = lax.all_to_all(slot_grads, "expert", 0, 0, tiled=True)
+    arrived = lax.all_to_all(row_major(slot_grads), "expert", 0, 0, tiled=True)
 
     grad_in = lax.dot_general(x_recv, pre_grad, over_slots, preferred_element_type=f32)
-    in_block = lax.psum_scatter(
-        (grad_in * trained_flag).astype(bf16), "dp", scatter_dimension=0, tiled=True
-    )
+    in_part = col_major((grad_in * trained_flag).astype(bf16))
+    in_block = lax.psum_scatter(in_part, "dp", scatter_dimension=0, tiled=True)
 
     in_grad = lax.dot_general(
         tok_sel_b, arrived, (((0, 1), (0, 1)), ((), ())), preferred_element_type=f32

time: 243 us -> 234 us (0.963)
  blocking collectives: 0 us -> 58.2 us
  waiting for transfers between devices: 115 us -> 73.4 us
  local copies, waits for them, and re-layouts: 27.5 us -> 10.1 us
  starting transfers between devices: 25.2 us -> 17 us
    all_to_all x0 -> x1, blocking collectives: none -> 58.2 us  [per_device(): arrived = lax.all_to_all(row_major(slot_grads), 'expert', 0, 0, tiled=True)]
    all_to_all x3 -> x2, waiting for transfers between devices: 107 us -> 62.9 us  [the longest x1 35.9 us: per_device(): s_recv = lax.all_to_all(row_major(s_send), 'expert', 0, 0, tiled=True)]
    optimization_barrier x2 -> x0, local copies, waits for them, and re-layouts: 11.8 us -> none  [the longest x1 5.92 us: per_device(): x_send, s_recv = lax.optimization_barrier((x_send, s_recv))]
    all_to_all x3 -> x2, starting transfers between devices: 24.7 us -> 16.8 us  [the longest x1 8.78 us: per_device(): s_recv = lax.all_to_all(row_major(s_send), 'expert', 0, 0, tiled=True)]
    convert_element_type x1 -> x0, local copies, waits for them, and re-layouts: 3.87 us -> none  [per_device(): s_send = (gate_slot[:, :, None] * og_slot).astype(bf16)]
    convert_element_type x0 -> x1, other arithmetic: none -> 2.62 us  [per_device(): hidden = (activated * up_pre).astype(bf16)]
    reduce_scatter x2, waiting for transfers between devices: 7.92 us -> 10.5 us  [the longest x1 10.5 us: per_device(): in_block = lax.psum_scatter(in_part, 'dp', scatter_dimension=0, tiled=True)]
  transfers between devices with their start and end apart: 5 -> 4, of which waited for: 4 -> 3; matrix products, arithmetic and copies ran while one was open for 27% -> 21% of each run, Pallas kernels for 0% -> 0%
where the time goes in v2:
time: 234 us; the launch traced here: 233 us
  waiting for transfers between devices  73.4 us (31%)
  blocking collectives  58.2 us (25%)
  matrix products  49.3 us (21%)
  starting transfers between devices  17 us (7%)
  between operations  14.9 us (6%)
  other arithmetic  10.4 us (4%)
  local copies, waits for them, and re-layouts  10.1 us (4%)
    all_to_all x1, blocking collectives, per_device(): arrived = lax.all_to_all(row_major(slot_grads), 'expert', 0, 0, tiled=True)  58.2 us
    all_to_all x1, waiting for transfers between devices, per_device(): s_recv = lax.all_to_all(row_major(s_send), 'expert', 0, 0, tiled=True)  35.9 us
    all_to_all x1, waiting for transfers between devices, per_device(): x_recv = lax.all_to_all(row_major(x_send), 'expert', 0, 0, tiled=True)  27 us
    dot_general x1, matrix products, per_device(): lax.dot_general(pre_grad, w_in[0], (((2,), (1,)), ((), ())), preferred_el...  10.9 us
    reduce_scatter x1, waiting for transfers between devices, per_device(): in_block = lax.psum_scatter(in_part, 'dp', scatter_dimension=0, tiled=True)  10.5 us
    dot_general x1, matrix products, per_device(): lax.dot_general(x_recv, pre_grad, over_slots, preferred_element_type=f32)  10.4 us
    dot_general x1, matrix products, per_device(): lax.dot_general(s_recv, w_down[0], (((2,), (1,)), ((), ())), preferred_el...  10.1 us
    all_to_all x1, starting transfers between devices, per_device(): s_recv = lax.all_to_all(row_major(s_send), 'expert', 0, 0, tiled=True)  8.78 us
  transfers between devices with their start and end apart: 4, of which 3 were waited for; matrix products, arithmetic and copies ran while one was open for 21% of the time, Pallas kernels for 0%

profile of v2, /device:TPU:1, one launch (start us, length us, event | category | flops | bytes accessed | tf_op | source)
XLA Modules:
  0.0 233.4 jit_solution(4018863702702790699)
XLA Ops:
  7.2 0.9 iota_compare_fusion.3
  8.0 0.8 copy.33
  9.1 1.7 reduce-window.6
  11.8 1.1 fusion.21
  13.0 4.3 %multiply_convert_fusion = bf16[32,25,2048]{2,1,0:T(8,128)(2,1)} fusion(f32[32,25]{1,0:T(8,128)S(1)} %copy.38, bf16[128,2048]{1,0:T(8,128)(2,1)} %param.9, pred[32,25,128]{2,0,1:T(8,128)(4,1)S(1)} %and_reduce_fusion), kind=kOutput, calls=%fused_computation.2 | convolution fusion | flops 422707200 | bytes 3906688 | tf_op jit(solution)/shard_map/dot_general | solution.py:40
  17.2 8.8 %all-to-all-start = ((bf16[32,25,2048]{2,1,0:T(8,128)(2,1)}), bf16[32,25,2048]{2,1,0:T(8,128)(2,1)}, u32[]{:S(2)}, u32[]{:S(2)}) async-start(bf16[32,25,2048]{2,1,0:T(8,128)(2,1)} %multiply_convert_fusion), calls=%async_computation | async-start | bytes 8388608 | tf_op jit(solution)/shard_map/all_to_all | solution.py:51
  26.1 0.6 compare_reduce_fusion
  27.4 4.3 %reshape.50 = bf16[32,25,1408]{2,1,0:T(8,128)(2,1)} reshape(bf16[1,1,800,1408]{3,2,1,0:T(8,128)(2,1)} %param.15) | data formatting | bytes 4505600 | tf_op jit(solution)/shard_map/reshape | solution.py:44
  31.6 2.8 %fusion.37 = (bf16[32,25,704]{2,1,0:T(8,128)(2,1)S(1)}, bf16[32,25,704]{2,1,0:T(8,128)(2,1)S(1)}) fusion(bf16[32,25,1408]{2,1,0:T(8,128)(2,1)} %reshape.50), kind=kLoop, calls=%fused_computation.54 | loop fusion | bytes 4505600 | tf_op jit(solution)/shard_map/slice | solution.py:45
  34.5 3.2 %convolution_convert_fusion = bf16[32,25,2048]{2,1,0:T(8,128)(2,1)} fusion(bf16[128,2048]{1,0:T(8,128)(2,1)S(1)} %copy-done.4, pred[32,25,128]{2,0,1:T(8,128)(4,1)S(1)} %and_reduce_fusion), kind=kOutput, calls=%fused_computation.8 | convolution fusion | flops 421068800 | bytes 3903488 | tf_op jit(solution)/shard_map/dot_general | solution.py:42
  37.7 2.6 %fusion.17 = bf16[32,25,704]{2,0,1:T(8,128)(2,1)} fusion(bf16[32,25,704]{2,1,0:T(8,128)(2,1)S(1)} %get-tuple-element.19, bf16[32,25,704]{2,1,0:T(8,128)(2,1)S(1)} %get-tuple-element.18), kind=kLoop, calls=%fused_computation.24 | loop fusion | flops 4505600 | bytes 3379200 | tf_op jit(solution)/shard_map/convert_element_type | solution.py:49
  40.3 35.9 %all-to-all-done = bf16[32,25,2048]{2,1,0:T(8,128)(2,1)} async-done(((bf16[32,25,2048]{2,1,0:T(8,128)(2,1)}), bf16[32,25,2048]{2,1,0:T(8,128)(2,1)}, u32[]{:S(2)}, u32[]{:S(2)}) %all-to-all-start) | async-done | bytes 3276832 | tf_op jit(solution)/shard_map/all_to_all | solution.py:51
  76.3 7.5 %fusion.3 = bf16[2048,704]{0,1:T(8,128)(2,1)} fusion(bf16[32,25,2048]{2,1,0:T(8,128)(2,1)} %all-to-all-done, f32[]{:T(128)S(6)} %convert_element_type.43, bf16[32,25,704]{2,0,1:T(8,128)(2,1)} %fusion.17), kind=kOutput, calls=%fused_computation.6 | convolution fusion | flops 2309750784 | bytes 7286788 | tf_op jit(solution)/shard_map/dot_general | solution.py:57
  83.8 8.0 %all-to-all-start.1 = ((bf16[32,25,2048]{2,1,0:T(8,128)(2,1)}), bf16[32,25,2048]{2,1,0:T(8,128)(2,1)}, u32[]{:S(2)}, u32[]{:S(2)}) async-start(bf16[32,25,2048]{2,1,0:T(8,128)(2,1)} %convolution_convert_fusion), calls=%async_computation.1 | async-start | bytes 8388608 | tf_op jit(solution)/shard_map/all_to_all | solution.py:53
  92.0 10.1 %fusion.20 = (bf16[32,25,704]{2,0,1:T(8,128)(2,1)S(1)}, bf16[32,25,704]{2,0,1:T(8,128)(2,1)S(1)}) fusion(bf16[32,25,704]{2,1,0:T(8,128)(2,1)} %copy-done.2, bf16[32,25,704]{2,1,0:T(8,128)(2,1)} %copy-done.1, bf16[1,704,2048]{2,1,0:T(8,128)(2,1)S(1)} %copy-done, bf16[32,25,2048]{2,1,0:T(8,128)(2,1)} %all-to-all-done), kind=kOutput, calls=%fused_computation.27 | convolution fusion | flops 2315315200 | bytes 10665984 | tf_op jit(solution)/shard_map/dot_general | solution.py:62
  102.1 0.7 pad_maximum_fusion
  102.9 1.4 copy-done.3
  104.3 10.9 %fusion.4 = bf16[32,25,2048]{2,1,0:T(8,128)(2,1)} fusion(bf16[1,2048,1408]{2,1,0:T(8,128)(2,1)} %param.13, bf16[32,25,1408]{2,0,1:T(8,128)(2,1)S(1)} %pad_maximum_fusion), kind=kOutput, calls=%fused_computation.7 | convolution fusion | flops 4615372800 | bytes 11296768 | tf_op jit(solution)/shard_map/dot_general | solution.py:72
  115.2 27.0 %all-to-all-done.1 = bf16[32,25,2048]{2,1,0:T(8,128)(2,1)} async-done(((bf16[32,25,2048]{2,1,0:T(8,128)(2,1)}), bf16[32,25,2048]{2,1,0:T(8,128)(2,1)}, u32[]{:S(2)}, u32[]{:S(2)}) %all-to-all-start.1) | async-done | bytes 3276832 | tf_op jit(solution)/shard_map/all_to_all | solution.py:53
  142.2 10.4 %fusion = bf16[2048,1408]{0,1:T(8,128)(2,1)} fusion(bf16[32,25,2048]{2,1,0:T(8,128)(2,1)} %all-to-all-done.1, f32[]{:T(128)S(6)} %convert_element_type.43, bf16[32,25,1408]{2,0,1:T(8,128)(2,1)} %copy-done.3), kind=kOutput, calls=%fused_computation.1 | convolution fusion | flops 4619501568 | bytes 11296772 | tf_op jit(solution)/shard_map/dot_general | solution.py:79
  152.6 58.2 %all_to_all.15 = bf16[32,25,2048]{2,1,0:T(8,128)(2,1)S(1)} all-to-all(bf16[32,25,2048]{2,1,0:T(8,128)(2,1)} %fusion.4), channel_id=1, replica_groups=mesh['dp'=8,'expert'=32] {'expert'}, dimensions={0} | all-to-all | bytes 6553600 | tf_op jit(solution)/shard_map/all_to_all | solution.py:77
  210.9 2.9 %fusion.26 = bf16[128,2048]{1,0:T(8,128)(2,1)} fusion(pred[32,25,128]{2,0,1:T(8,128)(4,1)S(1)} %and_reduce_fusion, bf16[32,25,2048]{2,1,0:T(8,128)(2,1)S(1)} %all_to_all.15), kind=kOutput, calls=%fused_computation.34 | convolution fusion | flops 419692544 | bytes 3903488 | tf_op jit(solution)/shard_map/dot_general | solution.py:83
  213.8 10.5 %reduce-scatter.3.cloned.1.call-done = bf16[256,1408]{0,1:T(8,128)(2,1)} async-done(((bf16[2048,1408]{0,1:T(8,128)(2,1)}), bf16[256,1408]{0,1:T(8,128)(2,1)}) %reduce-scatter.3.cloned.1.call-update) | async-done | bytes 720912 | tf_op jit(solution)/shard_map/reduce_scatter | solution.py:81
  224.2 2.3 maximum_bitcast_fusion
  (28 shorter events, 1.5 us)
Async XLA Ops:
  7.2 84.8 %copy-start = (bf16[1,704,2048]{2,1,0:T(8,128)(2,1)S(1)}, bf16[1,704,2048]{2,1,0:T(8,128)(2,1)}, u32[]{:S(2)}) copy-start(bf16[1,704,2048]{2,1,0:T(8,128)(2,1)} %param.14) | copy-start | bytes 8650756
  17.2 8.8 %copy-start.5 = (s32[8]{0:T(128)S(1)}, s32[8]{0:T(128)}, u32[]{:S(2)}) copy-start(s32[8]{0:T(128)} %param.12) | copy-start | bytes 100
  17.2 59.1 %all-to-all-start = ((bf16[32,25,2048]{2,1,0:T(8,128)(2,1)}), bf16[32,25,2048]{2,1,0:T(8,128)(2,1)}, u32[]{:S(2)}, u32[]{:S(2)}) async-start(bf16[32,25,2048]{2,1,0:T(8,128)(2,1)} %multiply_convert_fusion), calls=%async_computation | async-start | bytes 8388608 | tf_op jit(solution)/shard_map/all_to_all | solution.py:51
  26.0 187.7 %reduce-scatter.5.cloned.1.call-start = ((), (), s32[]{:S(2)}) async-start(), calls=%async_computation.6 | async-start | bytes 3244032 | tf_op jit(solution)/shard_map/reduce_scatter | solution.py:60
  31.6 2.8 %copy-start.4 = (bf16[128,2048]{1,0:T(8,128)(2,1)S(1)}, bf16[128,2048]{1,0:T(8,128)(2,1)}, u32[]{:S(2)}) copy-start(bf16[128,2048]{1,0:T(8,128)(2,1)} %param.8) | copy-start | bytes 1572868
  34.5 3.2 %copy-start.1 = (bf16[32,25,704]{2,1,0:T(8,128)(2,1)}, bf16[32,25,704]{2,1,0:T(8,128)(2,1)S(1)}, u32[]{:S(2)}) copy-start(bf16[32,25,704]{2,1,0:T(8,128)(2,1)S(1)} %get-tuple-element.18) | copy-start | bytes 3379204
  34.5 3.2 %copy-start.2 = (bf16[32,25,704]{2,1,0:T(8,128)(2,1)}, bf16[32,25,704]{2,1,0:T(8,128)(2,1)S(1)}, u32[]{:S(2)}) copy-start(bf16[32,25,704]{2,1,0:T(8,128)(2,1)S(1)} %get-tuple-element.19) | copy-start | bytes 3379204
  83.8 58.4 %all-to-all-start.1 = ((bf16[32,25,2048]{2,1,0:T(8,128)(2,1)}), bf16[32,25,2048]{2,1,0:T(8,128)(2,1)}, u32[]{:S(2)}, u32[]{:S(2)}) async-start(bf16[32,25,2048]{2,1,0:T(8,128)(2,1)} %convolution_convert_fusion), calls=%async_computation.1 | async-start | bytes 8388608 | tf_op jit(solution)/shard_map/all_to_all | solution.py:53
  91.8 132.5 %reduce-scatter.3.cloned.1.call-start = ((), (), s32[]{:S(2)}) async-start(), calls=%async_computation.5 | async-start | bytes 6488064 | tf_op jit(solution)/shard_map/reduce_scatter | solution.py:81
  102.8 1.4 copy-start.3
Sparse Core Ops, SparseCore 0:
  83.9 42.8 reduce-scatter.4
  152.7 71.4 reduce-scatter.2

commit v3 on v2

--- a/solution.py
+++ b/solution.py
@@ -35,11 +35,18 @@
     tok_sel = jnp.any(sel, axis=3)
     tok_sel_b = tok_sel.astype(bf16)
     gate_slot = jnp.sum(jnp.where(sel, gate_weights[None, None, :, :], 0.0), axis=(2, 3))
+    slot_tok = jnp.sum(jnp.where(tok_sel, jnp.arange(tok_count, dtype=jnp.int32), 0), axis=2)
+    filled = jnp.any(tok_sel, axis=2).reshape(-1)
 
-    pick = (((2,), (0,)), ((), ()))
-    og_slot = lax.dot_general(tok_sel_b, out_grad, pick, preferred_element_type=f32)
-    s_send = (gate_slot[:, :, None] * og_slot).astype(bf16)
-    x_send = lax.dot_general(tok_sel_b, tokens, pick, preferred_element_type=f32).astype(bf16)
+    lanes = 128
+    rows = tokens.shape[1] // lanes
+    flat = (groups, capacity * rows, lanes)
+    tok3 = tokens.reshape(tok_count, rows, lanes)
+    og3 = out_grad.reshape(tok_count, rows, lanes)
+    slot_rows = slot_tok.reshape(-1)
+    x_send = jnp.where(filled[:, None, None], tok3[slot_rows], jnp.zeros((), bf16)).reshape(flat)
+    s_send = (gate_slot.reshape(-1)[:, None, None] * og3[slot_rows].astype(f32)).astype(bf16)
+    s_send = s_send.reshape(flat)
 
     saved3 = saved.reshape(groups, capacity, 2 * hidden_units)
     gate_pre = saved3[:, :, :hidden_units].astype(f32)
@@ -49,8 +56,10 @@
     hidden = (activated * up_pre).astype(bf16)
 
     s_recv = lax.all_to_all(row_major(s_send), "expert", 0, 0, tiled=True)
+    s_recv = s_recv.reshape(groups, capacity, rows * lanes)
     x_send, s_recv, hidden = lax.optimization_barrier((x_send, s_recv, hidden))
     x_recv = lax.all_to_all(row_major(x_send), "expert", 0, 0, tiled=True)
+    x_recv = x_recv.reshape(groups, capacity, rows * lanes)
 
     trained_flag = jnp.any(trained == lax.axis_index("expert")).astype(f32)
     over_slots = (((0, 1), (0, 1)), ((), ()))
@@ -74,15 +83,17 @@
     ).astype(bf16)
 
     slot_grads, x_recv = lax.optimization_barrier((slot_grads, x_recv))
+    slot_grads = slot_grads.reshape(flat)
     arrived = lax.all_to_all(row_major(slot_grads), "expert", 0, 0, tiled=True)
 
     grad_in = lax.dot_general(x_recv, pre_grad, over_slots, preferred_element_type=f32)
     in_part = col_major((grad_in * trained_flag).astype(bf16))
     in_block = lax.psum_scatter(in_part, "dp", scatter_dimension=0, tiled=True)
 
-    in_grad = lax.dot_general(
-        tok_sel_b, arrived, (((0, 1), (0, 1)), ((), ())), preferred_element_type=f32
-    ).astype(bf16)
+    slot_index = flat_ids * capacity + slot_rank
+    picked = arrived.reshape(groups * capacity, rows, lanes)[slot_index]
+    in_grad = jnp.sum(picked.reshape(tok_count, fanout, rows, lanes).astype(f32), axis=1)
+    in_grad = in_grad.astype(bf16).reshape(tok_count, rows * lanes)
     weight_block = jnp.concatenate([in_block, down_block], axis=1)
     return (in_grad, weight_block[None])
 

time: 234 us -> 235 us (level)
  blocking collectives: 58.2 us -> 0 us
  local copies, waits for them, and re-layouts: 10.1 us -> 51.4 us
  other arithmetic: 10.4 us -> 24.5 us
  matrix products: 49.3 us -> 38 us
  waiting for transfers between devices: 73.4 us -> 80.8 us
  starting transfers between devices: 17 us -> 24 us
    all_to_all x1 -> x0, blocking collectives: 58.2 us -> none  [per_device(): arrived = lax.all_to_all(row_major(slot_grads), 'expert', 0, 0, tiled=True)]
    all_to_all x0 -> x1, waiting for transfers between devices: none -> 40.4 us  [per_device(): arrived = lax.all_to_all(row_major(slot_grads), 'expert', 0, 0, tiled=True)]
    reshape x0 -> x4, local copies, waits for them, and re-layouts: none -> 19.9 us  [the longest x1 6.68 us: per_device(): slot_grads = slot_grads.reshape(flat)]
    all_to_all x1, waiting for transfers between devices: 35.9 us -> 18.8 us  [per_device(): s_recv = lax.all_to_all(row_major(s_send), 'expert', 0, 0, tiled=True)]
    gather x0 -> x3, local copies, waits for them, and re-layouts: none -> 12.8 us  [the longest x1 4.94 us: per_device(): picked = arrived.reshape(groups * capacity, rows, lanes)[slot_index]]
    dot_general x3 -> x0, matrix products: 10.4 us -> none  [the longest x1 4.26 us: per_device(): lax.dot_general(tok_sel_b, out_grad, pick, preferred_element_type=f32)]
    reduce_scatter x1, waiting for transfers between devices: 10.5 us -> 1.39 us  [per_device(): in_block = lax.psum_scatter(in_part, 'dp', scatter_dimension=0, tiled=True)]
    all_to_all x0 -> x1, starting transfers between devices: none -> 7.61 us  [per_device(): arrived = lax.all_to_all(row_major(slot_grads), 'expert', 0, 0, tiled=True)]
  transfers between devices with their start and end apart: 4 -> 5, of which waited for: 3 -> 4; matrix products, arithmetic and copies ran while one was open for 21% -> 34% of each run, Pallas kernels for 0% -> 0%
where the time goes in v3:
time: 235 us; the launch traced here: 233 us
  waiting for transfers between devices  80.8 us (34%)
  local copies, waits for them, and re-layouts  51.4 us (22%)
  matrix products  38 us (16%)
  other arithmetic  24.5 us (10%)
  starting transfers between devices  24 us (10%)
  between operations  15 us (6%)
    all_to_all x1, waiting for transfers between devices, per_device(): arrived = lax.all_to_all(row_major(slot_grads), 'expert', 0, 0, tiled=True)  40.4 us
    all_to_all x1, waiting for transfers between devices, per_device(): x_recv = lax.all_to_all(row_major(x_send), 'expert', 0, 0, tiled=True)  20.2 us
    all_to_all x1, waiting for transfers between devices, per_device(): s_recv = lax.all_to_all(row_major(s_send), 'expert', 0, 0, tiled=True)  18.8 us
    dot_general x1, matrix products, per_device(): lax.dot_general(x_recv, pre_grad, over_slots, preferred_element_type=f32)  10.8 us
    dot_general x1, matrix products, per_device(): lax.dot_general(s_recv, w_down[0], (((2,), (1,)), ((), ())), preferred_el...  10.1 us
    dot_general x1, matrix products, per_device(): lax.dot_general(pre_grad, w_in[0], (((2,), (1,)), ((), ())), preferred_el...  9.61 us
    all_to_all x1, starting transfers between devices, per_device(): s_recv = lax.all_to_all(row_major(s_send), 'expert', 0, 0, tiled=True)  8.64 us
    all_to_all x1, starting transfers between devices, per_device(): x_recv = lax.all_to_all(row_major(x_send), 'expert', 0, 0, tiled=True)  7.62 us
  transfers between devices with their start and end apart: 5, of which 4 were waited for; matrix products, arithmetic and copies ran while one was open for 34% of the time, Pallas kernels for 0%

profile of v3, /device:TPU:1, one launch (start us, length us, event | category | flops | bytes accessed | tf_op | source)
XLA Modules:
  0.0 233.5 jit_solution(4132528903971225735)
XLA Ops:
  15.2 3.9 %gather_fusion.1 = bf16[800,16,128]{2,1,0:T(8,128)(2,1)} fusion(bf16[128,16,128]{2,1,0:T(8,128)(2,1)S(1)} %bitcast.63, s32[1024]{0:T(1024)S(1)} %pad_clamp_fusion.1), kind=kCustom, calls=%fused_computation.1 | custom fusion | bytes 6556800 | tf_op jit(solution)/shard_map/gather | solution.py:48
  19.2 5.2 %fusion.1 = bf16[32,400,128]{2,1,0:T(8,128)(2,1)} fusion(f32[32,400]{1,0:T(8,128)S(1)} %copy.49, bf16[32,400,128]{2,1,0:T(8,128)(2,1)} %bitcast.65), kind=kLoop, calls=%fused_computation.6 | loop fusion | flops 4915200 | bytes 6604800 | tf_op jit(solution)/shard_map/convert_element_type | solution.py:48
  24.4 8.6 %all-to-all-start = ((bf16[32,400,128]{2,1,0:T(8,128)(2,1)}), bf16[32,400,128]{2,1,0:T(8,128)(2,1)}, u32[]{:S(2)}, u32[]{:S(2)}) async-start(bf16[32,400,128]{2,1,0:T(8,128)(2,1)} %fusion.1), calls=%async_computation | async-start | bytes 6553600 | tf_op jit(solution)/shard_map/all_to_all | solution.py:58
  33.1 4.3 %reshape.158 = bf16[32,25,1408]{2,1,0:T(8,128)(2,1)} reshape(bf16[1,1,800,1408]{3,2,1,0:T(8,128)(2,1)} %param.15) | data formatting | bytes 4505600 | tf_op jit(solution)/shard_map/reshape | solution.py:51
  38.8 3.9 %gather_fusion = bf16[800,16,128]{2,1,0:T(8,128)(2,1)} fusion(bf16[128,16,128]{2,1,0:T(8,128)(2,1)S(1)} %bitcast.62, s32[1024]{0:T(1024)S(1)} %pad_clamp_fusion.1), kind=kCustom, calls=%fused_computation | custom fusion | bytes 6556800 | tf_op jit(solution)/shard_map/gather | solution.py:47
  44.0 2.9 %fusion.27 = (bf16[32,25,704]{2,1,0:T(8,128)(2,1)S(1)}, bf16[32,25,704]{2,1,0:T(8,128)(2,1)S(1)}) fusion(bf16[32,25,1408]{2,1,0:T(8,128)(2,1)} %reshape.158), kind=kLoop, calls=%fused_computation.59 | loop fusion | bytes 4505600 | tf_op jit(solution)/shard_map/slice | solution.py:52
  47.0 5.2 %bitcast_select_fusion = bf16[32,400,128]{2,1,0:T(8,128)(2,1)} fusion(pred[32,400]{1,0:T(8,128)(4,1)S(1)} %copy.47, bf16[32,400,128]{2,1,0:T(8,128)(2,1)S(1)} %bitcast.64), kind=kLoop, calls=%fused_computation.18 | loop fusion | flops 1638400 | bytes 6566400 | tf_op jit(solution)/shard_map/jit(_where)/select_n | solution.py:47
  52.1 2.7 %fusion.12 = bf16[32,25,704]{2,0,1:T(8,128)(2,1)} fusion(bf16[32,25,704]{2,1,0:T(8,128)(2,1)S(1)} %get-tuple-element.21, bf16[32,25,704]{2,1,0:T(8,128)(2,1)S(1)} %get-tuple-element.20), kind=kLoop, calls=%fused_computation.25 | loop fusion | flops 4505600 | bytes 3379200 | tf_op jit(solution)/shard_map/convert_element_type | solution.py:56
  54.8 18.8 %all-to-all-done = bf16[32,400,128]{2,1,0:T(8,128)(2,1)} async-done(((bf16[32,400,128]{2,1,0:T(8,128)(2,1)}), bf16[32,400,128]{2,1,0:T(8,128)(2,1)}, u32[]{:S(2)}, u32[]{:S(2)}) %all-to-all-start) | async-done | bytes 3276832 | tf_op jit(solution)/shard_map/all_to_all | solution.py:58
  73.6 6.6 %reshape.157 = bf16[32,25,2048]{2,1,0:T(8,128)(2,1)} reshape(bf16[32,400,128]{2,1,0:T(8,128)(2,1)} %all-to-all-done) | data formatting | bytes 6553600 | tf_op jit(solution)/shard_map/reshape | solution.py:59
  80.2 7.5 %fusion.4 = bf16[2048,704]{0,1:T(8,128)(2,1)} fusion(bf16[32,25,2048]{2,1,0:T(8,128)(2,1)} %reshape.157, f32[]{:T(128)S(6)} %convert_element_type.47, bf16[32,25,704]{2,0,1:T(8,128)(2,1)} %fusion.12), kind=kOutput, calls=%fused_computation.10 | convolution fusion | flops 2309750784 | bytes 7286788 | tf_op jit(solution)/shard_map/dot_general | solution.py:66
  87.7 7.6 %all-to-all-start.1 = ((bf16[32,400,128]{2,1,0:T(8,128)(2,1)}), bf16[32,400,128]{2,1,0:T(8,128)(2,1)}, u32[]{:S(2)}, u32[]{:S(2)}) async-start(bf16[32,400,128]{2,1,0:T(8,128)(2,1)} %bitcast_select_fusion), calls=%async_computation.1 | async-start | bytes 6553600 | tf_op jit(solution)/shard_map/all_to_all | solution.py:61
  95.3 10.1 %fusion.15 = (bf16[32,25,704]{2,0,1:T(8,128)(2,1)S(1)}, bf16[32,25,704]{2,0,1:T(8,128)(2,1)S(1)}) fusion(bf16[32,25,704]{2,1,0:T(8,128)(2,1)} %copy-done.4, bf16[32,25,704]{2,1,0:T(8,128)(2,1)} %copy-done.3, bf16[1,704,2048]{2,1,0:T(8,128)(2,1)S(1)} %copy-done, bf16[32,25,2048]{2,1,0:T(8,128)(2,1)} %reshape.157), kind=kOutput, calls=%fused_computation.28 | convolution fusion | flops 2315315200 | bytes 10665984 | tf_op jit(solution)/shard_map/dot_general | solution.py:71
  106.2 9.6 %fusion.5 = bf16[32,25,2048]{2,0,1:T(8,128)(2,1)} fusion(bf16[32,25,1408]{2,0,1:T(8,128)(2,1)S(1)} %pad_maximum_fusion, bf16[1,2048,1408]{2,1,0:T(8,128)(2,1)} %param.13), kind=kOutput, calls=%fused_computation.17 | convolution fusion | flops 4615372800 | bytes 11296768 | tf_op jit(solution)/shard_map/dot_general | solution.py:81
  115.8 20.2 %all-to-all-done.1 = bf16[32,400,128]{2,1,0:T(8,128)(2,1)} async-done(((bf16[32,400,128]{2,1,0:T(8,128)(2,1)}), bf16[32,400,128]{2,1,0:T(8,128)(2,1)}, u32[]{:S(2)}, u32[]{:S(2)}) %all-to-all-start.1) | async-done | bytes 3276832 | tf_op jit(solution)/shard_map/all_to_all | solution.py:61
  136.0 6.6 %reshape.159 = bf16[32,25,2048]{2,1,0:T(8,128)(2,1)} reshape(bf16[32,400,128]{2,1,0:T(8,128)(2,1)} %all-to-all-done.1) | data formatting | bytes 6553600 | tf_op jit(solution)/shard_map/reshape | solution.py:62
  142.5 10.8 %fusion = bf16[2048,1408]{0,1:T(8,128)(2,1)} fusion(bf16[32,25,2048]{2,1,0:T(8,128)(2,1)} %reshape.159, f32[]{:T(128)S(6)} %convert_element_type.47, bf16[32,25,1408]{2,0,1:T(8,128)(2,1)S(1)} %pad_maximum_fusion), kind=kOutput, calls=%fused_computation.4 | convolution fusion | flops 4619501568 | bytes 11296772 | tf_op jit(solution)/shard_map/dot_general | solution.py:89
  153.4 5.9 %copy.54 = bf16[32,25,2048]{2,1,0:T(8,128)(2,1)} copy(bf16[32,25,2048]{2,0,1:T(8,128)(2,1)} %fusion.5) | data formatting | bytes 6553600 | tf_op jit(solution)/shard_map/optimization_barrier | solution.py:85
  159.2 6.7 %reshape.160 = bf16[32,400,128]{2,1,0:T(8,128)(2,1)} reshape(bf16[32,25,2048]{2,1,0:T(8,128)(2,1)} %copy.54) | data formatting | bytes 6553600 | tf_op jit(solution)/shard_map/reshape | solution.py:86
  165.9 7.6 %all-to-all-start.2 = ((bf16[32,400,128]{2,1,0:T(8,128)(2,1)}), bf16[32,400,128]{2,1,0:T(8,128)(2,1)}, u32[]{:S(2)}, u32[]{:S(2)}) async-start(bf16[32,400,128]{2,1,0:T(8,128)(2,1)} %reshape.160), calls=%async_computation.2 | async-start | bytes 6553600 | tf_op jit(solution)/shard_map/all_to_all | solution.py:87
  173.9 40.4 %all-to-all-done.2 = bf16[32,400,128]{2,1,0:T(8,128)(2,1)} async-done(((bf16[32,400,128]{2,1,0:T(8,128)(2,1)}), bf16[32,400,128]{2,1,0:T(8,128)(2,1)}, u32[]{:S(2)}, u32[]{:S(2)}) %all-to-all-start.2) | async-done | bytes 3276832 | tf_op jit(solution)/shard_map/all_to_all | solution.py:87
  214.2 4.9 %gather_fusion.2 = bf16[768,16,128]{2,1,0:T(8,128)(2,1)} fusion(bf16[800,16,128]{2,1,0:T(8,128)(2,1)} %bitcast.10, s32[1024]{0:T(1024)S(1)} %pad_clamp_fusion), kind=kCustom, calls=%fused_computation.2 | custom fusion | bytes 6294528 | tf_op jit(solution)/shard_map/gather | solution.py:94
  219.2 2.9 %reduce_sum.42 = bf16[128,16,128]{2,1,0:T(8,128)(2,1)S(1)} reduce(bf16[128,6,16,128]{3,2,1,0:T(8,128)(2,1)} %bitcast.66, bf16[]{:T(256)} %constant.6.clone.1), dimensions={1}, to_apply=%region_8.9 | reduce | flops 1310720 | bytes 3670018 | tf_op jit(solution)/shard_map/reduce_sum | solution.py:95
  224.4 2.3 maximum_bitcast_fusion
  (54 shorter events, 13.4 us)
Async XLA Ops:
  7.2 88.2 %copy-start = (bf16[1,704,2048]{2,1,0:T(8,128)(2,1)S(1)}, bf16[1,704,2048]{2,1,0:T(8,128)(2,1)}, u32[]{:S(2)}) copy-start(bf16[1,704,2048]{2,1,0:T(8,128)(2,1)} %param.14) | copy-start | bytes 8650756
  24.4 49.2 %all-to-all-start = ((bf16[32,400,128]{2,1,0:T(8,128)(2,1)}), bf16[32,400,128]{2,1,0:T(8,128)(2,1)}, u32[]{:S(2)}, u32[]{:S(2)}) async-start(bf16[32,400,128]{2,1,0:T(8,128)(2,1)} %fusion.1), calls=%async_computation | async-start | bytes 6553600 | tf_op jit(solution)/shard_map/all_to_all | solution.py:58
  33.1 189.9 %reduce-scatter.5.cloned.1.call-start = ((), (), s32[]{:S(2)}) async-start(), calls=%async_computation.6 | async-start | bytes 3244032 | tf_op jit(solution)/shard_map/reduce_scatter | solution.py:69
  38.8 4.0 %copy-start.6 = (s32[8]{0:T(128)S(1)}, s32[8]{0:T(128)}, u32[]{:S(2)}) copy-start(s32[8]{0:T(128)} %param.12) | copy-start | bytes 100
  44.0 3.0 %copy-start.2 = (bf16[800,16,128]{2,1,0:T(8,128)(2,1)S(1)}, bf16[800,16,128]{2,1,0:T(8,128)(2,1)}, u32[]{:S(2)}) copy-start(bf16[800,16,128]{2,1,0:T(8,128)(2,1)} %gather_fusion) | copy-start | bytes 9830404
  46.9 5.2 %copy-start.3 = (bf16[32,25,704]{2,1,0:T(8,128)(2,1)}, bf16[32,25,704]{2,1,0:T(8,128)(2,1)S(1)}, u32[]{:S(2)}) copy-start(bf16[32,25,704]{2,1,0:T(8,128)(2,1)S(1)} %get-tuple-element.20) | copy-start | bytes 3379204
  47.0 5.2 %copy-start.4 = (bf16[32,25,704]{2,1,0:T(8,128)(2,1)}, bf16[32,25,704]{2,1,0:T(8,128)(2,1)S(1)}, u32[]{:S(2)}) copy-start(bf16[32,25,704]{2,1,0:T(8,128)(2,1)S(1)} %get-tuple-element.21) | copy-start | bytes 3379204
  87.7 48.3 %all-to-all-start.1 = ((bf16[32,400,128]{2,1,0:T(8,128)(2,1)}), bf16[32,400,128]{2,1,0:T(8,128)(2,1)}, u32[]{:S(2)}, u32[]{:S(2)}) async-start(bf16[32,400,128]{2,1,0:T(8,128)(2,1)} %bitcast_select_fusion), calls=%async_computation.1 | async-start | bytes 6553600 | tf_op jit(solution)/shard_map/all_to_all | solution.py:61
  95.3 129.1 %reduce-scatter.3.cloned.1.call-start = ((), (), s32[]{:S(2)}) async-start(), calls=%async_computation.5 | async-start | bytes 6488064 | tf_op jit(solution)/shard_map/reduce_scatter | solution.py:91
  165.9 7.6 %copy-start.5 = (s32[128,6]{0,1:T(8,128)S(1)}, s32[128,6]{0,1:T(8,128)}, u32[]{:S(2)}) copy-start(s32[128,6]{0,1:T(8,128)} %param.10) | copy-start | bytes 9220
  165.9 48.3 %all-to-all-start.2 = ((bf16[32,400,128]{2,1,0:T(8,128)(2,1)}), bf16[32,400,128]{2,1,0:T(8,128)(2,1)}, u32[]{:S(2)}, u32[]{:S(2)}) async-start(bf16[32,400,128]{2,1,0:T(8,128)(2,1)} %reshape.160), calls=%async_computation.2 | async-start | bytes 6553600 | tf_op jit(solution)/shard_map/all_to_all | solution.py:87
  219.2 7.5 %copy-start.1 = (bf16[1,704,2048]{2,1,0:T(8,128)(2,1)S(1)}, bf16[1,704,2048]{2,1,0:T(8,128)(2,1)}, u32[]{:S(2)}) copy-start(bf16[1,704,2048]{2,1,0:T(8,128)(2,1)} %param.14) | copy-start | bytes 8650756
Sparse Core Ops, SparseCore 0:
  87.8 42.2 reduce-scatter.4
  153.5 70.8 reduce-scatter.2

commit v4 on v2

--- a/solution.py
+++ b/solution.py
@@ -39,7 +39,13 @@
     pick = (((2,), (0,)), ((), ()))
     og_slot = lax.dot_general(tok_sel_b, out_grad, pick, preferred_element_type=f32)
     s_send = (gate_slot[:, :, None] * og_slot).astype(bf16)
-    x_send = lax.dot_general(tok_sel_b, tokens, pick, preferred_element_type=f32).astype(bf16)
+    lanes = 128
+    rows = tokens.shape[1] // lanes
+    slot_tok = jnp.sum(jnp.where(tok_sel, jnp.arange(tok_count, dtype=jnp.int32), 0), axis=2)
+    filled = jnp.any(tok_sel, axis=2).reshape(-1)
+    tok3 = tokens.reshape(tok_count, rows, lanes)
+    x_send = jnp.where(filled[:, None, None], tok3[slot_tok.reshape(-1)], jnp.zeros((), bf16))
+    x_send = x_send.reshape(groups, capacity * rows, lanes)
 
     saved3 = saved.reshape(groups, capacity, 2 * hidden_units)
     gate_pre = saved3[:, :, :hidden_units].astype(f32)
@@ -76,8 +82,10 @@
     slot_grads, x_recv = lax.optimization_barrier((slot_grads, x_recv))
     arrived = lax.all_to_all(row_major(slot_grads), "expert", 0, 0, tiled=True)
 
-    grad_in = lax.dot_general(x_recv, pre_grad, over_slots, preferred_element_type=f32)
-    in_part = col_major((grad_in * trained_flag).astype(bf16))
+    x_rows = x_recv.reshape(groups * capacity, rows, lanes)
+    pre_rows = pre_grad.reshape(groups * capacity, 2 * hidden_units)
+    grad_in = lax.dot_general(x_rows, pre_rows, (((0,), (0,)), ((), ())), preferred_element_type=f32)
+    in_part = (grad_in.reshape(rows * lanes, 2 * hidden_units) * trained_flag).astype(bf16)
     in_block = lax.psum_scatter(in_part, "dp", scatter_dimension=0, tiled=True)
 
     in_grad = lax.dot_general(

time: 234 us -> 228 us (0.974)
  blocking collectives: 58.2 us -> 0 us
  waiting for transfers between devices: 73.4 us -> 94 us
  local copies, waits for them, and re-layouts: 10.1 us -> 24.8 us
  starting transfers between devices: 17 us -> 24.4 us
  other arithmetic: 10.4 us -> 17.7 us
  matrix products: 49.3 us -> 51.7 us
    all_to_all x1 -> x0, blocking collectives: 58.2 us -> none  [per_device(): arrived = lax.all_to_all(row_major(slot_grads), 'expert', 0, 0, tiled=True)]
    all_to_all x0 -> x1, waiting for transfers between devices: none -> 49.2 us  [per_device(): arrived = lax.all_to_all(row_major(slot_grads), 'expert', 0, 0, tiled=True)]
    all_to_all x1, waiting for transfers between devices: 27 us -> 9.13 us  [per_device(): x_recv = lax.all_to_all(row_major(x_send), 'expert', 0, 0, tiled=True)]
    all_to_all x1, waiting for transfers between devices: 35.9 us -> 27.7 us  [per_device(): s_recv = lax.all_to_all(row_major(s_send), 'expert', 0, 0, tiled=True)]
    all_to_all x0 -> x1, starting transfers between devices: none -> 7.45 us  [per_device(): arrived = lax.all_to_all(row_major(slot_grads), 'expert', 0, 0, tiled=True)]
    select_n x0 -> x2, other arithmetic: none -> 5.18 us  [the longest x1 5.16 us: per_device(): jnp.where(filled[:, None, None], tok3[slot_tok.reshape(-1)], jnp.zeros(()...]
    gather x0 -> x1, local copies, waits for them, and re-layouts: none -> 4 us  [per_device(): tok3[slot_tok.reshape(-1)]]
    concatenate x0 -> x2, local copies, waits for them, and re-layouts: none -> 3.2 us  [per_device(): jnp.concatenate([hidden_grad * up_pre * sigmoid_gate * (1.0 + gate_pre *...]
  transfers between devices with their start and end apart: 4 -> 5, of which waited for: 3 -> 4; matrix products, arithmetic and copies ran while one was open for 21% -> 31% of each run, Pallas kernels for 0% -> 0%
where the time goes in v4:
time: 228 us
  waiting for transfers between devices  94 us (41%)
  matrix products  51.7 us (23%)
  local copies, waits for them, and re-layouts  24.8 us (11%)
  starting transfers between devices  24.4 us (11%)
  other arithmetic  17.7 us (8%)
  between operations  14.9 us (7%)
    all_to_all x1, waiting for transfers between devices, per_device(): arrived = lax.all_to_all(row_major(slot_grads), 'expert', 0, 0, tiled=True)  49.2 us
    all_to_all x1, waiting for transfers between devices, per_device(): s_recv = lax.all_to_all(row_major(s_send), 'expert', 0, 0, tiled=True)  27.7 us
    dot_general x1, matrix products, per_device(): lax.dot_general(x_rows, pre_rows, (((0,), (0,)), ((), ())), preferred_ele...  12.4 us
    dot_general x1, matrix products, per_device(): lax.dot_general(s_recv, w_down[0], (((2,), (1,)), ((), ())), preferred_el...  11.1 us
    dot_general x1, matrix products, per_device(): lax.dot_general(pre_grad, w_in[0], (((2,), (1,)), ((), ())), preferred_el...  11.1 us
    all_to_all x1, waiting for transfers between devices, per_device(): x_recv = lax.all_to_all(row_major(x_send), 'expert', 0, 0, tiled=True)  9.13 us
    all_to_all x1, starting transfers between devices, per_device(): s_recv = lax.all_to_all(row_major(s_send), 'expert', 0, 0, tiled=True)  8.78 us
    all_to_all x1, starting transfers between devices, per_device(): x_recv = lax.all_to_all(row_major(x_send), 'expert', 0, 0, tiled=True)  7.94 us
  transfers between devices with their start and end apart: 5, of which 4 were waited for; matrix products, arithmetic and copies ran while one was open for 31% of the time, Pallas kernels for 0%

profile of v4, /device:TPU:1, one launch (start us, length us, event | category | flops | bytes accessed | tf_op | source)
XLA Modules:
  0.0 227.5 jit_solution(15605901593065125808)
XLA Ops:
  9.1 1.7 reduce-window.6
  13.3 4.3 %multiply_convert_fusion.1 = bf16[32,25,2048]{2,1,0:T(8,128)(2,1)} fusion(f32[32,25]{1,0:T(8,128)S(1)} %copy.77, bf16[128,2048]{1,0:T(8,128)(2,1)} %param.9, pred[32,25,128]{2,0,1:T(8,128)(4,1)S(1)} %get-tuple-element.27), kind=kOutput, calls=%fused_computation.2 | convolution fusion | flops 422707200 | bytes 3906688 | tf_op jit(solution)/shard_map/dot_general | solution.py:40
  17.5 8.8 %all-to-all-start = ((bf16[32,25,2048]{2,1,0:T(8,128)(2,1)}), bf16[32,25,2048]{2,1,0:T(8,128)(2,1)}, u32[]{:S(2)}, u32[]{:S(2)}) async-start(bf16[32,25,2048]{2,1,0:T(8,128)(2,1)} %multiply_convert_fusion.1), calls=%async_computation | async-start | bytes 8388608 | tf_op jit(solution)/shard_map/all_to_all | solution.py:57
  29.7 4.3 %reshape.103 = bf16[32,25,1408]{2,1,0:T(8,128)(2,1)} reshape(bf16[1,1,800,1408]{3,2,1,0:T(8,128)(2,1)} %param.15) | data formatting | bytes 4505600 | tf_op jit(solution)/shard_map/reshape | solution.py:50
  34.0 4.0 %gather_fusion = bf16[800,16,128]{2,1,0:T(8,128)(2,1)} fusion(bf16[128,16,128]{2,1,0:T(8,128)(2,1)S(1)} %bitcast.60, s32[1024]{0:T(1024)S(1)} %pad_clamp_fusion), kind=kCustom, calls=%fused_computation | custom fusion | bytes 6556800 | tf_op jit(solution)/shard_map/gather | solution.py:47
  38.0 2.9 %fusion.40 = (bf16[32,25,704]{2,1,0:T(8,128)(2,1)S(1)}, bf16[32,25,704]{2,1,0:T(8,128)(2,1)S(1)}) fusion(bf16[32,25,1408]{2,1,0:T(8,128)(2,1)} %reshape.103), kind=kLoop, calls=%fused_computation.62 | loop fusion | bytes 4505600 | tf_op jit(solution)/shard_map/slice | solution.py:51
  41.0 5.2 %bitcast_select_fusion = bf16[32,400,128]{2,1,0:T(8,128)(2,1)} fusion(pred[32,400]{1,0:T(8,128)(4,1)S(1)} %copy.75, bf16[32,400,128]{2,1,0:T(8,128)(2,1)S(1)} %bitcast.61), kind=kLoop, calls=%fused_computation.16 | loop fusion | flops 1638400 | bytes 6566400 | tf_op jit(solution)/shard_map/jit(_where)/select_n | solution.py:47
  46.1 2.7 %fusion.17 = bf16[32,25,704]{2,0,1:T(8,128)(2,1)} fusion(bf16[32,25,704]{2,1,0:T(8,128)(2,1)S(1)} %get-tuple-element.31, bf16[32,25,704]{2,1,0:T(8,128)(2,1)S(1)} %get-tuple-element.30), kind=kLoop, calls=%fused_computation.26 | loop fusion | flops 4505600 | bytes 3379200 | tf_op jit(solution)/shard_map/convert_element_type | solution.py:55
  48.9 27.7 %all-to-all-done = bf16[32,25,2048]{2,1,0:T(8,128)(2,1)} async-done(((bf16[32,25,2048]{2,1,0:T(8,128)(2,1)}), bf16[32,25,2048]{2,1,0:T(8,128)(2,1)}, u32[]{:S(2)}, u32[]{:S(2)}) %all-to-all-start) | async-done | bytes 3276832 | tf_op jit(solution)/shard_map/all_to_all | solution.py:57
  76.6 7.5 %fusion.2 = bf16[2048,704]{0,1:T(8,128)(2,1)} fusion(bf16[32,25,2048]{2,1,0:T(8,128)(2,1)} %all-to-all-done, f32[]{:T(128)S(6)} %convert_element_type.40, bf16[32,25,704]{2,0,1:T(8,128)(2,1)} %fusion.17), kind=kOutput, calls=%fused_computation.6 | convolution fusion | flops 2309750784 | bytes 7286788 | tf_op jit(solution)/shard_map/dot_general | solution.py:63
  84.1 7.9 %all-to-all-start.1 = ((bf16[32,400,128]{2,1,0:T(8,128)(2,1)}), bf16[32,400,128]{2,1,0:T(8,128)(2,1)}, u32[]{:S(2)}, u32[]{:S(2)}) async-start(bf16[32,400,128]{2,1,0:T(8,128)(2,1)} %bitcast_select_fusion), calls=%async_computation.1 | async-start | bytes 6553600 | tf_op jit(solution)/shard_map/all_to_all | solution.py:59
  92.3 11.1 %fusion.20 = (bf16[32,25,704]{2,0,1:T(8,128)(2,1)S(1)}, bf16[32,25,704]{2,0,1:T(8,128)(2,1)}) fusion(bf16[32,25,704]{2,1,0:T(8,128)(2,1)} %copy-done.4, bf16[32,25,704]{2,1,0:T(8,128)(2,1)} %copy-done.3, bf16[1,704,2048]{2,1,0:T(8,128)(2,1)S(1)} %copy-done, bf16[32,25,2048]{2,1,0:T(8,128)(2,1)} %all-to-all-done), kind=kOutput, calls=%fused_computation.29 | convolution fusion | flops 2315315200 | bytes 10665984 | tf_op jit(solution)/shard_map/dot_general | solution.py:68
  105.1 1.7 concatenate.16
  106.9 2.1 copy.86
  110.5 2.0 pad_maximum_fusion
  112.5 11.1 %fusion.3 = bf16[32,25,2048]{2,1,0:T(8,128)(2,1)} fusion(bf16[1,2048,1408]{2,1,0:T(8,128)(2,1)} %param.13, bf16[32,25,1408]{2,0,1:T(8,128)(2,1)S(1)} %pad_maximum_fusion), kind=kOutput, calls=%fused_computation.7 | convolution fusion | flops 4615372800 | bytes 11296768 | tf_op jit(solution)/shard_map/dot_general | solution.py:78
  123.6 9.1 %all-to-all-done.1 = bf16[32,400,128]{2,1,0:T(8,128)(2,1)} async-done(((bf16[32,400,128]{2,1,0:T(8,128)(2,1)}), bf16[32,400,128]{2,1,0:T(8,128)(2,1)}, u32[]{:S(2)}, u32[]{:S(2)}) %all-to-all-start.1) | async-done | bytes 3276832 | tf_op jit(solution)/shard_map/all_to_all | solution.py:59
  132.7 12.4 %multiply_convert_fusion = bf16[2048,1408]{1,0:T(8,128)(2,1)} fusion(f32[]{:T(128)S(6)} %convert_element_type.40, bf16[100,8,16,128]{3,2,1,0:T(8,128)(2,1)} %bitcast.20, bf16[800,704]{1,0:T(8,128)(2,1)S(1)} %copy-done.8, bf16[800,704]{1,0:T(8,128)(2,1)S(1)} %copy-done.7), kind=kOutput, calls=%fused_computation.1 | convolution fusion | flops 4624007168 | bytes 11296772 | tf_op jit(solution)/shard_map/dot_general | solution.py:87
  145.2 7.5 %all-to-all-start.2 = ((bf16[32,25,2048]{2,1,0:T(8,128)(2,1)}), bf16[32,25,2048]{2,1,0:T(8,128)(2,1)}, u32[]{:S(2)}, u32[]{:S(2)}) async-start(bf16[32,25,2048]{2,1,0:T(8,128)(2,1)} %fusion.3), calls=%async_computation.2 | async-start | bytes 8388608 | tf_op jit(solution)/shard_map/all_to_all | solution.py:83
  153.8 49.2 %all-to-all-done.2 = bf16[32,25,2048]{2,1,0:T(8,128)(2,1)} async-done(((bf16[32,25,2048]{2,1,0:T(8,128)(2,1)}), bf16[32,25,2048]{2,1,0:T(8,128)(2,1)}, u32[]{:S(2)}, u32[]{:S(2)}) %all-to-all-start.2) | async-done | bytes 3276832 | tf_op jit(solution)/shard_map/all_to_all | solution.py:83
  203.0 5.3 %fusion.26 = bf16[128,2048]{1,0:T(8,128)(2,1)} fusion(pred[32,25,128]{2,0,1:T(8,128)(4,1)S(1)} %get-tuple-element.27, bf16[32,25,2048]{2,1,0:T(8,128)(2,1)} %all-to-all-done.2), kind=kOutput, calls=%fused_computation.36 | convolution fusion | flops 419692544 | bytes 3903488 | tf_op jit(solution)/shard_map/dot_general | solution.py:91
  208.3 7.9 %reduce-scatter.3.cloned.1.call-done = bf16[256,1408]{1,0:T(8,128)(2,1)} async-done(((bf16[2048,1408]{1,0:T(8,128)(2,1)}), bf16[256,1408]{1,0:T(8,128)(2,1)}) %reduce-scatter.3.cloned.1.call-update) | async-done | bytes 720912 | tf_op jit(solution)/shard_map/reduce_scatter | solution.py:89
  216.2 2.2 maximum_bitcast_fusion
  218.4 2.3 %copy.88 = bf16[1,256,2112]{1,2,0:T(8,128)(2,1)} copy(bf16[1,256,2112]{2,1,0:T(8,128)(2,1)} %maximum_bitcast_fusion) | data formatting | bytes 2162688
  (52 shorter events, 11.7 us)
Async XLA Ops:
  7.2 85.1 %copy-start = (bf16[1,704,2048]{2,1,0:T(8,128)(2,1)S(1)}, bf16[1,704,2048]{2,1,0:T(8,128)(2,1)}, u32[]{:S(2)}) copy-start(bf16[1,704,2048]{2,1,0:T(8,128)(2,1)} %param.14) | copy-start | bytes 8650756
  17.5 8.8 %copy-start.9 = (s32[8]{0:T(128)S(1)}, s32[8]{0:T(128)}, u32[]{:S(2)}) copy-start(s32[8]{0:T(128)} %param.12) | copy-start | bytes 100
  17.5 59.0 %all-to-all-start = ((bf16[32,25,2048]{2,1,0:T(8,128)(2,1)}), bf16[32,25,2048]{2,1,0:T(8,128)(2,1)}, u32[]{:S(2)}, u32[]{:S(2)}) async-start(bf16[32,25,2048]{2,1,0:T(8,128)(2,1)} %multiply_convert_fusion.1), calls=%async_computation | async-start | bytes 8388608 | tf_op jit(solution)/shard_map/all_to_all | solution.py:57
  26.3 126.3 %reduce-scatter.5.cloned.1.call-start = ((), (), s32[]{:S(2)}) async-start(), calls=%async_computation.6 | async-start | bytes 3244032 | tf_op jit(solution)/shard_map/reduce_scatter | solution.py:66
  38.0 3.0 %copy-start.2 = (bf16[800,16,128]{2,1,0:T(8,128)(2,1)S(1)}, bf16[800,16,128]{2,1,0:T(8,128)(2,1)}, u32[]{:S(2)}) copy-start(bf16[800,16,128]{2,1,0:T(8,128)(2,1)} %gather_fusion) | copy-start | bytes 9830404
  40.9 5.2 %copy-start.3 = (bf16[32,25,704]{2,1,0:T(8,128)(2,1)}, bf16[32,25,704]{2,1,0:T(8,128)(2,1)S(1)}, u32[]{:S(2)}) copy-start(bf16[32,25,704]{2,1,0:T(8,128)(2,1)S(1)} %get-tuple-element.30) | copy-start | bytes 3379204
  40.9 5.2 %copy-start.4 = (bf16[32,25,704]{2,1,0:T(8,128)(2,1)}, bf16[32,25,704]{2,1,0:T(8,128)(2,1)S(1)}, u32[]{:S(2)}) copy-start(bf16[32,25,704]{2,1,0:T(8,128)(2,1)S(1)} %get-tuple-element.31) | copy-start | bytes 3379204
  84.1 48.6 %all-to-all-start.1 = ((bf16[32,400,128]{2,1,0:T(8,128)(2,1)}), bf16[32,400,128]{2,1,0:T(8,128)(2,1)}, u32[]{:S(2)}, u32[]{:S(2)}) async-start(bf16[32,400,128]{2,1,0:T(8,128)(2,1)} %bitcast_select_fusion), calls=%async_computation.1 | async-start | bytes 6553600 | tf_op jit(solution)/shard_map/all_to_all | solution.py:59
  92.0 124.1 %reduce-scatter.3.cloned.1.call-start = ((), (), s32[]{:S(2)}) async-start(), calls=%async_computation.5 | async-start | bytes 6488064 | tf_op jit(solution)/shard_map/reduce_scatter | solution.py:89
  103.4 1.0 copy-start.5
  106.9 3.6 %copy-start.6 = (bf16[32,25,704]{2,0,1:T(8,128)(2,1)S(1)}, bf16[32,25,704]{2,0,1:T(8,128)(2,1)}, u32[]{:S(2)}) copy-start(bf16[32,25,704]{2,0,1:T(8,128)(2,1)} %copy-done.5) | copy-start | bytes 3379204
  112.5 20.3 %copy-start.7 = (bf16[800,704]{1,0:T(8,128)(2,1)S(1)}, bf16[800,704]{1,0:T(8,128)(2,1)}, u32[]{:S(2)}) copy-start(bf16[800,704]{1,0:T(8,128)(2,1)} %concatenate.16) | copy-start | bytes 3379204
  112.5 20.3 %copy-start.8 = (bf16[800,704]{1,0:T(8,128)(2,1)S(1)}, bf16[800,704]{1,0:T(8,128)(2,1)}, u32[]{:S(2)}) copy-start(bf16[800,704]{1,0:T(8,128)(2,1)} %concatenate.17) | copy-start | bytes 3379204
  145.2 57.8 %all-to-all-start.2 = ((bf16[32,25,2048]{2,1,0:T(8,128)(2,1)}), bf16[32,25,2048]{2,1,0:T(8,128)(2,1)}, u32[]{:S(2)}, u32[]{:S(2)}) async-start(bf16[32,25,2048]{2,1,0:T(8,128)(2,1)} %fusion.3), calls=%async_computation.2 | async-start | bytes 8388608 | tf_op jit(solution)/shard_map/all_to_all | solution.py:83
  203.0 17.6 %copy-start.1 = (bf16[1,704,2048]{2,1,0:T(8,128)(2,1)S(1)}, bf16[1,704,2048]{2,1,0:T(8,128)(2,1)}, u32[]{:S(2)}) copy-start(bf16[1,704,2048]{2,1,0:T(8,128)(2,1)} %param.14) | copy-start | bytes 8650756
Sparse Core Ops, SparseCore 0:
  84.2 43.1 reduce-scatter.4
  145.3 70.8 reduce-scatter.2

commit v5 on v4

--- a/solution.py
+++ b/solution.py
@@ -36,16 +36,15 @@
     tok_sel_b = tok_sel.astype(bf16)
     gate_slot = jnp.sum(jnp.where(sel, gate_weights[None, None, :, :], 0.0), axis=(2, 3))
 
-    pick = (((2,), (0,)), ((), ()))
-    og_slot = lax.dot_general(tok_sel_b, out_grad, pick, preferred_element_type=f32)
-    s_send = (gate_slot[:, :, None] * og_slot).astype(bf16)
     lanes = 128
     rows = tokens.shape[1] // lanes
+    flat = (groups, capacity * rows, lanes)
     slot_tok = jnp.sum(jnp.where(tok_sel, jnp.arange(tok_count, dtype=jnp.int32), 0), axis=2)
     filled = jnp.any(tok_sel, axis=2).reshape(-1)
+    slot_rows = slot_tok.reshape(-1)
+    og_send = out_grad.reshape(tok_count, rows, lanes)[slot_rows].reshape(flat)
     tok3 = tokens.reshape(tok_count, rows, lanes)
-    x_send = jnp.where(filled[:, None, None], tok3[slot_tok.reshape(-1)], jnp.zeros((), bf16))
-    x_send = x_send.reshape(groups, capacity * rows, lanes)
+    x_send = jnp.where(filled[:, None, None], tok3[slot_rows], jnp.zeros((), bf16)).reshape(flat)
 
     saved3 = saved.reshape(groups, capacity, 2 * hidden_units)
     gate_pre = saved3[:, :, :hidden_units].astype(f32)
@@ -54,15 +53,26 @@
     activated = gate_pre * sigmoid_gate
     hidden = (activated * up_pre).astype(bf16)
 
-    s_recv = lax.all_to_all(row_major(s_send), "expert", 0, 0, tiled=True)
-    x_send, s_recv, hidden = lax.optimization_barrier((x_send, s_recv, hidden))
+    og_recv = lax.all_to_all(row_major(og_send), "expert", 0, 0, tiled=True)
+    gate_recv = lax.all_to_all(gate_slot, "expert", 0, 0, tiled=True)
+    x_send, og_recv, gate_recv, hidden = lax.optimization_barrier(
+        (x_send, og_recv, gate_recv, hidden)
+    )
+    slot_count = groups * capacity
+    s_rows = (
+        gate_recv.reshape(slot_count, 1, 1) * og_recv.reshape(slot_count, rows, lanes).astype(f32)
+    ).astype(bf16)
     x_recv = lax.all_to_all(row_major(x_send), "expert", 0, 0, tiled=True)
 
     trained_flag = jnp.any(trained == lax.axis_index("expert")).astype(f32)
     over_slots = (((0, 1), (0, 1)), ((), ()))
-    grad_down = lax.dot_general(s_recv, hidden, over_slots, preferred_element_type=f32)
-    down_part = col_major((grad_down * trained_flag).astype(bf16))
-    down_part, s_recv = lax.optimization_barrier((down_part, s_recv))
+    grad_down = lax.dot_general(
+        s_rows, hidden.reshape(slot_count, hidden_units), (((0,), (0,)), ((), ())),
+        preferred_element_type=f32,
+    )
+    down_part = (grad_down.reshape(rows * lanes, hidden_units) * trained_flag).astype(bf16)
+    down_part, s_rows = lax.optimization_barrier((down_part, s_rows))
+    s_recv = s_rows.reshape(groups, capacity, rows * lanes)
     down_block = lax.psum_scatter(down_part, "dp", scatter_dimension=0, tiled=True)
 
     hidden_grad = lax.dot_general(
@@ -82,8 +92,8 @@
     slot_grads, x_recv = lax.optimization_barrier((slot_grads, x_recv))
     arrived = lax.all_to_all(row_major(slot_grads), "expert", 0, 0, tiled=True)
 
-    x_rows = x_recv.reshape(groups * capacity, rows, lanes)
-    pre_rows = pre_grad.reshape(groups * capacity, 2 * hidden_units)
+    x_rows = x_recv.reshape(slot_count, rows, lanes)
+    pre_rows = pre_grad.reshape(slot_count, 2 * hidden_units)
     grad_in = lax.dot_general(x_rows, pre_rows, (((0,), (0,)), ((), ())), preferred_element_type=f32)
     in_part = (grad_in.reshape(rows * lanes, 2 * hidden_units) * trained_flag).astype(bf16)
     in_block = lax.psum_scatter(in_part, "dp", scatter_dimension=0, tiled=True)

time: 228 us -> 237 us (1.039)
  local copies, waits for them, and re-layouts: 24.8 us -> 44.4 us
  waiting for transfers between devices: 94 us -> 78.8 us
  starting transfers between devices: 24.4 us -> 31 us
  matrix products: 51.7 us -> 45.2 us
  other arithmetic: 17.7 us -> 21.4 us
    reshape x1 -> x3, local copies, waits for them, and re-layouts: 0.11 us -> 9.33 us  [the longest x1 6.57 us: per_device(): s_recv = s_rows.reshape(groups, capacity, rows * lanes)]
    all_to_all x1 -> x2, waiting for transfers between devices: 27.7 us -> 19.2 us  [the longest x1 18.7 us: per_device(): og_recv = lax.all_to_all(row_major(og_send), 'expert', 0, 0, tiled=True)]
    all_to_all x1 -> x2, starting transfers between devices: 8.78 us -> 15.7 us  [the longest x1 8.59 us: per_device(): gate_recv = lax.all_to_all(gate_slot, 'expert', 0, 0, tiled=True)]
    dot_general x2 -> x1, matrix products: 11.7 us -> 4.95 us  [per_device(): lax.dot_general(s_rows, hidden.reshape(slot_count, hidden_units), (((0,),...]
    all_to_all x1, waiting for transfers between devices: 9.13 us -> 2.47 us  [per_device(): x_recv = lax.all_to_all(row_major(x_send), 'expert', 0, 0, tiled=True)]
    gather x1 -> x2, local copies, waits for them, and re-layouts: 4 us -> 7.95 us  [the longest x1 4.01 us: per_device(): tok3[slot_rows]]
    convert_element_type x0 -> x1, other arithmetic: none -> 3.79 us  [per_device(): s_rows = (gate_recv.reshape(slot_count, 1, 1) * og_recv.reshape(slot_coun...]
    optimization_barrier x0 -> x1, local copies, waits for them, and re-layouts: none -> 3.14 us  [per_device(): lax.optimization_barrier((x_send, og_recv, gate_recv, hidden))]
  transfers between devices with their start and end apart: 5 -> 6, of which waited for: 4 -> 5; matrix products, arithmetic and copies ran while one was open for 31% -> 35% of each run, Pallas kernels for 0% -> 0%
where the time goes in v5:
time: 237 us; the launch traced here: 236 us
  waiting for transfers between devices  78.8 us (33%)
  matrix products  45.2 us (19%)
  local copies, waits for them, and re-layouts  44.4 us (19%)
  starting transfers between devices  31 us (13%)
  other arithmetic  21.4 us (9%)
  between operations  15 us (6%)
    all_to_all x1, waiting for transfers between devices, per_device(): arrived = lax.all_to_all(row_major(slot_grads), 'expert', 0, 0, tiled=True)  49.2 us
    all_to_all x1, waiting for transfers between devices, per_device(): og_recv = lax.all_to_all(row_major(og_send), 'expert', 0, 0, tiled=True)  18.7 us
    dot_general x1, matrix products, per_device(): lax.dot_general(x_rows, pre_rows, (((0,), (0,)), ((), ())), preferred_ele...  12.4 us
    dot_general x1, matrix products, per_device(): lax.dot_general(pre_grad, w_in[0], (((2,), (1,)), ((), ())), preferred_el...  11.4 us
    dot_general x1, matrix products, per_device(): lax.dot_general(s_recv, w_down[0], (((2,), (1,)), ((), ())), preferred_el...  11.1 us
    all_to_all x1, starting transfers between devices, per_device(): gate_recv = lax.all_to_all(gate_slot, 'expert', 0, 0, tiled=True)  8.59 us
    unnamed x28, local copies, waits for them, and re-layouts  8.19 us
    reduce_scatter x1, waiting for transfers between devices, per_device(): in_block = lax.psum_scatter(in_part, 'dp', scatter_dimension=0, tiled=True)  7.9 us
  transfers between devices with their start and end apart: 6, of which 5 were waited for; matrix products, arithmetic and copies ran while one was open for 35% of the time, Pallas kernels for 0%

profile of v5, /device:TPU:1, one launch (start us, length us, event | category | flops | bytes accessed | tf_op | source)
XLA Modules:
  0.0 235.8 jit_solution(1632152138716088801)
XLA Ops:
  13.3 8.6 %all-to-all-start.1 = ((f32[32,1,25]{2,1,0:T(1,128)}), f32[32,1,25]{2,1,0:T(1,128)S(1)}, u32[]{:S(2)}, u32[]{:S(2)}) async-start(f32[32,1,25]{2,1,0:T(1,128)} %copy.71), calls=%async_computation.1 | async-start | bytes 32768 | tf_op jit(solution)/shard_map/all_to_all | solution.py:57
  24.4 3.9 %gather_fusion.1 = bf16[800,16,128]{2,1,0:T(8,128)(2,1)} fusion(bf16[128,16,128]{2,1,0:T(8,128)(2,1)S(1)} %bitcast.68, s32[1024]{0:T(1024)S(1)} %pad_clamp_fusion), kind=kCustom, calls=%fused_computation.1 | custom fusion | bytes 6556800 | tf_op jit(solution)/shard_map/gather | solution.py:45
  28.8 7.1 %all-to-all-start = ((bf16[32,400,128]{2,1,0:T(8,128)(2,1)}), bf16[32,400,128]{2,1,0:T(8,128)(2,1)}, u32[]{:S(2)}, u32[]{:S(2)}) async-start(bf16[32,400,128]{2,1,0:T(8,128)(2,1)} %bitcast.70), calls=%async_computation | async-start | bytes 6553600 | tf_op jit(solution)/shard_map/all_to_all | solution.py:56
  38.8 4.0 %gather_fusion = bf16[800,16,128]{2,1,0:T(8,128)(2,1)} fusion(bf16[128,16,128]{2,1,0:T(8,128)(2,1)S(1)} %bitcast.67, s32[1024]{0:T(1024)S(1)} %pad_clamp_fusion), kind=kCustom, calls=%fused_computation | custom fusion | bytes 6556800 | tf_op jit(solution)/shard_map/gather | solution.py:47
  42.8 4.3 %reshape.125 = bf16[32,25,1408]{2,1,0:T(8,128)(2,1)} reshape(bf16[1,1,800,1408]{3,2,1,0:T(8,128)(2,1)} %param.15) | data formatting | bytes 4505600 | tf_op jit(solution)/shard_map/reshape | solution.py:49
  47.0 2.9 %fusion.39 = (bf16[32,25,704]{2,1,0:T(8,128)(2,1)S(1)}, bf16[32,25,704]{2,1,0:T(8,128)(2,1)S(1)}) fusion(bf16[32,25,1408]{2,1,0:T(8,128)(2,1)} %reshape.125), kind=kLoop, calls=%fused_computation.62 | loop fusion | bytes 4505600 | tf_op jit(solution)/shard_map/slice | solution.py:50
  50.0 5.2 %bitcast_select_fusion = bf16[32,400,128]{2,1,0:T(8,128)(2,1)} fusion(pred[32,400]{1,0:T(8,128)(4,1)S(1)} %copy.69, bf16[32,400,128]{2,1,0:T(8,128)(2,1)S(1)} %bitcast.71), kind=kLoop, calls=%fused_computation.19 | loop fusion | flops 1638400 | bytes 6566400 | tf_op jit(solution)/shard_map/jit(_where)/select_n | solution.py:47
  55.1 2.6 %fusion.19 = bf16[32,25,704]{2,0,1:T(8,128)(2,1)} fusion(bf16[32,25,704]{2,1,0:T(8,128)(2,1)S(1)} %get-tuple-element.33, bf16[32,25,704]{2,1,0:T(8,128)(2,1)S(1)} %get-tuple-element.32), kind=kLoop, calls=%fused_computation.29 | loop fusion | flops 4505600 | bytes 3379200 | tf_op jit(solution)/shard_map/convert_element_type | solution.py:54
  57.8 18.7 %all-to-all-done = bf16[32,400,128]{2,1,0:T(8,128)(2,1)} async-done(((bf16[32,400,128]{2,1,0:T(8,128)(2,1)}), bf16[32,400,128]{2,1,0:T(8,128)(2,1)}, u32[]{:S(2)}, u32[]{:S(2)}) %all-to-all-start) | async-done | bytes 3276832 | tf_op jit(solution)/shard_map/all_to_all | solution.py:56
  76.6 3.1 %copy.74 = bf16[32,25,704]{2,1,0:T(8,128)(2,1)} copy(bf16[32,25,704]{2,0,1:T(8,128)(2,1)} %fusion.19) | data formatting | bytes 2252800 | tf_op jit(solution)/shard_map/optimization_barrier | solution.py:58
  79.7 2.6 %reshape.126 = bf16[800,704]{1,0:T(8,128)(2,1)} reshape(bf16[32,25,704]{2,1,0:T(8,128)(2,1)} %copy.74) | data formatting | bytes 2252800 | tf_op jit(solution)/shard_map/reshape | solution.py:70
  82.4 3.8 %fusion = bf16[800,16,128]{2,1,0:T(8,128)(2,1)S(1)} fusion(bf16[800,16,128]{2,1,0:T(8,128)(2,1)} %bitcast.16, f32[800]{0:T(1024)S(1)} %mul.49), kind=kLoop, calls=%fused_computation.4 | loop fusion | flops 4915200 | bytes 6556800 | tf_op jit(solution)/shard_map/convert_element_type | solution.py:64
  87.9 5.0 %multiply_convert_fusion.1 = bf16[2048,704]{0,1:T(8,128)(2,1)} fusion(bf16[800,704]{1,0:T(8,128)(2,1)S(1)} %copy-done.10, bf16[100,8,16,128]{3,2,1,0:T(8,128)(2,1)S(1)} %bitcast.69, f32[]{:T(128)S(6)} %convert_element_type.48), kind=kOutput, calls=%fused_computation.7 | convolution fusion | flops 2309750784 | bytes 7286788 | tf_op jit(solution)/shard_map/dot_general | solution.py:69
  92.8 7.4 %all-to-all-start.2 = ((bf16[32,400,128]{2,1,0:T(8,128)(2,1)}), bf16[32,400,128]{2,1,0:T(8,128)(2,1)}, u32[]{:S(2)}, u32[]{:S(2)}) async-start(bf16[32,400,128]{2,1,0:T(8,128)(2,1)} %bitcast_select_fusion), calls=%async_computation.2 | async-start | bytes 6553600 | tf_op jit(solution)/shard_map/all_to_all | solution.py:65
  100.6 6.6 %reshape.127 = bf16[32,25,2048]{2,1,0:T(8,128)(2,1)} reshape(bf16[800,16,128]{2,1,0:T(8,128)(2,1)} %copy-done.2) | data formatting | bytes 6553600 | tf_op jit(solution)/shard_map/reshape | solution.py:75
  107.1 11.1 %fusion.22 = (bf16[32,25,704]{2,0,1:T(8,128)(2,1)S(1)}, bf16[32,25,704]{2,0,1:T(8,128)(2,1)}) fusion(bf16[32,25,704]{2,1,0:T(8,128)(2,1)} %copy-done.5, bf16[32,25,704]{2,1,0:T(8,128)(2,1)} %copy-done.4, bf16[1,704,2048]{2,1,0:T(8,128)(2,1)S(1)} %copy-done, bf16[32,25,2048]{2,1,0:T(8,128)(2,1)} %reshape.127), kind=kOutput, calls=%fused_computation.32 | convolution fusion | flops 2315315200 | bytes 10665984 | tf_op jit(solution)/shard_map/dot_general | solution.py:78
  127.1 11.4 %fusion.3 = bf16[32,25,2048]{2,1,0:T(8,128)(2,1)} fusion(bf16[1,2048,1408]{2,1,0:T(8,128)(2,1)} %param.13, bf16[32,25,1408]{2,0,1:T(8,128)(2,1)S(1)} %pad_maximum_fusion), kind=kOutput, calls=%fused_computation.8 | convolution fusion | flops 4615372800 | bytes 11296768 | tf_op jit(solution)/shard_map/dot_general | solution.py:88
  138.5 2.5 %all-to-all-done.2 = bf16[32,400,128]{2,1,0:T(8,128)(2,1)} async-done(((bf16[32,400,128]{2,1,0:T(8,128)(2,1)}), bf16[32,400,128]{2,1,0:T(8,128)(2,1)}, u32[]{:S(2)}, u32[]{:S(2)}) %all-to-all-start.2) | async-done | bytes 3276832 | tf_op jit(solution)/shard_map/all_to_all | solution.py:65
  141.0 12.4 %multiply_convert_fusion = bf16[2048,1408]{1,0:T(8,128)(2,1)} fusion(f32[]{:T(128)S(6)} %convert_element_type.48, bf16[100,8,16,128]{3,2,1,0:T(8,128)(2,1)} %bitcast.30, bf16[800,704]{1,0:T(8,128)(2,1)S(1)} %copy-done.9, bf16[800,704]{1,0:T(8,128)(2,1)S(1)} %copy-done.8), kind=kOutput, calls=%fused_computation.2 | convolution fusion | flops 4624007168 | bytes 11296772 | tf_op jit(solution)/shard_map/dot_general | solution.py:97
  153.4 7.4 %all-to-all-start.3 = ((bf16[32,25,2048]{2,1,0:T(8,128)(2,1)}), bf16[32,25,2048]{2,1,0:T(8,128)(2,1)}, u32[]{:S(2)}, u32[]{:S(2)}) async-start(bf16[32,25,2048]{2,1,0:T(8,128)(2,1)} %fusion.3), calls=%async_computation.3 | async-start | bytes 8388608 | tf_op jit(solution)/shard_map/all_to_all | solution.py:93
  162.1 49.2 %all-to-all-done.3 = bf16[32,25,2048]{2,1,0:T(8,128)(2,1)} async-done(((bf16[32,25,2048]{2,1,0:T(8,128)(2,1)}), bf16[32,25,2048]{2,1,0:T(8,128)(2,1)}, u32[]{:S(2)}, u32[]{:S(2)}) %all-to-all-start.3) | async-done | bytes 3276832 | tf_op jit(solution)/shard_map/all_to_all | solution.py:93
  211.3 5.3 %fusion.28 = bf16[128,2048]{1,0:T(8,128)(2,1)} fusion(pred[32,25,128]{2,0,1:T(8,128)(4,1)S(1)} %get-tuple-element.29, bf16[32,25,2048]{2,1,0:T(8,128)(2,1)} %all-to-all-done.3), kind=kOutput, calls=%fused_computation.39 | convolution fusion | flops 419692544 | bytes 3903488 | tf_op jit(solution)/shard_map/dot_general | solution.py:101
  216.5 7.9 %reduce-scatter.3.cloned.1.call-done = bf16[256,1408]{1,0:T(8,128)(2,1)} async-done(((bf16[2048,1408]{1,0:T(8,128)(2,1)}), bf16[256,1408]{1,0:T(8,128)(2,1)}) %reduce-scatter.3.cloned.1.call-update) | async-done | bytes 720912 | tf_op jit(solution)/shard_map/reduce_scatter | solution.py:99
  226.6 2.3 copy.81
  (64 shorter events, 25.5 us)
Async XLA Ops:
  7.2 100.0 %copy-start = (bf16[1,704,2048]{2,1,0:T(8,128)(2,1)S(1)}, bf16[1,704,2048]{2,1,0:T(8,128)(2,1)}, u32[]{:S(2)}) copy-start(bf16[1,704,2048]{2,1,0:T(8,128)(2,1)} %param.14) | copy-start | bytes 8650756
  13.3 15.5 %all-to-all-start.1 = ((f32[32,1,25]{2,1,0:T(1,128)}), f32[32,1,25]{2,1,0:T(1,128)S(1)}, u32[]{:S(2)}, u32[]{:S(2)}) async-start(f32[32,1,25]{2,1,0:T(1,128)} %copy.71), calls=%async_computation.1 | async-start | bytes 32768 | tf_op jit(solution)/shard_map/all_to_all | solution.py:57
  28.8 7.3 %copy-start.11 = (s32[8]{0:T(128)S(1)}, s32[8]{0:T(128)}, u32[]{:S(2)}) copy-start(s32[8]{0:T(128)} %param.12) | copy-start | bytes 100
  28.8 47.7 %all-to-all-start = ((bf16[32,400,128]{2,1,0:T(8,128)(2,1)}), bf16[32,400,128]{2,1,0:T(8,128)(2,1)}, u32[]{:S(2)}, u32[]{:S(2)}) async-start(bf16[32,400,128]{2,1,0:T(8,128)(2,1)} %bitcast.70), calls=%async_computation | async-start | bytes 6553600 | tf_op jit(solution)/shard_map/all_to_all | solution.py:56
  35.9 125.0 %reduce-scatter.5.cloned.1.call-start = ((), (), s32[]{:S(2)}) async-start(), calls=%async_computation.7 | async-start | bytes 3244032 | tf_op jit(solution)/shard_map/reduce_scatter | solution.py:76
  47.0 3.0 %copy-start.3 = (bf16[800,16,128]{2,1,0:T(8,128)(2,1)S(1)}, bf16[800,16,128]{2,1,0:T(8,128)(2,1)}, u32[]{:S(2)}) copy-start(bf16[800,16,128]{2,1,0:T(8,128)(2,1)} %gather_fusion) | copy-start | bytes 9830404
  49.9 5.2 %copy-start.4 = (bf16[32,25,704]{2,1,0:T(8,128)(2,1)}, bf16[32,25,704]{2,1,0:T(8,128)(2,1)S(1)}, u32[]{:S(2)}) copy-start(bf16[32,25,704]{2,1,0:T(8,128)(2,1)S(1)} %get-tuple-element.32) | copy-start | bytes 3379204
  50.0 5.2 %copy-start.5 = (bf16[32,25,704]{2,1,0:T(8,128)(2,1)}, bf16[32,25,704]{2,1,0:T(8,128)(2,1)S(1)}, u32[]{:S(2)}) copy-start(bf16[32,25,704]{2,1,0:T(8,128)(2,1)S(1)} %get-tuple-element.33) | copy-start | bytes 3379204
  82.4 5.5 %copy-start.10 = (bf16[800,704]{1,0:T(8,128)(2,1)S(1)}, bf16[800,704]{1,0:T(8,128)(2,1)}, u32[]{:S(2)}) copy-start(bf16[800,704]{1,0:T(8,128)(2,1)} %reshape.126) | copy-start | bytes 3379204
  86.2 1.7 copy-start.2
  92.8 48.1 %all-to-all-start.2 = ((bf16[32,400,128]{2,1,0:T(8,128)(2,1)}), bf16[32,400,128]{2,1,0:T(8,128)(2,1)}, u32[]{:S(2)}, u32[]{:S(2)}) async-start(bf16[32,400,128]{2,1,0:T(8,128)(2,1)} %bitcast_select_fusion), calls=%async_computation.2 | async-start | bytes 6553600 | tf_op jit(solution)/shard_map/all_to_all | solution.py:65
  100.3 124.1 %reduce-scatter.3.cloned.1.call-start = ((), (), s32[]{:S(2)}) async-start(), calls=%async_computation.6 | async-start | bytes 6488064 | tf_op jit(solution)/shard_map/reduce_scatter | solution.py:99
  118.3 1.0 copy-start.6
  121.5 3.6 %copy-start.7 = (bf16[32,25,704]{2,0,1:T(8,128)(2,1)S(1)}, bf16[32,25,704]{2,0,1:T(8,128)(2,1)}, u32[]{:S(2)}) copy-start(bf16[32,25,704]{2,0,1:T(8,128)(2,1)} %copy-done.6) | copy-start | bytes 3379204
  127.1 13.9 %copy-start.8 = (bf16[800,704]{1,0:T(8,128)(2,1)S(1)}, bf16[800,704]{1,0:T(8,128)(2,1)}, u32[]{:S(2)}) copy-start(bf16[800,704]{1,0:T(8,128)(2,1)} %concatenate.16) | copy-start | bytes 3379204
  127.1 13.9 %copy-start.9 = (bf16[800,704]{1,0:T(8,128)(2,1)S(1)}, bf16[800,704]{1,0:T(8,128)(2,1)}, u32[]{:S(2)}) copy-start(bf16[800,704]{1,0:T(8,128)(2,1)} %concatenate.17) | copy-start | bytes 3379204
  153.4 57.8 %all-to-all-start.3 = ((bf16[32,25,2048]{2,1,0:T(8,128)(2,1)}), bf16[32,25,2048]{2,1,0:T(8,128)(2,1)}, u32[]{:S(2)}, u32[]{:S(2)}) async-start(bf16[32,25,2048]{2,1,0:T(8,128)(2,1)} %fusion.3), calls=%async_computation.3 | async-start | bytes 8388608 | tf_op jit(solution)/shard_map/all_to_all | solution.py:93
  211.3 17.7 %copy-start.1 = (bf16[1,704,2048]{2,1,0:T(8,128)(2,1)S(1)}, bf16[1,704,2048]{2,1,0:T(8,128)(2,1)}, u32[]{:S(2)}) copy-start(bf16[1,704,2048]{2,1,0:T(8,128)(2,1)} %param.14) | copy-start | bytes 8650756
Sparse Core Ops, SparseCore 0:
  93.0 42.3 reduce-scatter.4
  153.6 70.8 reduce-scatter.2

commit v6 on v5

--- a/solution.py
+++ b/solution.py
@@ -39,40 +39,40 @@
     lanes = 128
     rows = tokens.shape[1] // lanes
     flat = (groups, capacity * rows, lanes)
+    slot_count = groups * capacity
     slot_tok = jnp.sum(jnp.where(tok_sel, jnp.arange(tok_count, dtype=jnp.int32), 0), axis=2)
     filled = jnp.any(tok_sel, axis=2).reshape(-1)
     slot_rows = slot_tok.reshape(-1)
-    og_send = out_grad.reshape(tok_count, rows, lanes)[slot_rows].reshape(flat)
+    og3 = out_grad.reshape(tok_count, rows, lanes)
+    s_send = (gate_slot.reshape(-1)[:, None, None] * og3[slot_rows].astype(f32)).astype(bf16)
+    s_send = s_send.reshape(flat)
     tok3 = tokens.reshape(tok_count, rows, lanes)
     x_send = jnp.where(filled[:, None, None], tok3[slot_rows], jnp.zeros((), bf16)).reshape(flat)
+
+    saved_rows = saved.reshape(slot_count, 2 * hidden_units)
+    gate_rows = saved_rows[:, :hidden_units].astype(f32)
+    activated_rows = gate_rows * jax.nn.sigmoid(gate_rows)
+    hidden_rows = (activated_rows * saved_rows[:, hidden_units:].astype(f32)).astype(bf16)
 
     saved3 = saved.reshape(groups, capacity, 2 * hidden_units)
     gate_pre = saved3[:, :, :hidden_units].astype(f32)
     up_pre = saved3[:, :, hidden_units:].astype(f32)
     sigmoid_gate = jax.nn.sigmoid(gate_pre)
     activated = gate_pre * sigmoid_gate
-    hidden = (activated * up_pre).astype(bf16)
 
-    og_recv = lax.all_to_all(row_major(og_send), "expert", 0, 0, tiled=True)
-    gate_recv = lax.all_to_all(gate_slot, "expert", 0, 0, tiled=True)
-    x_send, og_recv, gate_recv, hidden = lax.optimization_barrier(
-        (x_send, og_recv, gate_recv, hidden)
-    )
-    slot_count = groups * capacity
-    s_rows = (
-        gate_recv.reshape(slot_count, 1, 1) * og_recv.reshape(slot_count, rows, lanes).astype(f32)
-    ).astype(bf16)
+    s_recv = lax.all_to_all(row_major(s_send), "expert", 0, 0, tiled=True)
+    x_send, s_recv, hidden_rows = lax.optimization_barrier((x_send, s_recv, hidden_rows))
     x_recv = lax.all_to_all(row_major(x_send), "expert", 0, 0, tiled=True)
 
     trained_flag = jnp.any(trained == lax.axis_index("expert")).astype(f32)
     over_slots = (((0, 1), (0, 1)), ((), ()))
     grad_down = lax.dot_general(
-        s_rows, hidden.reshape(slot_count, hidden_units), (((0,), (0,)), ((), ())),
+        s_recv.reshape(slot_count, rows, lanes), hidden_rows, (((0,), (0,)), ((), ())),
         preferred_element_type=f32,
     )
     down_part = (grad_down.reshape(rows * lanes, hidden_units) * trained_flag).astype(bf16)
-    down_part, s_rows = lax.optimization_barrier((down_part, s_rows))
-    s_recv = s_rows.reshape(groups, capacity, rows * lanes)
+    down_part, s_recv = lax.optimization_barrier((down_part, s_recv))
+    s_recv = s_recv.reshape(groups, capacity, rows * lanes)
     down_block = lax.psum_scatter(down_part, "dp", scatter_dimension=0, tiled=True)
 
     hidden_grad = lax.dot_general(

time: 237 us -> 234 us (0.987)
  starting transfers between devices: 31 us -> 24 us
  local copies, waits for them, and re-layouts: 44.4 us -> 38.5 us
  waiting for transfers between devices: 78.8 us -> 83.3 us
  other arithmetic: 21.4 us -> 24.9 us
    all_to_all x2 -> x1, starting transfers between devices: 15.7 us -> 8.77 us  [per_device(): s_recv = lax.all_to_all(row_major(s_send), 'expert', 0, 0, tiled=True)]
    all_to_all x2 -> x1, waiting for transfers between devices: 19.2 us -> 24.3 us  [per_device(): s_recv = lax.all_to_all(row_major(s_send), 'expert', 0, 0, tiled=True)]
    optimization_barrier x1 -> x0, local copies, waits for them, and re-layouts: 3.14 us -> none  [per_device(): lax.optimization_barrier((x_send, og_recv, gate_recv, hidden))]
    reshape x2 -> x1, local copies, waits for them, and re-layouts: 9.21 us -> 6.55 us  [per_device(): s_recv = s_recv.reshape(groups, capacity, rows * lanes)]
    all_to_all x1, waiting for transfers between devices: 2.47 us -> 0.01 us  [per_device(): x_recv = lax.all_to_all(row_major(x_send), 'expert', 0, 0, tiled=True)]
    unnamed x28 -> x20, local copies, waits for them, and re-layouts: 8.19 us -> 6.47 us
  transfers between devices with their start and end apart: 6 -> 5, of which waited for: 5 -> 3; matrix products, arithmetic and copies ran while one was open for 35% -> 34% of each run, Pallas kernels for 0% -> 0%
where the time goes in v6:
time: 234 us; the launch traced here: 233 us
  waiting for transfers between devices  83.3 us (36%)
  matrix products  47.3 us (20%)
  local copies, waits for them, and re-layouts  38.5 us (16%)
  other arithmetic  24.9 us (11%)
  starting transfers between devices  24 us (10%)
  between operations  14.9 us (6%)
    all_to_all x1, waiting for transfers between devices, per_device(): arrived = lax.all_to_all(row_major(slot_grads), 'expert', 0, 0, tiled=True)  49.1 us
    all_to_all x1, waiting for transfers between devices, per_device(): s_recv = lax.all_to_all(row_major(s_send), 'expert', 0, 0, tiled=True)  24.3 us
    dot_general x1, matrix products, per_device(): lax.dot_general(x_rows, pre_rows, (((0,), (0,)), ((), ())), preferred_ele...  12.4 us
    dot_general x1, matrix products, per_device(): lax.dot_general(pre_grad, w_in[0], (((2,), (1,)), ((), ())), preferred_el...  11.3 us
    dot_general x1, matrix products, per_device(): lax.dot_general(s_recv, w_down[0], (((2,), (1,)), ((), ())), preferred_el...  11.3 us
    reduce_scatter x1, waiting for transfers between devices, per_device(): in_block = lax.psum_scatter(in_part, 'dp', scatter_dimension=0, tiled=True)  9.93 us
    all_to_all x1, starting transfers between devices, per_device(): s_recv = lax.all_to_all(row_major(s_send), 'expert', 0, 0, tiled=True)  8.77 us
    all_to_all x1, starting transfers between devices, per_device(): arrived = lax.all_to_all(row_major(slot_grads), 'expert', 0, 0, tiled=True)  7.59 us
  transfers between devices with their start and end apart: 5, of which 3 were waited for; matrix products, arithmetic and copies ran while one was open for 34% of the time, Pallas kernels for 0%

profile of v6, /device:TPU:1, one launch (start us, length us, event | category | flops | bytes accessed | tf_op | source)
XLA Modules:
  0.0 233.0 jit_solution(10785798099410915721)
XLA Ops:
  9.1 1.7 reduce-window.6
  15.9 3.9 %gather_fusion.1 = bf16[800,16,128]{2,1,0:T(8,128)(2,1)} fusion(bf16[128,16,128]{2,1,0:T(8,128)(2,1)S(1)} %bitcast.71, s32[1024]{0:T(1024)S(1)} %pad_clamp_fusion), kind=kCustom, calls=%fused_computation.1 | custom fusion | bytes 6556800 | tf_op jit(solution)/shard_map/gather | solution.py:47
  19.8 5.4 %fusion = bf16[32,400,128]{2,1,0:T(8,128)(2,1)} fusion(f32[32,400]{1,0:T(8,128)} %copy.72, bf16[32,400,128]{2,1,0:T(8,128)(2,1)} %bitcast.73), kind=kLoop, calls=%fused_computation.4 | loop fusion | flops 4915200 | bytes 6604800 | tf_op jit(solution)/shard_map/convert_element_type | solution.py:47
  25.2 8.8 %all-to-all-start = ((bf16[32,400,128]{2,1,0:T(8,128)(2,1)}), bf16[32,400,128]{2,1,0:T(8,128)(2,1)}, u32[]{:S(2)}, u32[]{:S(2)}) async-start(bf16[32,400,128]{2,1,0:T(8,128)(2,1)} %fusion), calls=%async_computation | async-start | bytes 6553600 | tf_op jit(solution)/shard_map/all_to_all | solution.py:63
  36.6 4.0 %gather_fusion = bf16[800,16,128]{2,1,0:T(8,128)(2,1)} fusion(bf16[128,16,128]{2,1,0:T(8,128)(2,1)S(1)} %bitcast.70, s32[1024]{0:T(1024)S(1)} %pad_clamp_fusion), kind=kCustom, calls=%fused_computation | custom fusion | bytes 6556800 | tf_op jit(solution)/shard_map/gather | solution.py:50
  40.6 7.4 %bitcast_select_fusion = bf16[32,400,128]{2,1,0:T(8,128)(2,1)} fusion(pred[32,400]{1,0:T(8,128)(4,1)S(1)} %copy.70, bf16[32,400,128]{2,1,0:T(8,128)(2,1)} %bitcast.72), kind=kLoop, calls=%fused_computation.19 | loop fusion | flops 1638400 | bytes 6566400 | tf_op jit(solution)/shard_map/jit(_where)/select_n | solution.py:50
  48.0 2.2 fusion.32
  50.3 24.3 %all-to-all-done = bf16[32,400,128]{2,1,0:T(8,128)(2,1)} async-done(((bf16[32,400,128]{2,1,0:T(8,128)(2,1)}), bf16[32,400,128]{2,1,0:T(8,128)(2,1)}, u32[]{:S(2)}, u32[]{:S(2)}) %all-to-all-start) | async-done | bytes 3276832 | tf_op jit(solution)/shard_map/all_to_all | solution.py:63
  74.5 7.1 %multiply_convert_fusion.1 = bf16[2048,704]{0,1:T(8,128)(2,1)} fusion(bf16[800,704]{1,0:T(8,128)(2,1)} %fusion.32, bf16[100,8,16,128]{3,2,1,0:T(8,128)(2,1)} %bitcast.26, f32[]{:T(128)S(6)} %convert_element_type.56), kind=kOutput, calls=%fused_computation.7 | convolution fusion | flops 2309750784 | bytes 7286788 | tf_op jit(solution)/shard_map/dot_general | solution.py:69
  81.6 7.4 %all-to-all-start.1 = ((bf16[32,400,128]{2,1,0:T(8,128)(2,1)}), bf16[32,400,128]{2,1,0:T(8,128)(2,1)}, u32[]{:S(2)}, u32[]{:S(2)}) async-start(bf16[32,400,128]{2,1,0:T(8,128)(2,1)} %bitcast_select_fusion), calls=%async_computation.1 | async-start | bytes 6553600 | tf_op jit(solution)/shard_map/all_to_all | solution.py:65
  89.3 4.3 %reshape.129 = bf16[32,25,1408]{2,1,0:T(8,128)(2,1)} reshape(bf16[1,1,800,1408]{3,2,1,0:T(8,128)(2,1)} %param.15) | data formatting | bytes 4505600 | tf_op jit(solution)/shard_map/reshape | solution.py:57
  93.6 4.5 %fusion.44 = (bf16[32,25,704]{2,1,0:T(8,128)(2,1)}, bf16[32,25,704]{2,1,0:T(8,128)(2,1)}) fusion(bf16[32,25,1408]{2,1,0:T(8,128)(2,1)} %reshape.129), kind=kLoop, calls=%fused_computation.66 | loop fusion | bytes 4505600 | tf_op jit(solution)/shard_map/slice | solution.py:59
  98.1 6.5 %reshape.128 = bf16[32,25,2048]{2,1,0:T(8,128)(2,1)} reshape(bf16[32,400,128]{2,1,0:T(8,128)(2,1)} %all-to-all-done) | data formatting | bytes 6553600 | tf_op jit(solution)/shard_map/reshape | solution.py:75
  104.6 11.3 %fusion.28 = (bf16[32,25,704]{2,0,1:T(8,128)(2,1)S(1)}, bf16[32,25,704]{2,0,1:T(8,128)(2,1)}) fusion(bf16[32,25,704]{2,1,0:T(8,128)(2,1)} %get-tuple-element.30, bf16[32,25,704]{2,1,0:T(8,128)(2,1)} %get-tuple-element.31, bf16[1,704,2048]{2,1,0:T(8,128)(2,1)S(1)} %copy-done, bf16[32,25,2048]{2,1,0:T(8,128)(2,1)} %reshape.128), kind=kOutput, calls=%fused_computation.38 | convolution fusion | flops 2315315200 | bytes 10665984 | tf_op jit(solution)/shard_map/dot_general | solution.py:78
  119.2 2.1 copy.79
  122.8 2.0 pad_maximum_fusion
  124.8 11.3 %fusion.3 = bf16[32,25,2048]{2,1,0:T(8,128)(2,1)} fusion(bf16[1,2048,1408]{2,1,0:T(8,128)(2,1)} %param.13, bf16[32,25,1408]{2,0,1:T(8,128)(2,1)S(1)} %pad_maximum_fusion), kind=kOutput, calls=%fused_computation.8 | convolution fusion | flops 4615372800 | bytes 11296768 | tf_op jit(solution)/shard_map/dot_general | solution.py:88
  136.1 12.4 %multiply_convert_fusion = bf16[2048,1408]{1,0:T(8,128)(2,1)} fusion(f32[]{:T(128)S(6)} %convert_element_type.56, bf16[100,8,16,128]{3,2,1,0:T(8,128)(2,1)} %bitcast.31, bf16[800,704]{1,0:T(8,128)(2,1)S(1)} %copy-done.6, bf16[800,704]{1,0:T(8,128)(2,1)S(1)} %copy-done.5), kind=kOutput, calls=%fused_computation.2 | convolution fusion | flops 4624007168 | bytes 11296772 | tf_op jit(solution)/shard_map/dot_general | solution.py:97
  148.6 7.6 %all-to-all-start.2 = ((bf16[32,25,2048]{2,1,0:T(8,128)(2,1)}), bf16[32,25,2048]{2,1,0:T(8,128)(2,1)}, u32[]{:S(2)}, u32[]{:S(2)}) async-start(bf16[32,25,2048]{2,1,0:T(8,128)(2,1)} %fusion.3), calls=%async_computation.2 | async-start | bytes 8388608 | tf_op jit(solution)/shard_map/all_to_all | solution.py:93
  157.4 49.1 %all-to-all-done.2 = bf16[32,25,2048]{2,1,0:T(8,128)(2,1)} async-done(((bf16[32,25,2048]{2,1,0:T(8,128)(2,1)}), bf16[32,25,2048]{2,1,0:T(8,128)(2,1)}, u32[]{:S(2)}, u32[]{:S(2)}) %all-to-all-start.2) | async-done | bytes 3276832 | tf_op jit(solution)/shard_map/all_to_all | solution.py:93
  206.5 5.3 %fusion.33 = bf16[128,2048]{1,0:T(8,128)(2,1)} fusion(pred[32,25,128]{2,0,1:T(8,128)(4,1)S(1)} %get-tuple-element.27, bf16[32,25,2048]{2,1,0:T(8,128)(2,1)} %all-to-all-done.2), kind=kOutput, calls=%fused_computation.43 | convolution fusion | flops 419692544 | bytes 3903488 | tf_op jit(solution)/shard_map/dot_general | solution.py:101
  211.7 9.9 %reduce-scatter.3.cloned.1.call-done = bf16[256,1408]{1,0:T(8,128)(2,1)} async-done(((bf16[2048,1408]{1,0:T(8,128)(2,1)}), bf16[256,1408]{1,0:T(8,128)(2,1)}) %reduce-scatter.3.cloned.1.call-update) | async-done | bytes 720912 | tf_op jit(solution)/shard_map/reduce_scatter | solution.py:99
  221.7 2.2 maximum_bitcast_fusion
  223.8 2.3 copy.81
  (52 shorter events, 15.1 us)
Async XLA Ops:
  7.2 97.5 %copy-start = (bf16[1,704,2048]{2,1,0:T(8,128)(2,1)S(1)}, bf16[1,704,2048]{2,1,0:T(8,128)(2,1)}, u32[]{:S(2)}) copy-start(bf16[1,704,2048]{2,1,0:T(8,128)(2,1)} %param.14) | copy-start | bytes 8650756
  25.2 8.8 %copy-start.7 = (s32[8]{0:T(128)S(1)}, s32[8]{0:T(128)}, u32[]{:S(2)}) copy-start(s32[8]{0:T(128)} %param.12) | copy-start | bytes 100
  25.2 49.3 %all-to-all-start = ((bf16[32,400,128]{2,1,0:T(8,128)(2,1)}), bf16[32,400,128]{2,1,0:T(8,128)(2,1)}, u32[]{:S(2)}, u32[]{:S(2)}) async-start(bf16[32,400,128]{2,1,0:T(8,128)(2,1)} %fusion), calls=%async_computation | async-start | bytes 6553600 | tf_op jit(solution)/shard_map/all_to_all | solution.py:63
  34.0 122.2 %reduce-scatter.5.cloned.1.call-start = ((), (), s32[]{:S(2)}) async-start(), calls=%async_computation.6 | async-start | bytes 3244032 | tf_op jit(solution)/shard_map/reduce_scatter | solution.py:76
  40.6 7.4 %copy-start.2 = (bf16[1,1,800,1408]{3,2,1,0:T(8,128)(2,1)S(1)}, bf16[1,1,800,1408]{3,2,1,0:T(8,128)(2,1)}, u32[]{:S(2)}) copy-start(bf16[1,1,800,1408]{3,2,1,0:T(8,128)(2,1)} %param.15) | copy-start | bytes 6758404
  81.6 54.5 %all-to-all-start.1 = ((bf16[32,400,128]{2,1,0:T(8,128)(2,1)}), bf16[32,400,128]{2,1,0:T(8,128)(2,1)}, u32[]{:S(2)}, u32[]{:S(2)}) async-start(bf16[32,400,128]{2,1,0:T(8,128)(2,1)} %bitcast_select_fusion), calls=%async_computation.1 | async-start | bytes 6553600 | tf_op jit(solution)/shard_map/all_to_all | solution.py:65
  89.1 132.6 %reduce-scatter.3.cloned.1.call-start = ((), (), s32[]{:S(2)}) async-start(), calls=%async_computation.5 | async-start | bytes 6488064 | tf_op jit(solution)/shard_map/reduce_scatter | solution.py:99
  115.9 1.0 copy-start.3
  119.2 3.6 %copy-start.4 = (bf16[32,25,704]{2,0,1:T(8,128)(2,1)S(1)}, bf16[32,25,704]{2,0,1:T(8,128)(2,1)}, u32[]{:S(2)}) copy-start(bf16[32,25,704]{2,0,1:T(8,128)(2,1)} %copy-done.3) | copy-start | bytes 3379204
  124.8 11.3 %copy-start.5 = (bf16[800,704]{1,0:T(8,128)(2,1)S(1)}, bf16[800,704]{1,0:T(8,128)(2,1)}, u32[]{:S(2)}) copy-start(bf16[800,704]{1,0:T(8,128)(2,1)} %concatenate.16) | copy-start | bytes 3379204
  124.8 11.3 %copy-start.6 = (bf16[800,704]{1,0:T(8,128)(2,1)S(1)}, bf16[800,704]{1,0:T(8,128)(2,1)}, u32[]{:S(2)}) copy-start(bf16[800,704]{1,0:T(8,128)(2,1)} %concatenate.17) | copy-start | bytes 3379204
  148.6 57.9 %all-to-all-start.2 = ((bf16[32,25,2048]{2,1,0:T(8,128)(2,1)}), bf16[32,25,2048]{2,1,0:T(8,128)(2,1)}, u32[]{:S(2)}, u32[]{:S(2)}) async-start(bf16[32,25,2048]{2,1,0:T(8,128)(2,1)} %fusion.3), calls=%async_computation.2 | async-start | bytes 8388608 | tf_op jit(solution)/shard_map/all_to_all | solution.py:93
  206.4 19.7 %copy-start.1 = (bf16[1,704,2048]{2,1,0:T(8,128)(2,1)S(1)}, bf16[1,704,2048]{2,1,0:T(8,128)(2,1)}, u32[]{:S(2)}) copy-start(bf16[1,704,2048]{2,1,0:T(8,128)(2,1)} %param.14) | copy-start | bytes 8650756
Sparse Core Ops, SparseCore 0:
  81.7 42.4 reduce-scatter.4
  148.7 72.9 reduce-scatter.2

commit v7 on v4

--- a/solution.py
+++ b/solution.py
@@ -25,8 +25,12 @@
     f32, bf16 = jnp.float32, jnp.bfloat16
 
     flat_ids = expert_ids.reshape(-1)
-    onehot = (flat_ids[:, None] == jnp.arange(experts, dtype=jnp.int32)[None, :]).astype(jnp.int32)
-    slot_rank = jnp.sum(jnp.cumsum(onehot, axis=0) * onehot, axis=1) - 1
+    entries = flat_ids.shape[0]
+    onehot = (flat_ids[:, None] == jnp.arange(experts, dtype=jnp.int32)[None, :]).astype(bf16)
+    order = jnp.arange(entries, dtype=jnp.int32)
+    earlier = (order[:, None] > order[None, :]).astype(bf16)
+    before = lax.dot_general(earlier, onehot, (((1,), (0,)), ((), ())), preferred_element_type=f32)
+    slot_rank = jnp.sum(before * onehot.astype(f32), axis=1).astype(jnp.int32)
     ids4 = flat_ids.reshape(1, 1, tok_count, fanout)
     rank4 = slot_rank.reshape(1, 1, tok_count, fanout)
     sel = (ids4 == jnp.arange(experts, dtype=jnp.int32)[:, None, None, None]) & (

time: 228 us -> 226 us (level)
  no operation moved by 1% of the time
where the time goes in v7:
time: 226 us
  waiting for transfers between devices  94 us (42%)
  matrix products  52 us (23%)
  local copies, waits for them, and re-layouts  24.4 us (11%)
  starting transfers between devices  24.4 us (11%)
  other arithmetic  15.8 us (7%)
  between operations  14.9 us (7%)
    all_to_all x1, waiting for transfers between devices, per_device(): arrived = lax.all_to_all(row_major(slot_grads), 'expert', 0, 0, tiled=True)  49 us
    all_to_all x1, waiting for transfers between devices, per_device(): s_recv = lax.all_to_all(row_major(s_send), 'expert', 0, 0, tiled=True)  27.7 us
    dot_general x1, matrix products, per_device(): lax.dot_general(x_rows, pre_rows, (((0,), (0,)), ((), ())), preferred_ele...  12.4 us
    dot_general x1, matrix products, per_device(): lax.dot_general(pre_grad, w_in[0], (((2,), (1,)), ((), ())), preferred_el...  11.1 us
    dot_general x1, matrix products, per_device(): lax.dot_general(s_recv, w_down[0], (((2,), (1,)), ((), ())), preferred_el...  11.1 us
    all_to_all x1, waiting for transfers between devices, per_device(): x_recv = lax.all_to_all(row_major(x_send), 'expert', 0, 0, tiled=True)  9.12 us
    all_to_all x1, starting transfers between devices, per_device(): s_recv = lax.all_to_all(row_major(s_send), 'expert', 0, 0, tiled=True)  8.78 us
    reduce_scatter x1, waiting for transfers between devices, per_device(): in_block = lax.psum_scatter(in_part, 'dp', scatter_dimension=0, tiled=True)  8.04 us
  transfers between devices with their start and end apart: 5, of which 4 were waited for; matrix products, arithmetic and copies ran while one was open for 31% of the time, Pallas kernels for 0%

profile of v7, /device:TPU:1, one launch (start us, length us, event | category | flops | bytes accessed | tf_op | source)
XLA Modules:
  0.0 225.6 jit_solution(11317991101015988063)
XLA Ops:
  11.3 4.3 %multiply_convert_fusion.1 = bf16[32,25,2048]{2,1,0:T(8,128)(2,1)} fusion(f32[32,25]{1,0:T(8,128)S(1)} %copy.69, bf16[128,2048]{1,0:T(8,128)(2,1)} %param.9, pred[32,25,128]{2,0,1:T(8,128)(4,1)S(1)} %get-tuple-element.27), kind=kOutput, calls=%fused_computation.2 | convolution fusion | flops 422707200 | bytes 3906688 | tf_op jit(solution)/shard_map/dot_general | solution.py:44
  15.6 8.8 %all-to-all-start = ((bf16[32,25,2048]{2,1,0:T(8,128)(2,1)}), bf16[32,25,2048]{2,1,0:T(8,128)(2,1)}, u32[]{:S(2)}, u32[]{:S(2)}) async-start(bf16[32,25,2048]{2,1,0:T(8,128)(2,1)} %multiply_convert_fusion.1), calls=%async_computation | async-start | bytes 8388608 | tf_op jit(solution)/shard_map/all_to_all | solution.py:61
  27.8 4.3 %reshape.85 = bf16[32,25,1408]{2,1,0:T(8,128)(2,1)} reshape(bf16[1,1,800,1408]{3,2,1,0:T(8,128)(2,1)} %param.15) | data formatting | bytes 4505600 | tf_op jit(solution)/shard_map/reshape | solution.py:54
  32.1 4.0 %gather_fusion = bf16[800,16,128]{2,1,0:T(8,128)(2,1)} fusion(bf16[128,16,128]{2,1,0:T(8,128)(2,1)S(1)} %bitcast.44, s32[1024]{0:T(1024)S(1)} %pad_clamp_fusion), kind=kCustom, calls=%fused_computation | custom fusion | bytes 6556800 | tf_op jit(solution)/shard_map/gather | solution.py:51
  36.1 2.9 %fusion.42 = (bf16[32,25,704]{2,1,0:T(8,128)(2,1)S(1)}, bf16[32,25,704]{2,1,0:T(8,128)(2,1)S(1)}) fusion(bf16[32,25,1408]{2,1,0:T(8,128)(2,1)} %reshape.85), kind=kLoop, calls=%fused_computation.60 | loop fusion | bytes 4505600 | tf_op jit(solution)/shard_map/slice | solution.py:55
  39.0 5.2 %bitcast_select_fusion = bf16[32,400,128]{2,1,0:T(8,128)(2,1)} fusion(pred[32,400]{1,0:T(8,128)(4,1)S(1)} %copy.67, bf16[32,400,128]{2,1,0:T(8,128)(2,1)S(1)} %bitcast.45), kind=kLoop, calls=%fused_computation.16 | loop fusion | flops 1638400 | bytes 6566400 | tf_op jit(solution)/shard_map/jit(_where)/select_n | solution.py:51
  44.2 2.7 %fusion.17 = bf16[32,25,704]{2,0,1:T(8,128)(2,1)} fusion(bf16[32,25,704]{2,1,0:T(8,128)(2,1)S(1)} %get-tuple-element.31, bf16[32,25,704]{2,1,0:T(8,128)(2,1)S(1)} %get-tuple-element.30), kind=kLoop, calls=%fused_computation.26 | loop fusion | flops 4505600 | bytes 3379200 | tf_op jit(solution)/shard_map/convert_element_type | solution.py:59
  46.9 27.7 %all-to-all-done = bf16[32,25,2048]{2,1,0:T(8,128)(2,1)} async-done(((bf16[32,25,2048]{2,1,0:T(8,128)(2,1)}), bf16[32,25,2048]{2,1,0:T(8,128)(2,1)}, u32[]{:S(2)}, u32[]{:S(2)}) %all-to-all-start) | async-done | bytes 3276832 | tf_op jit(solution)/shard_map/all_to_all | solution.py:61
  74.7 7.5 %fusion.2 = bf16[2048,704]{0,1:T(8,128)(2,1)} fusion(bf16[32,25,2048]{2,1,0:T(8,128)(2,1)} %all-to-all-done, f32[]{:T(128)S(6)} %convert_element_type.55, bf16[32,25,704]{2,0,1:T(8,128)(2,1)} %fusion.17), kind=kOutput, calls=%fused_computation.6 | convolution fusion | flops 2309750784 | bytes 7286788 | tf_op jit(solution)/shard_map/dot_general | solution.py:67
  82.2 7.9 %all-to-all-start.1 = ((bf16[32,400,128]{2,1,0:T(8,128)(2,1)}), bf16[32,400,128]{2,1,0:T(8,128)(2,1)}, u32[]{:S(2)}, u32[]{:S(2)}) async-start(bf16[32,400,128]{2,1,0:T(8,128)(2,1)} %bitcast_select_fusion), calls=%async_computation.1 | async-start | bytes 6553600 | tf_op jit(solution)/shard_map/all_to_all | solution.py:63
  90.3 11.1 %fusion.20 = (bf16[32,25,704]{2,0,1:T(8,128)(2,1)S(1)}, bf16[32,25,704]{2,0,1:T(8,128)(2,1)}) fusion(bf16[32,25,704]{2,1,0:T(8,128)(2,1)} %copy-done.4, bf16[32,25,704]{2,1,0:T(8,128)(2,1)} %copy-done.3, bf16[1,704,2048]{2,1,0:T(8,128)(2,1)S(1)} %copy-done, bf16[32,25,2048]{2,1,0:T(8,128)(2,1)} %all-to-all-done), kind=kOutput, calls=%fused_computation.29 | convolution fusion | flops 2315315200 | bytes 10665984 | tf_op jit(solution)/shard_map/dot_general | solution.py:72
  103.2 1.7 concatenate.16
  104.9 2.1 copy.78
  107.0 1.5 concatenate.17
  108.5 2.0 pad_maximum_fusion
  110.5 11.1 %fusion.3 = bf16[32,25,2048]{2,1,0:T(8,128)(2,1)} fusion(bf16[1,2048,1408]{2,1,0:T(8,128)(2,1)} %param.13, bf16[32,25,1408]{2,0,1:T(8,128)(2,1)S(1)} %pad_maximum_fusion), kind=kOutput, calls=%fused_computation.7 | convolution fusion | flops 4615372800 | bytes 11296768 | tf_op jit(solution)/shard_map/dot_general | solution.py:82
  121.7 9.1 %all-to-all-done.1 = bf16[32,400,128]{2,1,0:T(8,128)(2,1)} async-done(((bf16[32,400,128]{2,1,0:T(8,128)(2,1)}), bf16[32,400,128]{2,1,0:T(8,128)(2,1)}, u32[]{:S(2)}, u32[]{:S(2)}) %all-to-all-start.1) | async-done | bytes 3276832 | tf_op jit(solution)/shard_map/all_to_all | solution.py:63
  130.8 12.4 %multiply_convert_fusion = bf16[2048,1408]{1,0:T(8,128)(2,1)} fusion(f32[]{:T(128)S(6)} %convert_element_type.55, bf16[100,8,16,128]{3,2,1,0:T(8,128)(2,1)} %bitcast.17, bf16[800,704]{1,0:T(8,128)(2,1)S(1)} %copy-done.8, bf16[800,704]{1,0:T(8,128)(2,1)S(1)} %copy-done.7), kind=kOutput, calls=%fused_computation.1 | convolution fusion | flops 4624007168 | bytes 11296772 | tf_op jit(solution)/shard_map/dot_general | solution.py:91
  143.3 7.5 %all-to-all-start.2 = ((bf16[32,25,2048]{2,1,0:T(8,128)(2,1)}), bf16[32,25,2048]{2,1,0:T(8,128)(2,1)}, u32[]{:S(2)}, u32[]{:S(2)}) async-start(bf16[32,25,2048]{2,1,0:T(8,128)(2,1)} %fusion.3), calls=%async_computation.2 | async-start | bytes 8388608 | tf_op jit(solution)/shard_map/all_to_all | solution.py:87
  151.9 49.0 %all-to-all-done.2 = bf16[32,25,2048]{2,1,0:T(8,128)(2,1)} async-done(((bf16[32,25,2048]{2,1,0:T(8,128)(2,1)}), bf16[32,25,2048]{2,1,0:T(8,128)(2,1)}, u32[]{:S(2)}, u32[]{:S(2)}) %all-to-all-start.2) | async-done | bytes 3276832 | tf_op jit(solution)/shard_map/all_to_all | solution.py:87
  200.9 5.3 %fusion.26 = bf16[128,2048]{1,0:T(8,128)(2,1)} fusion(pred[32,25,128]{2,0,1:T(8,128)(4,1)S(1)} %get-tuple-element.27, bf16[32,25,2048]{2,1,0:T(8,128)(2,1)} %all-to-all-done.2), kind=kOutput, calls=%fused_computation.36 | convolution fusion | flops 419692544 | bytes 3903488 | tf_op jit(solution)/shard_map/dot_general | solution.py:95
  206.2 8.0 %reduce-scatter.3.cloned.1.call-done = bf16[256,1408]{1,0:T(8,128)(2,1)} async-done(((bf16[2048,1408]{1,0:T(8,128)(2,1)}), bf16[256,1408]{1,0:T(8,128)(2,1)}) %reduce-scatter.3.cloned.1.call-update) | async-done | bytes 720912 | tf_op jit(solution)/shard_map/reduce_scatter | solution.py:93
  214.2 2.2 maximum_bitcast_fusion
  216.4 2.3 %copy.80 = bf16[1,256,2112]{1,2,0:T(8,128)(2,1)} copy(bf16[1,256,2112]{2,1,0:T(8,128)(2,1)} %maximum_bitcast_fusion) | data formatting | bytes 2162688
  (47 shorter events, 10.0 us)
Async XLA Ops:
  7.2 83.2 %copy-start = (bf16[1,704,2048]{2,1,0:T(8,128)(2,1)S(1)}, bf16[1,704,2048]{2,1,0:T(8,128)(2,1)}, u32[]{:S(2)}) copy-start(bf16[1,704,2048]{2,1,0:T(8,128)(2,1)} %param.14) | copy-start | bytes 8650756
  15.6 8.8 %copy-start.9 = (s32[8]{0:T(128)S(1)}, s32[8]{0:T(128)}, u32[]{:S(2)}) copy-start(s32[8]{0:T(128)} %param.12) | copy-start | bytes 100
  15.6 59.0 %all-to-all-start = ((bf16[32,25,2048]{2,1,0:T(8,128)(2,1)}), bf16[32,25,2048]{2,1,0:T(8,128)(2,1)}, u32[]{:S(2)}, u32[]{:S(2)}) async-start(bf16[32,25,2048]{2,1,0:T(8,128)(2,1)} %multiply_convert_fusion.1), calls=%async_computation | async-start | bytes 8388608 | tf_op jit(solution)/shard_map/all_to_all | solution.py:61
  24.4 126.4 %reduce-scatter.5.cloned.1.call-start = ((), (), s32[]{:S(2)}) async-start(), calls=%async_computation.6 | async-start | bytes 3244032 | tf_op jit(solution)/shard_map/reduce_scatter | solution.py:70
  36.1 3.0 %copy-start.2 = (bf16[800,16,128]{2,1,0:T(8,128)(2,1)S(1)}, bf16[800,16,128]{2,1,0:T(8,128)(2,1)}, u32[]{:S(2)}) copy-start(bf16[800,16,128]{2,1,0:T(8,128)(2,1)} %gather_fusion) | copy-start | bytes 9830404
  39.0 5.2 %copy-start.3 = (bf16[32,25,704]{2,1,0:T(8,128)(2,1)}, bf16[32,25,704]{2,1,0:T(8,128)(2,1)S(1)}, u32[]{:S(2)}) copy-start(bf16[32,25,704]{2,1,0:T(8,128)(2,1)S(1)} %get-tuple-element.30) | copy-start | bytes 3379204
  39.0 5.2 %copy-start.4 = (bf16[32,25,704]{2,1,0:T(8,128)(2,1)}, bf16[32,25,704]{2,1,0:T(8,128)(2,1)S(1)}, u32[]{:S(2)}) copy-start(bf16[32,25,704]{2,1,0:T(8,128)(2,1)S(1)} %get-tuple-element.31) | copy-start | bytes 3379204
  82.2 48.6 %all-to-all-start.1 = ((bf16[32,400,128]{2,1,0:T(8,128)(2,1)}), bf16[32,400,128]{2,1,0:T(8,128)(2,1)}, u32[]{:S(2)}, u32[]{:S(2)}) async-start(bf16[32,400,128]{2,1,0:T(8,128)(2,1)} %bitcast_select_fusion), calls=%async_computation.1 | async-start | bytes 6553600 | tf_op jit(solution)/shard_map/all_to_all | solution.py:63
  90.1 124.1 %reduce-scatter.3.cloned.1.call-start = ((), (), s32[]{:S(2)}) async-start(), calls=%async_computation.5 | async-start | bytes 6488064 | tf_op jit(solution)/shard_map/reduce_scatter | solution.py:93
  101.5 1.0 copy-start.5
  104.9 3.6 %copy-start.6 = (bf16[32,25,704]{2,0,1:T(8,128)(2,1)S(1)}, bf16[32,25,704]{2,0,1:T(8,128)(2,1)}, u32[]{:S(2)}) copy-start(bf16[32,25,704]{2,0,1:T(8,128)(2,1)} %copy-done.5) | copy-start | bytes 3379204
  110.5 20.3 %copy-start.7 = (bf16[800,704]{1,0:T(8,128)(2,1)S(1)}, bf16[800,704]{1,0:T(8,128)(2,1)}, u32[]{:S(2)}) copy-start(bf16[800,704]{1,0:T(8,128)(2,1)} %concatenate.16) | copy-start | bytes 3379204
  110.5 20.3 %copy-start.8 = (bf16[800,704]{1,0:T(8,128)(2,1)S(1)}, bf16[800,704]{1,0:T(8,128)(2,1)}, u32[]{:S(2)}) copy-start(bf16[800,704]{1,0:T(8,128)(2,1)} %concatenate.17) | copy-start | bytes 3379204
  143.3 57.7 %all-to-all-start.2 = ((bf16[32,25,2048]{2,1,0:T(8,128)(2,1)}), bf16[32,25,2048]{2,1,0:T(8,128)(2,1)}, u32[]{:S(2)}, u32[]{:S(2)}) async-start(bf16[32,25,2048]{2,1,0:T(8,128)(2,1)} %fusion.3), calls=%async_computation.2 | async-start | bytes 8388608 | tf_op jit(solution)/shard_map/all_to_all | solution.py:87
  200.9 17.8 %copy-start.1 = (bf16[1,704,2048]{2,1,0:T(8,128)(2,1)S(1)}, bf16[1,704,2048]{2,1,0:T(8,128)(2,1)}, u32[]{:S(2)}) copy-start(bf16[1,704,2048]{2,1,0:T(8,128)(2,1)} %param.14) | copy-start | bytes 8650756
Sparse Core Ops, SparseCore 0:
  82.3 42.7 reduce-scatter.4
  143.4 70.8 reduce-scatter.2

commit v8 on v7

--- a/solution.py
+++ b/solution.py
@@ -95,8 +95,9 @@
     in_grad = lax.dot_general(
         tok_sel_b, arrived, (((0, 1), (0, 1)), ((), ())), preferred_element_type=f32
     ).astype(bf16)
-    weight_block = jnp.concatenate([in_block, down_block], axis=1)
-    return (in_grad, weight_block[None])
+    weight_block = jnp.concatenate([in_block, down_block], axis=1)[None]
+    weight_block = with_layout_constraint(weight_block, Layout(major_to_minor=(0, 2, 1)))
+    return (in_grad, weight_block)
 
 
 def solution(mesh):

time: 226 us -> 223 us (0.987)
  blocking collectives: 0 us -> 58 us
  waiting for transfers between devices: 94 us -> 47.1 us
  starting transfers between devices: 24.4 us -> 17 us
  matrix products: 52 us -> 48.5 us
  local copies, waits for them, and re-layouts: 24.4 us -> 21 us
    all_to_all x0 -> x1, blocking collectives: none -> 58 us  [per_device(): arrived = lax.all_to_all(row_major(slot_grads), 'expert', 0, 0, tiled=True)]
    all_to_all x1 -> x0, waiting for transfers between devices: 49 us -> none  [per_device(): arrived = lax.all_to_all(row_major(slot_grads), 'expert', 0, 0, tiled=True)]
    all_to_all x1 -> x0, starting transfers between devices: 7.47 us -> none  [per_device(): arrived = lax.all_to_all(row_major(slot_grads), 'expert', 0, 0, tiled=True)]
    dot_general x1, matrix products: 5.27 us -> 2.88 us  [per_device(): lax.dot_general(tok_sel_b, arrived, (((0, 1), (0, 1)), ((), ())), preferr...]
    unnamed x23 -> x22, local copies, waits for them, and re-layouts: 5.34 us -> 3.04 us
  transfers between devices with their start and end apart: 5 -> 4, of which waited for: 4 -> 3; matrix products, arithmetic and copies ran while one was open for 31% -> 30% of each run, Pallas kernels for 0% -> 0%
where the time goes in v8:
time: 223 us; the launch traced here: 222 us
  blocking collectives  58 us (26%)
  matrix products  48.5 us (22%)
  waiting for transfers between devices  47.1 us (21%)
  local copies, waits for them, and re-layouts  21 us (9%)
  starting transfers between devices  17 us (8%)
  other arithmetic  15.8 us (7%)
  between operations  14.9 us (7%)
    all_to_all x1, blocking collectives, per_device(): arrived = lax.all_to_all(row_major(slot_grads), 'expert', 0, 0, tiled=True)  58 us
    all_to_all x1, waiting for transfers between devices, per_device(): s_recv = lax.all_to_all(row_major(s_send), 'expert', 0, 0, tiled=True)  27.9 us
    dot_general x1, matrix products, per_device(): lax.dot_general(x_rows, pre_rows, (((0,), (0,)), ((), ())), preferred_ele...  11.3 us
    dot_general x1, matrix products, per_device(): lax.dot_general(s_recv, w_down[0], (((2,), (1,)), ((), ())), preferred_el...  11.1 us
    dot_general x1, matrix products, per_device(): lax.dot_general(pre_grad, w_in[0], (((2,), (1,)), ((), ())), preferred_el...  11.1 us
    reduce_scatter x1, waiting for transfers between devices, per_device(): in_block = lax.psum_scatter(in_part, 'dp', scatter_dimension=0, tiled=True)  10.1 us
    all_to_all x1, waiting for transfers between devices, per_device(): x_recv = lax.all_to_all(row_major(x_send), 'expert', 0, 0, tiled=True)  9.01 us
    all_to_all x1, starting transfers between devices, per_device(): s_recv = lax.all_to_all(row_major(s_send), 'expert', 0, 0, tiled=True)  8.78 us
  transfers between devices with their start and end apart: 4, of which 3 were waited for; matrix products, arithmetic and copies ran while one was open for 30% of the time, Pallas kernels for 0%

profile of v8, /device:TPU:1, one launch (start us, length us, event | category | flops | bytes accessed | tf_op | source)
XLA Modules:
  0.0 222.2 jit_solution(1740515858939945065)
XLA Ops:
  10.1 1.1 fusion.25
  11.3 4.2 %multiply_convert_fusion.1 = bf16[32,25,2048]{2,1,0:T(8,128)(2,1)} fusion(f32[32,25]{1,0:T(8,128)S(1)} %copy.65, bf16[128,2048]{1,0:T(8,128)(2,1)} %param.9, pred[32,25,128]{2,0,1:T(8,128)(4,1)S(1)} %get-tuple-element.17), kind=kOutput, calls=%fused_computation.2 | convolution fusion | flops 422707200 | bytes 3906688 | tf_op jit(solution)/shard_map/dot_general | solution.py:44
  15.6 8.8 %all-to-all-start = ((bf16[32,25,2048]{2,1,0:T(8,128)(2,1)}), bf16[32,25,2048]{2,1,0:T(8,128)(2,1)}, u32[]{:S(2)}, u32[]{:S(2)}) async-start(bf16[32,25,2048]{2,1,0:T(8,128)(2,1)} %multiply_convert_fusion.1), calls=%async_computation | async-start | bytes 8388608 | tf_op jit(solution)/shard_map/all_to_all | solution.py:61
  26.6 1.1 copy.83
  27.7 4.3 %reshape.85 = bf16[32,25,1408]{2,1,0:T(8,128)(2,1)} reshape(bf16[1,1,800,1408]{3,2,1,0:T(8,128)(2,1)} %param.15) | data formatting | bytes 4505600 | tf_op jit(solution)/shard_map/reshape | solution.py:54
  32.0 4.0 %gather_fusion = bf16[800,16,128]{2,1,0:T(8,128)(2,1)} fusion(bf16[128,16,128]{2,1,0:T(8,128)(2,1)S(1)} %bitcast.44, s32[1024]{0:T(1024)S(1)} %pad_clamp_fusion), kind=kCustom, calls=%fused_computation | custom fusion | bytes 6556800 | tf_op jit(solution)/shard_map/gather | solution.py:51
  36.0 2.9 %fusion.42 = (bf16[32,25,704]{2,1,0:T(8,128)(2,1)S(1)}, bf16[32,25,704]{2,1,0:T(8,128)(2,1)S(1)}) fusion(bf16[32,25,1408]{2,1,0:T(8,128)(2,1)} %reshape.85), kind=kLoop, calls=%fused_computation.60 | loop fusion | bytes 4505600 | tf_op jit(solution)/shard_map/slice | solution.py:55
  39.0 5.1 %bitcast_select_fusion = bf16[32,400,128]{2,1,0:T(8,128)(2,1)} fusion(pred[32,400]{1,0:T(8,128)(4,1)S(1)} %copy.63, bf16[32,400,128]{2,1,0:T(8,128)(2,1)S(1)} %bitcast.45), kind=kLoop, calls=%fused_computation.16 | loop fusion | flops 1638400 | bytes 6566400 | tf_op jit(solution)/shard_map/jit(_where)/select_n | solution.py:51
  44.1 2.6 %fusion.17 = bf16[32,25,704]{2,0,1:T(8,128)(2,1)} fusion(bf16[32,25,704]{2,1,0:T(8,128)(2,1)S(1)} %get-tuple-element.21, bf16[32,25,704]{2,1,0:T(8,128)(2,1)S(1)} %get-tuple-element.20), kind=kLoop, calls=%fused_computation.26 | loop fusion | flops 4505600 | bytes 3379200 | tf_op jit(solution)/shard_map/convert_element_type | solution.py:59
  46.7 27.9 %all-to-all-done = bf16[32,25,2048]{2,1,0:T(8,128)(2,1)} async-done(((bf16[32,25,2048]{2,1,0:T(8,128)(2,1)}), bf16[32,25,2048]{2,1,0:T(8,128)(2,1)}, u32[]{:S(2)}, u32[]{:S(2)}) %all-to-all-start) | async-done | bytes 3276832 | tf_op jit(solution)/shard_map/all_to_all | solution.py:61
  74.6 7.5 %fusion.2 = bf16[2048,704]{0,1:T(8,128)(2,1)} fusion(bf16[32,25,2048]{2,1,0:T(8,128)(2,1)} %all-to-all-done, f32[]{:T(128)S(6)} %convert_element_type.55, bf16[32,25,704]{2,0,1:T(8,128)(2,1)} %fusion.17), kind=kOutput, calls=%fused_computation.6 | convolution fusion | flops 2309750784 | bytes 7286788 | tf_op jit(solution)/shard_map/dot_general | solution.py:67
  82.1 7.9 %all-to-all-start.1 = ((bf16[32,400,128]{2,1,0:T(8,128)(2,1)}), bf16[32,400,128]{2,1,0:T(8,128)(2,1)}, u32[]{:S(2)}, u32[]{:S(2)}) async-start(bf16[32,400,128]{2,1,0:T(8,128)(2,1)} %bitcast_select_fusion), calls=%async_computation.1 | async-start | bytes 6553600 | tf_op jit(solution)/shard_map/all_to_all | solution.py:63
  90.3 11.1 %fusion.20 = (bf16[32,25,704]{2,0,1:T(8,128)(2,1)S(1)}, bf16[32,25,704]{2,0,1:T(8,128)(2,1)}) fusion(bf16[32,25,704]{2,1,0:T(8,128)(2,1)} %copy-done.4, bf16[32,25,704]{2,1,0:T(8,128)(2,1)} %copy-done.3, bf16[1,704,2048]{2,1,0:T(8,128)(2,1)S(1)} %copy-done, bf16[32,25,2048]{2,1,0:T(8,128)(2,1)} %all-to-all-done), kind=kOutput, calls=%fused_computation.29 | convolution fusion | flops 2315315200 | bytes 10665984 | tf_op jit(solution)/shard_map/dot_general | solution.py:72
  103.2 1.7 concatenate.16
  104.9 2.1 copy.74
  107.1 1.5 concatenate.17
  108.6 2.0 pad_maximum_fusion
  110.6 11.1 %fusion.3 = bf16[32,25,2048]{2,1,0:T(8,128)(2,1)} fusion(bf16[1,2048,1408]{2,1,0:T(8,128)(2,1)} %param.13, bf16[32,25,1408]{2,0,1:T(8,128)(2,1)S(1)} %pad_maximum_fusion), kind=kOutput, calls=%fused_computation.7 | convolution fusion | flops 4615372800 | bytes 11296768 | tf_op jit(solution)/shard_map/dot_general | solution.py:82
  121.7 9.0 %all-to-all-done.1 = bf16[32,400,128]{2,1,0:T(8,128)(2,1)} async-done(((bf16[32,400,128]{2,1,0:T(8,128)(2,1)}), bf16[32,400,128]{2,1,0:T(8,128)(2,1)}, u32[]{:S(2)}, u32[]{:S(2)}) %all-to-all-start.1) | async-done | bytes 3276832 | tf_op jit(solution)/shard_map/all_to_all | solution.py:63
  130.8 11.3 %multiply_convert_fusion = bf16[2048,1408]{0,1:T(8,128)(2,1)} fusion(f32[]{:T(128)S(6)} %convert_element_type.55, bf16[100,8,16,128]{3,2,1,0:T(8,128)(2,1)} %bitcast.17, bf16[800,704]{1,0:T(8,128)(2,1)S(1)} %copy-done.8, bf16[800,704]{1,0:T(8,128)(2,1)S(1)} %copy-done.7), kind=kOutput, calls=%fused_computation.1 | convolution fusion | flops 4624007168 | bytes 11296772 | tf_op jit(solution)/shard_map/dot_general | solution.py:91
  142.1 58.0 %all_to_all.15 = bf16[32,25,2048]{2,1,0:T(8,128)(2,1)S(1)} all-to-all(bf16[32,25,2048]{2,1,0:T(8,128)(2,1)} %fusion.3), channel_id=1, replica_groups=mesh['dp'=8,'expert'=32] {'expert'}, dimensions={0} | all-to-all | bytes 6553600 | tf_op jit(solution)/shard_map/all_to_all | solution.py:87
  200.1 2.9 %fusion.26 = bf16[128,2048]{1,0:T(8,128)(2,1)} fusion(pred[32,25,128]{2,0,1:T(8,128)(4,1)S(1)} %get-tuple-element.17, bf16[32,25,2048]{2,1,0:T(8,128)(2,1)S(1)} %all_to_all.15), kind=kOutput, calls=%fused_computation.36 | convolution fusion | flops 419692544 | bytes 3903488 | tf_op jit(solution)/shard_map/dot_general | solution.py:95
  203.0 10.1 %reduce-scatter.3.cloned.1.call-done = bf16[256,1408]{0,1:T(8,128)(2,1)} async-done(((bf16[2048,1408]{0,1:T(8,128)(2,1)}), bf16[256,1408]{0,1:T(8,128)(2,1)}) %reduce-scatter.3.cloned.1.call-update) | async-done | bytes 720912 | tf_op jit(solution)/shard_map/reduce_scatter | solution.py:93
  213.1 2.3 %maximum_bitcast_fusion = bf16[1,256,2112]{1,2,0:T(8,128)(2,1)} fusion(bf16[256,704]{0,1:T(8,128)(2,1)} %reduce-scatter.5.cloned.1.call-done, bf16[256,1408]{0,1:T(8,128)(2,1)} %reduce-scatter.3.cloned.1.call-done), kind=kLoop, calls=%fused_computation.46 | loop fusion | flops 2162688 | bytes 2162688 | tf_op jit(solution)/shard_map/broadcast_in_dim | solution.py:98
  (44 shorter events, 6.6 us)
Async XLA Ops:
  7.2 83.1 %copy-start = (bf16[1,704,2048]{2,1,0:T(8,128)(2,1)S(1)}, bf16[1,704,2048]{2,1,0:T(8,128)(2,1)}, u32[]{:S(2)}) copy-start(bf16[1,704,2048]{2,1,0:T(8,128)(2,1)} %param.14) | copy-start | bytes 8650756
  15.6 8.8 %copy-start.9 = (s32[8]{0:T(128)S(1)}, s32[8]{0:T(128)}, u32[]{:S(2)}) copy-start(s32[8]{0:T(128)} %param.12) | copy-start | bytes 100
  15.6 59.0 %all-to-all-start = ((bf16[32,25,2048]{2,1,0:T(8,128)(2,1)}), bf16[32,25,2048]{2,1,0:T(8,128)(2,1)}, u32[]{:S(2)}, u32[]{:S(2)}) async-start(bf16[32,25,2048]{2,1,0:T(8,128)(2,1)} %multiply_convert_fusion.1), calls=%async_computation | async-start | bytes 8388608 | tf_op jit(solution)/shard_map/all_to_all | solution.py:61
  24.4 178.6 %reduce-scatter.5.cloned.1.call-start = ((), (), s32[]{:S(2)}) async-start(), calls=%async_computation.6 | async-start | bytes 3244032 | tf_op jit(solution)/shard_map/reduce_scatter | solution.py:70
  36.0 3.0 %copy-start.2 = (bf16[800,16,128]{2,1,0:T(8,128)(2,1)S(1)}, bf16[800,16,128]{2,1,0:T(8,128)(2,1)}, u32[]{:S(2)}) copy-start(bf16[800,16,128]{2,1,0:T(8,128)(2,1)} %gather_fusion) | copy-start | bytes 9830404
  38.9 5.2 %copy-start.3 = (bf16[32,25,704]{2,1,0:T(8,128)(2,1)}, bf16[32,25,704]{2,1,0:T(8,128)(2,1)S(1)}, u32[]{:S(2)}) copy-start(bf16[32,25,704]{2,1,0:T(8,128)(2,1)S(1)} %get-tuple-element.20) | copy-start | bytes 3379204
  38.9 5.2 %copy-start.4 = (bf16[32,25,704]{2,1,0:T(8,128)(2,1)}, bf16[32,25,704]{2,1,0:T(8,128)(2,1)S(1)}, u32[]{:S(2)}) copy-start(bf16[32,25,704]{2,1,0:T(8,128)(2,1)S(1)} %get-tuple-element.21) | copy-start | bytes 3379204
  82.1 48.6 %all-to-all-start.1 = ((bf16[32,400,128]{2,1,0:T(8,128)(2,1)}), bf16[32,400,128]{2,1,0:T(8,128)(2,1)}, u32[]{:S(2)}, u32[]{:S(2)}) async-start(bf16[32,400,128]{2,1,0:T(8,128)(2,1)} %bitcast_select_fusion), calls=%async_computation.1 | async-start | bytes 6553600 | tf_op jit(solution)/shard_map/all_to_all | solution.py:63
  90.1 123.0 %reduce-scatter.3.cloned.1.call-start = ((), (), s32[]{:S(2)}) async-start(), calls=%async_computation.5 | async-start | bytes 6488064 | tf_op jit(solution)/shard_map/reduce_scatter | solution.py:93
  101.5 1.0 copy-start.5
  104.9 3.6 %copy-start.6 = (bf16[32,25,704]{2,0,1:T(8,128)(2,1)S(1)}, bf16[32,25,704]{2,0,1:T(8,128)(2,1)}, u32[]{:S(2)}) copy-start(bf16[32,25,704]{2,0,1:T(8,128)(2,1)} %copy-done.5) | copy-start | bytes 3379204
  110.6 20.2 %copy-start.7 = (bf16[800,704]{1,0:T(8,128)(2,1)S(1)}, bf16[800,704]{1,0:T(8,128)(2,1)}, u32[]{:S(2)}) copy-start(bf16[800,704]{1,0:T(8,128)(2,1)} %concatenate.16) | copy-start | bytes 3379204
  110.6 20.2 %copy-start.8 = (bf16[800,704]{1,0:T(8,128)(2,1)S(1)}, bf16[800,704]{1,0:T(8,128)(2,1)}, u32[]{:S(2)}) copy-start(bf16[800,704]{1,0:T(8,128)(2,1)} %concatenate.17) | copy-start | bytes 3379204
  142.1 73.3 %copy-start.1 = (bf16[1,704,2048]{2,1,0:T(8,128)(2,1)S(1)}, bf16[1,704,2048]{2,1,0:T(8,128)(2,1)}, u32[]{:S(2)}) copy-start(bf16[1,704,2048]{2,1,0:T(8,128)(2,1)} %param.14) | copy-start | bytes 8650756
Sparse Core Ops, SparseCore 0:
  82.2 42.9 reduce-scatter.4
  142.2 70.8 reduce-scatter.2

commit v9 on v8

--- a/solution.py
+++ b/solution.py
@@ -41,10 +41,13 @@
     gate_slot = jnp.sum(jnp.where(sel, gate_weights[None, None, :, :], 0.0), axis=(2, 3))
 
     pick = (((2,), (0,)), ((), ()))
-    og_slot = lax.dot_general(tok_sel_b, out_grad, pick, preferred_element_type=f32)
-    s_send = (gate_slot[:, :, None] * og_slot).astype(bf16)
     lanes = 128
     rows = tokens.shape[1] // lanes
+    slot_count = groups * capacity
+    og3 = out_grad.reshape(tok_count, rows, lanes)
+    og_slot = lax.dot_general(tok_sel_b, og3, pick, preferred_element_type=f32)
+    s_send = (gate_slot[:, :, None, None] * og_slot).astype(bf16)
+    s_send = s_send.reshape(groups, capacity * rows, lanes)
     slot_tok = jnp.sum(jnp.where(tok_sel, jnp.arange(tok_count, dtype=jnp.int32), 0), axis=2)
     filled = jnp.any(tok_sel, axis=2).reshape(-1)
     tok3 = tokens.reshape(tok_count, rows, lanes)
@@ -52,23 +55,33 @@
     x_send = x_send.reshape(groups, capacity * rows, lanes)
 
     saved3 = saved.reshape(groups, capacity, 2 * hidden_units)
+    saved_rows = saved.reshape(slot_count, 2 * hidden_units)
+    gate_rows = saved_rows[:, :hidden_units].astype(f32)
+    activated_rows = gate_rows * jax.nn.sigmoid(gate_rows)
+    hidden_rows = (activated_rows * saved_rows[:, hidden_units:].astype(f32)).astype(bf16)
+
+    s_recv = lax.all_to_all(row_major(s_send), "expert", 0, 0, tiled=True)
+    x_send, s_recv, hidden_rows, saved3 = lax.optimization_barrier(
+        (x_send, s_recv, hidden_rows, saved3)
+    )
+    x_recv = lax.all_to_all(row_major(x_send), "expert", 0, 0, tiled=True)
+
+    trained_flag = jnp.any(trained == lax.axis_index("expert")).astype(f32)
+    over_slots = (((0, 1), (0, 1)), ((), ()))
+    grad_down = lax.dot_general(
+        s_recv.reshape(slot_count, rows, lanes), hidden_rows, (((0,), (0,)), ((), ())),
+        preferred_element_type=f32,
+    )
+    down_part = (grad_down.reshape(rows * lanes, hidden_units) * trained_flag).astype(bf16)
+    down_part = col_major(down_part)
+    down_part, s_recv = lax.optimization_barrier((down_part, s_recv))
+    s_recv = s_recv.reshape(groups, capacity, rows * lanes)
+    down_block = lax.psum_scatter(down_part, "dp", scatter_dimension=0, tiled=True)
+
     gate_pre = saved3[:, :, :hidden_units].astype(f32)
     up_pre = saved3[:, :, hidden_units:].astype(f32)
     sigmoid_gate = jax.nn.sigmoid(gate_pre)
     activated = gate_pre * sigmoid_gate
-    hidden = (activated * up_pre).astype(bf16)
-
-    s_recv = lax.all_to_all(row_major(s_send), "expert", 0, 0, tiled=True)
-    x_send, s_recv, hidden = lax.optimization_barrier((x_send, s_recv, hidden))
-    x_recv = lax.all_to_all(row_major(x_send), "expert", 0, 0, tiled=True)
-
-    trained_flag = jnp.any(trained == lax.axis_index("expert")).astype(f32)
-    over_slots = (((0, 1), (0, 1)), ((), ()))
-    grad_down = lax.dot_general(s_recv, hidden, over_slots, preferred_element_type=f32)
-    down_part = col_major((grad_down * trained_flag).astype(bf16))
-    down_part, s_recv = lax.optimization_barrier((down_part, s_recv))
-    down_block = lax.psum_scatter(down_part, "dp", scatter_dimension=0, tiled=True)
-
     hidden_grad = lax.dot_general(
         s_recv, w_down[0], (((2,), (1,)), ((), ())), preferred_element_type=f32
     )

time: 223 us -> 214 us (0.960)
  waiting for transfers between devices: 47.1 us -> 33.6 us
  local copies, waits for them, and re-layouts: 21 us -> 30.4 us
  matrix products: 48.5 us -> 41.6 us
    all_to_all x1, waiting for transfers between devices: 27.9 us -> 19.3 us  [per_device(): s_recv = lax.all_to_all(row_major(s_send), 'expert', 0, 0, tiled=True)]
    reshape x0 -> x1, local copies, waits for them, and re-layouts: none -> 6.57 us  [per_device(): s_recv = s_recv.reshape(groups, capacity, rows * lanes)]
    all_to_all x1, waiting for transfers between devices: 9.01 us -> 4.18 us  [per_device(): x_recv = lax.all_to_all(row_major(x_send), 'expert', 0, 0, tiled=True)]
    dot_general x1, matrix products: 11.1 us -> 6.54 us  [per_device(): lax.dot_general(s_recv, w_down[0], (((2,), (1,)), ((), ())), preferred_el...]
    convert_element_type x0 -> x1, local copies, waits for them, and re-layouts: none -> 3.02 us  [per_device(): s_send = (gate_slot[:, :, None, None] * og_slot).astype(bf16)]
    slice x1 -> x0, local copies, waits for them, and re-layouts: 2.92 us -> none  [per_device(): gate_pre = saved3[:, :, :hidden_units].astype(f32)]
    optimization_barrier x0 -> x1, local copies, waits for them, and re-layouts: none -> 2.66 us  [per_device(): lax.optimization_barrier((x_send, s_recv, hidden_rows, saved3))]
    dot_general x2, matrix products: 11.7 us -> 9.12 us  [the longest x1 7.08 us: per_device(): lax.dot_general(s_recv.reshape(slot_count, rows, lanes), hidden_rows, (((...]
  transfers between devices with their start and end apart: 4 -> 4, of which waited for: 3 -> 3; matrix products, arithmetic and copies ran while one was open for 30% -> 33% of each run, Pallas kernels for 0% -> 0%
where the time goes in v9:
time: 214 us; the launch traced here: 213 us
  blocking collectives  58 us (27%)
  matrix products  41.6 us (19%)
  waiting for transfers between devices  33.6 us (16%)
  local copies, waits for them, and re-layouts  30.4 us (14%)
  other arithmetic  17.7 us (8%)
  starting transfers between devices  16.5 us (8%)
  between operations  14.9 us (7%)
    all_to_all x1, blocking collectives, per_device(): arrived = lax.all_to_all(row_major(slot_grads), 'expert', 0, 0, tiled=True)  58 us
    all_to_all x1, waiting for transfers between devices, per_device(): s_recv = lax.all_to_all(row_major(s_send), 'expert', 0, 0, tiled=True)  19.3 us
    dot_general x1, matrix products, per_device(): lax.dot_general(x_rows, pre_rows, (((0,), (0,)), ((), ())), preferred_ele...  11.5 us
    dot_general x1, matrix products, per_device(): lax.dot_general(pre_grad, w_in[0], (((2,), (1,)), ((), ())), preferred_el...  11.2 us
    reduce_scatter x1, waiting for transfers between devices, per_device(): in_block = lax.psum_scatter(in_part, 'dp', scatter_dimension=0, tiled=True)  10.1 us
    all_to_all x1, starting transfers between devices, per_device(): s_recv = lax.all_to_all(row_major(s_send), 'expert', 0, 0, tiled=True)  8.77 us
    all_to_all x1, starting transfers between devices, per_device(): x_recv = lax.all_to_all(row_major(x_send), 'expert', 0, 0, tiled=True)  7.43 us
    select_n x1, other arithmetic, per_device(): jnp.where(filled[:, None, None], tok3[slot_tok.reshape(-1)], jnp.zeros(()...  7.42 us
  transfers between devices with their start and end apart: 4, of which 3 were waited for; matrix products, arithmetic and copies ran while one was open for 33% of the time, Pallas kernels for 0%

profile of v9, /device:TPU:1, one launch (start us, length us, event | category | flops | bytes accessed | tf_op | source)
XLA Modules:
  0.0 212.6 jit_solution(135562716666429703)
XLA Ops:
  11.3 2.0 multiply_convert_fusion.1
  13.3 3.0 %copy.66 = bf16[32,25,16,128]{3,2,1,0:T(8,128)(2,1)} copy(bf16[32,25,16,128]{3,0,2,1:T(8,128)(2,1)S(1)} %multiply_convert_fusion.1) | data formatting | bytes 6553600 | tf_op jit(solution)/shard_map/convert_element_type | solution.py:49
  16.3 8.8 %all-to-all-start = ((bf16[32,400,128]{2,1,0:T(8,128)(2,1)}), bf16[32,400,128]{2,1,0:T(8,128)(2,1)}, u32[]{:S(2)}, u32[]{:S(2)}) async-start(bf16[32,400,128]{2,1,0:T(8,128)(2,1)} %bitcast.64), calls=%async_computation | async-start | bytes 6553600 | tf_op jit(solution)/shard_map/all_to_all | solution.py:63
  28.5 4.3 %reshape.105 = bf16[32,25,1408]{2,1,0:T(8,128)(2,1)} reshape(bf16[1,1,800,1408]{3,2,1,0:T(8,128)(2,1)} %param.15) | data formatting | bytes 4505600 | tf_op jit(solution)/shard_map/reshape | solution.py:57
  32.9 3.9 %gather_fusion = bf16[800,16,128]{2,1,0:T(8,128)(2,1)} fusion(bf16[128,16,128]{2,1,0:T(8,128)(2,1)S(1)} %bitcast.63, s32[1024]{0:T(1024)S(1)} %pad_clamp_fusion), kind=kCustom, calls=%fused_computation | custom fusion | bytes 6556800 | tf_op jit(solution)/shard_map/gather | solution.py:54
  36.8 7.4 %bitcast_select_fusion = bf16[32,400,128]{2,1,0:T(8,128)(2,1)} fusion(pred[32,400]{1,0:T(8,128)(4,1)S(1)} %copy.63, bf16[32,400,128]{2,1,0:T(8,128)(2,1)} %bitcast.65), kind=kLoop, calls=%fused_computation.17 | loop fusion | flops 1638400 | bytes 6566400 | tf_op jit(solution)/shard_map/jit(_where)/select_n | solution.py:54
  44.2 2.2 %fusion.31 = bf16[800,704]{1,0:T(8,128)(2,1)} fusion(bf16[800,1408]{1,0:T(8,128)(2,1)S(1)} %bitcast.66), kind=kLoop, calls=%fused_computation.40 | loop fusion | flops 4505600 | bytes 3379200 | tf_op jit(solution)/shard_map/convert_element_type | solution.py:61
  46.4 19.3 %all-to-all-done = bf16[32,400,128]{2,1,0:T(8,128)(2,1)} async-done(((bf16[32,400,128]{2,1,0:T(8,128)(2,1)}), bf16[32,400,128]{2,1,0:T(8,128)(2,1)}, u32[]{:S(2)}, u32[]{:S(2)}) %all-to-all-start) | async-done | bytes 3276832 | tf_op jit(solution)/shard_map/all_to_all | solution.py:63
  65.7 7.1 %multiply_convert_fusion.2 = bf16[2048,704]{0,1:T(8,128)(2,1)} fusion(bf16[800,704]{1,0:T(8,128)(2,1)} %fusion.31, bf16[100,8,16,128]{3,2,1,0:T(8,128)(2,1)} %bitcast.26, f32[]{:T(128)S(6)} %convert_element_type.61), kind=kOutput, calls=%fused_computation.5 | convolution fusion | flops 2309750784 | bytes 7286788 | tf_op jit(solution)/shard_map/dot_general | solution.py:71
  72.8 7.4 %all-to-all-start.1 = ((bf16[32,400,128]{2,1,0:T(8,128)(2,1)}), bf16[32,400,128]{2,1,0:T(8,128)(2,1)}, u32[]{:S(2)}, u32[]{:S(2)}) async-start(bf16[32,400,128]{2,1,0:T(8,128)(2,1)} %bitcast_select_fusion), calls=%async_computation.1 | async-start | bytes 6553600 | tf_op jit(solution)/shard_map/all_to_all | solution.py:67
  80.4 6.6 %reshape.107 = bf16[32,25,2048]{2,1,0:T(8,128)(2,1)} reshape(bf16[32,400,128]{2,1,0:T(8,128)(2,1)} %all-to-all-done) | data formatting | bytes 6553600 | tf_op jit(solution)/shard_map/reshape | solution.py:78
  87.0 2.7 %copy.68 = bf16[32,25,1408]{2,0,1:T(8,128)(2,1)S(1)} copy(bf16[32,25,1408]{2,1,0:T(8,128)(2,1)} %reshape.105) | data formatting | bytes 4505600 | tf_op jit(solution)/shard_map/optimization_barrier | solution.py:64
  90.1 6.5 %fusion.27 = (bf16[32,25,704]{2,0,1:T(8,128)(2,1)S(1)}, bf16[32,25,704]{2,0,1:T(8,128)(2,1)}) fusion(bf16[32,25,1408]{2,0,1:T(8,128)(2,1)S(1)} %copy.68, bf16[1,704,2048]{2,1,0:T(8,128)(2,1)S(1)} %copy-done, bf16[32,25,2048]{2,1,0:T(8,128)(2,1)S(1)} %copy-done.5), kind=kOutput, calls=%fused_computation.36 | convolution fusion | flops 2315315200 | bytes 10665984 | tf_op jit(solution)/shard_map/dot_general | solution.py:85
  98.4 1.5 concatenate.16
  99.9 2.1 copy.73
  102.0 1.5 concatenate.17
  103.5 2.0 pad_maximum_fusion
  105.5 11.2 %fusion.2 = bf16[32,25,2048]{2,1,0:T(8,128)(2,1)} fusion(bf16[1,2048,1408]{2,1,0:T(8,128)(2,1)} %param.13, bf16[32,25,1408]{2,0,1:T(8,128)(2,1)S(1)} %pad_maximum_fusion), kind=kOutput, calls=%fused_computation.6 | convolution fusion | flops 4615372800 | bytes 11296768 | tf_op jit(solution)/shard_map/dot_general | solution.py:95
  116.7 4.2 %all-to-all-done.1 = bf16[32,400,128]{2,1,0:T(8,128)(2,1)} async-done(((bf16[32,400,128]{2,1,0:T(8,128)(2,1)}), bf16[32,400,128]{2,1,0:T(8,128)(2,1)}, u32[]{:S(2)}, u32[]{:S(2)}) %all-to-all-start.1) | async-done | bytes 3276832 | tf_op jit(solution)/shard_map/all_to_all | solution.py:67
  120.9 11.5 %multiply_convert_fusion = bf16[2048,1408]{0,1:T(8,128)(2,1)} fusion(f32[]{:T(128)S(6)} %convert_element_type.61, bf16[100,8,16,128]{3,2,1,0:T(8,128)(2,1)} %bitcast.30, bf16[800,704]{1,0:T(8,128)(2,1)S(1)} %copy-done.7, bf16[800,704]{1,0:T(8,128)(2,1)S(1)} %copy-done.6), kind=kOutput, calls=%fused_computation.1 | convolution fusion | flops 4624007168 | bytes 11296772 | tf_op jit(solution)/shard_map/dot_general | solution.py:104
  132.5 58.0 %all_to_all.15 = bf16[32,25,2048]{2,1,0:T(8,128)(2,1)S(1)} all-to-all(bf16[32,25,2048]{2,1,0:T(8,128)(2,1)} %fusion.2), channel_id=1, replica_groups=mesh['dp'=8,'expert'=32] {'expert'}, dimensions={0} | all-to-all | bytes 6553600 | tf_op jit(solution)/shard_map/all_to_all | solution.py:100
  190.4 2.9 %fusion.32 = bf16[128,2048]{1,0:T(8,128)(2,1)} fusion(pred[32,25,128]{2,0,1:T(8,128)(4,1)S(1)} %get-tuple-element.19, bf16[32,25,2048]{2,1,0:T(8,128)(2,1)S(1)} %all_to_all.15), kind=kOutput, calls=%fused_computation.41 | convolution fusion | flops 419692544 | bytes 3903488 | tf_op jit(solution)/shard_map/dot_general | solution.py:108
  193.3 10.1 %reduce-scatter.3.cloned.1.call-done = bf16[256,1408]{0,1:T(8,128)(2,1)} async-done(((bf16[2048,1408]{0,1:T(8,128)(2,1)}), bf16[256,1408]{0,1:T(8,128)(2,1)}) %reduce-scatter.3.cloned.1.call-update) | async-done | bytes 720912 | tf_op jit(solution)/shard_map/reduce_scatter | solution.py:106
  203.5 2.3 %maximum_bitcast_fusion = bf16[1,256,2112]{1,2,0:T(8,128)(2,1)} fusion(bf16[256,704]{0,1:T(8,128)(2,1)} %reduce-scatter.5.cloned.1.call-done, bf16[256,1408]{0,1:T(8,128)(2,1)} %reduce-scatter.3.cloned.1.call-done), kind=kLoop, calls=%fused_computation.50 | loop fusion | flops 2162688 | bytes 2162688 | tf_op jit(solution)/shard_map/broadcast_in_dim | solution.py:111
  (43 shorter events, 9.1 us)
Async XLA Ops:
  7.2 82.5 %copy-start = (bf16[1,704,2048]{2,1,0:T(8,128)(2,1)S(1)}, bf16[1,704,2048]{2,1,0:T(8,128)(2,1)}, u32[]{:S(2)}) copy-start(bf16[1,704,2048]{2,1,0:T(8,128)(2,1)} %param.14) | copy-start | bytes 8650756
  16.3 8.8 %copy-start.8 = (s32[8]{0:T(128)S(1)}, s32[8]{0:T(128)}, u32[]{:S(2)}) copy-start(s32[8]{0:T(128)} %param.12) | copy-start | bytes 100
  16.3 49.3 %all-to-all-start = ((bf16[32,400,128]{2,1,0:T(8,128)(2,1)}), bf16[32,400,128]{2,1,0:T(8,128)(2,1)}, u32[]{:S(2)}, u32[]{:S(2)}) async-start(bf16[32,400,128]{2,1,0:T(8,128)(2,1)} %bitcast.64), calls=%async_computation | async-start | bytes 6553600 | tf_op jit(solution)/shard_map/all_to_all | solution.py:63
  25.1 168.2 %reduce-scatter.5.cloned.1.call-start = ((), (), s32[]{:S(2)}) async-start(), calls=%async_computation.6 | async-start | bytes 3244032 | tf_op jit(solution)/shard_map/reduce_scatter | solution.py:79
  36.8 7.4 %copy-start.2 = (bf16[1,1,800,1408]{3,2,1,0:T(8,128)(2,1)S(1)}, bf16[1,1,800,1408]{3,2,1,0:T(8,128)(2,1)}, u32[]{:S(2)}) copy-start(bf16[1,1,800,1408]{3,2,1,0:T(8,128)(2,1)} %param.15) | copy-start | bytes 6758404
  72.8 48.1 %all-to-all-start.1 = ((bf16[32,400,128]{2,1,0:T(8,128)(2,1)}), bf16[32,400,128]{2,1,0:T(8,128)(2,1)}, u32[]{:S(2)}, u32[]{:S(2)}) async-start(bf16[32,400,128]{2,1,0:T(8,128)(2,1)} %bitcast_select_fusion), calls=%async_computation.1 | async-start | bytes 6553600 | tf_op jit(solution)/shard_map/all_to_all | solution.py:67
  80.2 123.3 %reduce-scatter.3.cloned.1.call-start = ((), (), s32[]{:S(2)}) async-start(), calls=%async_computation.5 | async-start | bytes 6488064 | tf_op jit(solution)/shard_map/reduce_scatter | solution.py:106
  87.0 3.1 %copy-start.5 = (bf16[32,25,2048]{2,1,0:T(8,128)(2,1)S(1)}, bf16[32,25,2048]{2,1,0:T(8,128)(2,1)}, u32[]{:S(2)}) copy-start(bf16[32,25,2048]{2,1,0:T(8,128)(2,1)} %reshape.107) | copy-start | bytes 9830404
  96.6 1.0 copy-start.3
  99.9 3.6 %copy-start.4 = (bf16[32,25,704]{2,0,1:T(8,128)(2,1)S(1)}, bf16[32,25,704]{2,0,1:T(8,128)(2,1)}, u32[]{:S(2)}) copy-start(bf16[32,25,704]{2,0,1:T(8,128)(2,1)} %copy-done.3) | copy-start | bytes 3379204
  105.5 15.4 %copy-start.6 = (bf16[800,704]{1,0:T(8,128)(2,1)S(1)}, bf16[800,704]{1,0:T(8,128)(2,1)}, u32[]{:S(2)}) copy-start(bf16[800,704]{1,0:T(8,128)(2,1)} %concatenate.16) | copy-start | bytes 3379204
  105.5 15.4 %copy-start.7 = (bf16[800,704]{1,0:T(8,128)(2,1)S(1)}, bf16[800,704]{1,0:T(8,128)(2,1)}, u32[]{:S(2)}) copy-start(bf16[800,704]{1,0:T(8,128)(2,1)} %concatenate.17) | copy-start | bytes 3379204
  132.4 73.3 %copy-start.1 = (bf16[1,704,2048]{2,1,0:T(8,128)(2,1)S(1)}, bf16[1,704,2048]{2,1,0:T(8,128)(2,1)}, u32[]{:S(2)}) copy-start(bf16[1,704,2048]{2,1,0:T(8,128)(2,1)} %param.14) | copy-start | bytes 8650756
Sparse Core Ops, SparseCore 0:
  72.9 42.5 reduce-scatter.4
  132.6 70.8 reduce-scatter.2

commit v10 on v9

--- a/solution.py
+++ b/solution.py
@@ -24,21 +24,20 @@
     hidden_units = w_down.shape[1]
     f32, bf16 = jnp.float32, jnp.bfloat16
 
-    flat_ids = expert_ids.reshape(-1)
-    entries = flat_ids.shape[0]
-    onehot = (flat_ids[:, None] == jnp.arange(experts, dtype=jnp.int32)[None, :]).astype(bf16)
-    order = jnp.arange(entries, dtype=jnp.int32)
+    labels = jnp.arange(experts, dtype=jnp.int32)
+    hit = expert_ids[:, :, None] == labels[None, None, :]
+    tok_mask = jnp.any(hit, axis=1)
+    tok_gate = jnp.sum(jnp.where(hit, gate_weights[:, :, None], 0.0), axis=1)
+    order = jnp.arange(tok_count, dtype=jnp.int32)
     earlier = (order[:, None] > order[None, :]).astype(bf16)
-    before = lax.dot_general(earlier, onehot, (((1,), (0,)), ((), ())), preferred_element_type=f32)
-    slot_rank = jnp.sum(before * onehot.astype(f32), axis=1).astype(jnp.int32)
-    ids4 = flat_ids.reshape(1, 1, tok_count, fanout)
-    rank4 = slot_rank.reshape(1, 1, tok_count, fanout)
-    sel = (ids4 == jnp.arange(experts, dtype=jnp.int32)[:, None, None, None]) & (
-        rank4 == jnp.arange(capacity, dtype=jnp.int32)[None, :, None, None]
+    before = lax.dot_general(
+        earlier, tok_mask.astype(bf16), (((1,), (0,)), ((), ())), preferred_element_type=f32
+    ).astype(jnp.int32)
+    tok_sel = tok_mask.T[:, None, :] & (
+        before.T[:, None, :] == jnp.arange(capacity, dtype=jnp.int32)[None, :, None]
     )
-    tok_sel = jnp.any(sel, axis=3)
     tok_sel_b = tok_sel.astype(bf16)
-    gate_slot = jnp.sum(jnp.where(sel, gate_weights[None, None, :, :], 0.0), axis=(2, 3))
+    gate_slot = jnp.sum(jnp.where(tok_sel, tok_gate.T[:, None, :], 0.0), axis=2)
 
     pick = (((2,), (0,)), ((), ()))
     lanes = 128

time: 214 us -> 211 us (0.986)
  no operation moved by 1% of the time
where the time goes in v10:
time: 211 us; the launch traced here: 210 us
  blocking collectives  58 us (27%)
  matrix products  41.4 us (20%)
  waiting for transfers between devices  33 us (16%)
  local copies, waits for them, and re-layouts  29.3 us (14%)
  other arithmetic  17.4 us (8%)
  starting transfers between devices  16.5 us (8%)
  between operations  14.8 us (7%)
    all_to_all x1, blocking collectives, per_device(): arrived = lax.all_to_all(row_major(slot_grads), 'expert', 0, 0, tiled=True)  58 us
    all_to_all x1, waiting for transfers between devices, per_device(): s_recv = lax.all_to_all(row_major(s_send), 'expert', 0, 0, tiled=True)  18.7 us
    dot_general x1, matrix products, per_device(): lax.dot_general(x_rows, pre_rows, (((0,), (0,)), ((), ())), preferred_ele...  11.5 us
    dot_general x1, matrix products, per_device(): lax.dot_general(pre_grad, w_in[0], (((2,), (1,)), ((), ())), preferred_el...  11.2 us
    reduce_scatter x1, waiting for transfers between devices, per_device(): in_block = lax.psum_scatter(in_part, 'dp', scatter_dimension=0, tiled=True)  10.1 us
    all_to_all x1, starting transfers between devices, per_device(): s_recv = lax.all_to_all(row_major(s_send), 'expert', 0, 0, tiled=True)  8.77 us
    all_to_all x1, starting transfers between devices, per_device(): x_recv = lax.all_to_all(row_major(x_send), 'expert', 0, 0, tiled=True)  7.43 us
    select_n x1, other arithmetic, per_device(): jnp.where(filled[:, None, None], tok3[slot_tok.reshape(-1)], jnp.zeros(()...  7.42 us
  transfers between devices with their start and end apart: 4, of which 3 were waited for; matrix products, arithmetic and copies ran while one was open for 33% of the time, Pallas kernels for 0%

profile of v10, /device:TPU:1, one launch (start us, length us, event | category | flops | bytes accessed | tf_op | source)
XLA Modules:
  0.0 210.4 jit_solution(2094326465684343545)
XLA Ops:
  9.1 2.1 multiply_convert_fusion.1
  11.2 3.0 %copy.61 = bf16[32,25,16,128]{3,2,1,0:T(8,128)(2,1)} copy(bf16[32,25,16,128]{3,0,2,1:T(8,128)(2,1)S(1)} %multiply_convert_fusion.1) | data formatting | bytes 6553600 | tf_op jit(solution)/shard_map/convert_element_type | solution.py:48
  14.2 8.8 %all-to-all-start = ((bf16[32,400,128]{2,1,0:T(8,128)(2,1)}), bf16[32,400,128]{2,1,0:T(8,128)(2,1)}, u32[]{:S(2)}, u32[]{:S(2)}) async-start(bf16[32,400,128]{2,1,0:T(8,128)(2,1)} %bitcast.66), calls=%async_computation | async-start | bytes 6553600 | tf_op jit(solution)/shard_map/all_to_all | solution.py:62
  26.9 4.3 %reshape.86 = bf16[32,25,1408]{2,1,0:T(8,128)(2,1)} reshape(bf16[1,1,800,1408]{3,2,1,0:T(8,128)(2,1)} %param.15) | data formatting | bytes 4505600 | tf_op jit(solution)/shard_map/reshape | solution.py:56
  31.2 3.9 %gather_fusion = bf16[800,16,128]{2,1,0:T(8,128)(2,1)} fusion(bf16[128,16,128]{2,1,0:T(8,128)(2,1)S(1)} %bitcast.65, s32[1024]{0:T(1024)S(1)} %pad_clamp_fusion), kind=kCustom, calls=%fused_computation | custom fusion | bytes 6556800 | tf_op jit(solution)/shard_map/gather | solution.py:53
  35.1 7.4 %bitcast_select_fusion = bf16[32,400,128]{2,1,0:T(8,128)(2,1)} fusion(pred[32,400]{1,0:T(8,128)(4,1)S(1)} %copy.58, bf16[32,400,128]{2,1,0:T(8,128)(2,1)} %bitcast.67), kind=kLoop, calls=%fused_computation.14 | loop fusion | flops 1638400 | bytes 6566400 | tf_op jit(solution)/shard_map/jit(_where)/select_n | solution.py:53
  42.6 2.2 %fusion.30 = bf16[800,704]{1,0:T(8,128)(2,1)} fusion(bf16[800,1408]{1,0:T(8,128)(2,1)S(1)} %bitcast.68), kind=kLoop, calls=%fused_computation.36 | loop fusion | flops 4505600 | bytes 3379200 | tf_op jit(solution)/shard_map/convert_element_type | solution.py:60
  44.8 18.7 %all-to-all-done = bf16[32,400,128]{2,1,0:T(8,128)(2,1)} async-done(((bf16[32,400,128]{2,1,0:T(8,128)(2,1)}), bf16[32,400,128]{2,1,0:T(8,128)(2,1)}, u32[]{:S(2)}, u32[]{:S(2)}) %all-to-all-start) | async-done | bytes 3276832 | tf_op jit(solution)/shard_map/all_to_all | solution.py:62
  63.5 7.1 %multiply_convert_fusion.2 = bf16[2048,704]{0,1:T(8,128)(2,1)} fusion(bf16[800,704]{1,0:T(8,128)(2,1)} %fusion.30, bf16[100,8,16,128]{3,2,1,0:T(8,128)(2,1)} %bitcast.28, f32[]{:T(128)S(6)} %convert_element_type.47), kind=kOutput, calls=%fused_computation.5 | convolution fusion | flops 2309750784 | bytes 7286788 | tf_op jit(solution)/shard_map/dot_general | solution.py:70
  70.6 7.4 %all-to-all-start.1 = ((bf16[32,400,128]{2,1,0:T(8,128)(2,1)}), bf16[32,400,128]{2,1,0:T(8,128)(2,1)}, u32[]{:S(2)}, u32[]{:S(2)}) async-start(bf16[32,400,128]{2,1,0:T(8,128)(2,1)} %bitcast_select_fusion), calls=%async_computation.1 | async-start | bytes 6553600 | tf_op jit(solution)/shard_map/all_to_all | solution.py:66
  78.3 6.6 %reshape.88 = bf16[32,25,2048]{2,1,0:T(8,128)(2,1)} reshape(bf16[32,400,128]{2,1,0:T(8,128)(2,1)} %all-to-all-done) | data formatting | bytes 6553600 | tf_op jit(solution)/shard_map/reshape | solution.py:77
  84.9 2.7 %copy.63 = bf16[32,25,1408]{2,0,1:T(8,128)(2,1)S(1)} copy(bf16[32,25,1408]{2,1,0:T(8,128)(2,1)} %reshape.86) | data formatting | bytes 4505600 | tf_op jit(solution)/shard_map/optimization_barrier | solution.py:63
  87.9 6.5 %fusion.27 = (bf16[32,25,704]{2,0,1:T(8,128)(2,1)S(1)}, bf16[32,25,704]{2,0,1:T(8,128)(2,1)}) fusion(bf16[32,25,1408]{2,0,1:T(8,128)(2,1)S(1)} %copy.63, bf16[1,704,2048]{2,1,0:T(8,128)(2,1)S(1)} %copy-done, bf16[32,25,2048]{2,1,0:T(8,128)(2,1)S(1)} %copy-done.5), kind=kOutput, calls=%fused_computation.33 | convolution fusion | flops 2315315200 | bytes 10665984 | tf_op jit(solution)/shard_map/dot_general | solution.py:84
  96.2 1.5 concatenate.16
  97.7 2.1 copy.68
  99.8 1.5 concatenate.17
  101.4 2.0 pad_maximum_fusion
  103.4 11.2 %fusion.2 = bf16[32,25,2048]{2,1,0:T(8,128)(2,1)} fusion(bf16[1,2048,1408]{2,1,0:T(8,128)(2,1)} %param.13, bf16[32,25,1408]{2,0,1:T(8,128)(2,1)S(1)} %pad_maximum_fusion), kind=kOutput, calls=%fused_computation.6 | convolution fusion | flops 4615372800 | bytes 11296768 | tf_op jit(solution)/shard_map/dot_general | solution.py:94
  114.6 4.2 %all-to-all-done.1 = bf16[32,400,128]{2,1,0:T(8,128)(2,1)} async-done(((bf16[32,400,128]{2,1,0:T(8,128)(2,1)}), bf16[32,400,128]{2,1,0:T(8,128)(2,1)}, u32[]{:S(2)}, u32[]{:S(2)}) %all-to-all-start.1) | async-done | bytes 3276832 | tf_op jit(solution)/shard_map/all_to_all | solution.py:66
  118.7 11.5 %multiply_convert_fusion = bf16[2048,1408]{0,1:T(8,128)(2,1)} fusion(f32[]{:T(128)S(6)} %convert_element_type.47, bf16[100,8,16,128]{3,2,1,0:T(8,128)(2,1)} %bitcast.32, bf16[800,704]{1,0:T(8,128)(2,1)S(1)} %copy-done.7, bf16[800,704]{1,0:T(8,128)(2,1)S(1)} %copy-done.6), kind=kOutput, calls=%fused_computation.1 | convolution fusion | flops 4624007168 | bytes 11296772 | tf_op jit(solution)/shard_map/dot_general | solution.py:103
  130.3 58.0 %all_to_all.15 = bf16[32,25,2048]{2,1,0:T(8,128)(2,1)S(1)} all-to-all(bf16[32,25,2048]{2,1,0:T(8,128)(2,1)} %fusion.2), channel_id=1, replica_groups=mesh['dp'=8,'expert'=32] {'expert'}, dimensions={0} | all-to-all | bytes 6553600 | tf_op jit(solution)/shard_map/all_to_all | solution.py:99
  188.3 2.9 %fusion.31 = bf16[128,2048]{1,0:T(8,128)(2,1)} fusion(bf16[32,25,2048]{2,1,0:T(8,128)(2,1)S(1)} %all_to_all.15, s32[32,128]{1,0:T(8,128)S(1)} %convolution_convert_fusion, pred[32,128]{1,0:T(8,128)(4,1)S(1)} %bitcast.75), kind=kOutput, calls=%fused_computation.37 | convolution fusion | flops 419897344 | bytes 3821568 | tf_op jit(solution)/shard_map/dot_general | solution.py:107
  191.2 10.1 %reduce-scatter.3.cloned.1.call-done = bf16[256,1408]{0,1:T(8,128)(2,1)} async-done(((bf16[2048,1408]{0,1:T(8,128)(2,1)}), bf16[256,1408]{0,1:T(8,128)(2,1)}) %reduce-scatter.3.cloned.1.call-update) | async-done | bytes 720912 | tf_op jit(solution)/shard_map/reduce_scatter | solution.py:105
  201.3 2.3 %maximum_bitcast_fusion = bf16[1,256,2112]{1,2,0:T(8,128)(2,1)} fusion(bf16[256,704]{0,1:T(8,128)(2,1)} %reduce-scatter.5.cloned.1.call-done, bf16[256,1408]{0,1:T(8,128)(2,1)} %reduce-scatter.3.cloned.1.call-done), kind=kLoop, calls=%fused_computation.43 | loop fusion | flops 2162688 | bytes 2162688 | tf_op jit(solution)/shard_map/broadcast_in_dim | solution.py:110
  (38 shorter events, 7.6 us)
Async XLA Ops:
  7.2 80.4 %copy-start = (bf16[1,704,2048]{2,1,0:T(8,128)(2,1)S(1)}, bf16[1,704,2048]{2,1,0:T(8,128)(2,1)}, u32[]{:S(2)}) copy-start(bf16[1,704,2048]{2,1,0:T(8,128)(2,1)} %param.14) | copy-start | bytes 8650756
  14.2 8.8 %copy-start.8 = (s32[8]{0:T(128)S(1)}, s32[8]{0:T(128)}, u32[]{:S(2)}) copy-start(s32[8]{0:T(128)} %param.12) | copy-start | bytes 100
  14.2 49.3 %all-to-all-start = ((bf16[32,400,128]{2,1,0:T(8,128)(2,1)}), bf16[32,400,128]{2,1,0:T(8,128)(2,1)}, u32[]{:S(2)}, u32[]{:S(2)}) async-start(bf16[32,400,128]{2,1,0:T(8,128)(2,1)} %bitcast.66), calls=%async_computation | async-start | bytes 6553600 | tf_op jit(solution)/shard_map/all_to_all | solution.py:62
  23.0 168.3 %reduce-scatter.5.cloned.1.call-start = ((), (), s32[]{:S(2)}) async-start(), calls=%async_computation.6 | async-start | bytes 3244032 | tf_op jit(solution)/shard_map/reduce_scatter | solution.py:78
  35.1 7.4 %copy-start.2 = (bf16[1,1,800,1408]{3,2,1,0:T(8,128)(2,1)S(1)}, bf16[1,1,800,1408]{3,2,1,0:T(8,128)(2,1)}, u32[]{:S(2)}) copy-start(bf16[1,1,800,1408]{3,2,1,0:T(8,128)(2,1)} %param.15) | copy-start | bytes 6758404
  70.6 48.1 %all-to-all-start.1 = ((bf16[32,400,128]{2,1,0:T(8,128)(2,1)}), bf16[32,400,128]{2,1,0:T(8,128)(2,1)}, u32[]{:S(2)}, u32[]{:S(2)}) async-start(bf16[32,400,128]{2,1,0:T(8,128)(2,1)} %bitcast_select_fusion), calls=%async_computation.1 | async-start | bytes 6553600 | tf_op jit(solution)/shard_map/all_to_all | solution.py:66
  78.1 123.2 %reduce-scatter.3.cloned.1.call-start = ((), (), s32[]{:S(2)}) async-start(), calls=%async_computation.5 | async-start | bytes 6488064 | tf_op jit(solution)/shard_map/reduce_scatter | solution.py:105
  84.9 3.1 %copy-start.5 = (bf16[32,25,2048]{2,1,0:T(8,128)(2,1)S(1)}, bf16[32,25,2048]{2,1,0:T(8,128)(2,1)}, u32[]{:S(2)}) copy-start(bf16[32,25,2048]{2,1,0:T(8,128)(2,1)} %reshape.88) | copy-start | bytes 9830404
  94.5 1.0 copy-start.3
  97.7 3.6 %copy-start.4 = (bf16[32,25,704]{2,0,1:T(8,128)(2,1)S(1)}, bf16[32,25,704]{2,0,1:T(8,128)(2,1)}, u32[]{:S(2)}) copy-start(bf16[32,25,704]{2,0,1:T(8,128)(2,1)} %copy-done.3) | copy-start | bytes 3379204
  103.4 15.4 %copy-start.6 = (bf16[800,704]{1,0:T(8,128)(2,1)S(1)}, bf16[800,704]{1,0:T(8,128)(2,1)}, u32[]{:S(2)}) copy-start(bf16[800,704]{1,0:T(8,128)(2,1)} %concatenate.16) | copy-start | bytes 3379204
  103.4 15.4 %copy-start.7 = (bf16[800,704]{1,0:T(8,128)(2,1)S(1)}, bf16[800,704]{1,0:T(8,128)(2,1)}, u32[]{:S(2)}) copy-start(bf16[800,704]{1,0:T(8,128)(2,1)} %concatenate.17) | copy-start | bytes 3379204
  130.3 73.3 %copy-start.1 = (bf16[1,704,2048]{2,1,0:T(8,128)(2,1)S(1)}, bf16[1,704,2048]{2,1,0:T(8,128)(2,1)}, u32[]{:S(2)}) copy-start(bf16[1,704,2048]{2,1,0:T(8,128)(2,1)} %param.14) | copy-start | bytes 8650756
Sparse Core Ops, SparseCore 0:
  70.7 42.4 reduce-scatter.4
  130.4 70.8 reduce-scatter.2

commit v11 on v10

--- a/solution.py
+++ b/solution.py
@@ -107,8 +107,11 @@
     in_grad = lax.dot_general(
         tok_sel_b, arrived, (((0, 1), (0, 1)), ((), ())), preferred_element_type=f32
     ).astype(bf16)
-    weight_block = jnp.concatenate([in_block, down_block], axis=1)[None]
-    weight_block = with_layout_constraint(weight_block, Layout(major_to_minor=(0, 2, 1)))
+    layout = Layout(major_to_minor=(0, 2, 1))
+    frame = jnp.concatenate([jnp.zeros_like(in_block), down_block], axis=1)[None]
+    frame = with_layout_constraint(frame, layout)
+    weight_block = lax.dynamic_update_slice(frame, in_block[None], (0, 0, 0))
+    weight_block = with_layout_constraint(weight_block, layout)
     return (in_grad, weight_block)
 
 

time: 211 us -> 211 us (level)
  blocking collectives: 58 us -> 0 us
  waiting for transfers between devices: 33 us -> 79.1 us
  starting transfers between devices: 16.5 us -> 23.9 us
  local copies, waits for them, and re-layouts: 29.3 us -> 33.5 us
  matrix products: 41.4 us -> 43.7 us
  other arithmetic: 17.4 us -> 15.1 us
    all_to_all x1 -> x0, blocking collectives: 58 us -> none  [per_device(): arrived = lax.all_to_all(row_major(slot_grads), 'expert', 0, 0, tiled=True)]
    all_to_all x0 -> x1, waiting for transfers between devices: none -> 48.2 us  [per_device(): arrived = lax.all_to_all(row_major(slot_grads), 'expert', 0, 0, tiled=True)]
    all_to_all x0 -> x1, starting transfers between devices: none -> 7.44 us  [per_device(): arrived = lax.all_to_all(row_major(slot_grads), 'expert', 0, 0, tiled=True)]
    broadcast_in_dim x1 -> x0, other arithmetic: 2.27 us -> none  [per_device(): weight_block = jnp.concatenate([in_block, down_block], axis=1)[None]]
    dot_general x1, matrix products: 2.94 us -> 5.16 us  [per_device(): lax.dot_general(tok_sel_b, arrived, (((0, 1), (0, 1)), ((), ())), preferr...]
    broadcast_in_dim x0 -> x1, local copies, waits for them, and re-layouts: none -> 2.19 us  [per_device(): jnp.concatenate([jnp.zeros_like(in_block), down_block], axis=1)[None]]
  transfers between devices with their start and end apart: 4 -> 5, of which waited for: 3 -> 4; matrix products, arithmetic and copies ran while one was open for 33% -> 36% of each run, Pallas kernels for 0% -> 0%
where the time goes in v11:
time: 211 us; the launch traced here: 210 us
  waiting for transfers between devices  79.1 us (37%)
  matrix products  43.7 us (21%)
  local copies, waits for them, and re-layouts  33.5 us (16%)
  starting transfers between devices  23.9 us (11%)
  other arithmetic  15.1 us (7%)
  between operations  14.9 us (7%)
    all_to_all x1, waiting for transfers between devices, per_device(): arrived = lax.all_to_all(row_major(slot_grads), 'expert', 0, 0, tiled=True)  48.2 us
    all_to_all x1, waiting for transfers between devices, per_device(): s_recv = lax.all_to_all(row_major(s_send), 'expert', 0, 0, tiled=True)  18.7 us
    dot_general x1, matrix products, per_device(): lax.dot_general(x_rows, pre_rows, (((0,), (0,)), ((), ())), preferred_ele...  11.5 us
    dot_general x1, matrix products, per_device(): lax.dot_general(pre_grad, w_in[0], (((2,), (1,)), ((), ())), preferred_el...  11.2 us
    all_to_all x1, starting transfers between devices, per_device(): s_recv = lax.all_to_all(row_major(s_send), 'expert', 0, 0, tiled=True)  8.77 us
    reduce_scatter x1, waiting for transfers between devices, per_device(): in_block = lax.psum_scatter(in_part, 'dp', scatter_dimension=0, tiled=True)  8.01 us
    all_to_all x1, starting transfers between devices, per_device(): arrived = lax.all_to_all(row_major(slot_grads), 'expert', 0, 0, tiled=True)  7.44 us
    all_to_all x1, starting transfers between devices, per_device(): x_recv = lax.all_to_all(row_major(x_send), 'expert', 0, 0, tiled=True)  7.43 us
  transfers between devices with their start and end apart: 5, of which 4 were waited for; matrix products, arithmetic and copies ran while one was open for 36% of the time, Pallas kernels for 0%

profile of v11, /device:TPU:1, one launch (start us, length us, event | category | flops | bytes accessed | tf_op | source)
XLA Modules:
  0.0 210.2 jit_solution(10819169739101455006)
XLA Ops:
  9.1 2.1 multiply_convert_fusion.1
  11.2 3.0 %copy.61 = bf16[32,25,16,128]{3,2,1,0:T(8,128)(2,1)} copy(bf16[32,25,16,128]{3,0,2,1:T(8,128)(2,1)S(1)} %multiply_convert_fusion.1) | data formatting | bytes 6553600 | tf_op jit(solution)/shard_map/convert_element_type | solution.py:48
  14.2 8.8 %all-to-all-start = ((bf16[32,400,128]{2,1,0:T(8,128)(2,1)}), bf16[32,400,128]{2,1,0:T(8,128)(2,1)}, u32[]{:S(2)}, u32[]{:S(2)}) async-start(bf16[32,400,128]{2,1,0:T(8,128)(2,1)} %bitcast.68), calls=%async_computation | async-start | bytes 6553600 | tf_op jit(solution)/shard_map/all_to_all | solution.py:62
  26.9 4.3 %reshape.86 = bf16[32,25,1408]{2,1,0:T(8,128)(2,1)} reshape(bf16[1,1,800,1408]{3,2,1,0:T(8,128)(2,1)} %param.15) | data formatting | bytes 4505600 | tf_op jit(solution)/shard_map/reshape | solution.py:56
  31.2 3.9 %gather_fusion = bf16[800,16,128]{2,1,0:T(8,128)(2,1)} fusion(bf16[128,16,128]{2,1,0:T(8,128)(2,1)S(1)} %bitcast.67, s32[1024]{0:T(1024)S(1)} %pad_clamp_fusion), kind=kCustom, calls=%fused_computation | custom fusion | bytes 6556800 | tf_op jit(solution)/shard_map/gather | solution.py:53
  35.1 7.4 %bitcast_select_fusion = bf16[32,400,128]{2,1,0:T(8,128)(2,1)} fusion(pred[32,400]{1,0:T(8,128)(4,1)S(1)} %copy.58, bf16[32,400,128]{2,1,0:T(8,128)(2,1)} %bitcast.69), kind=kLoop, calls=%fused_computation.14 | loop fusion | flops 1638400 | bytes 6566400 | tf_op jit(solution)/shard_map/jit(_where)/select_n | solution.py:53
  42.6 2.2 %fusion.30 = bf16[800,704]{1,0:T(8,128)(2,1)} fusion(bf16[800,1408]{1,0:T(8,128)(2,1)S(1)} %bitcast.70), kind=kLoop, calls=%fused_computation.36 | loop fusion | flops 4505600 | bytes 3379200 | tf_op jit(solution)/shard_map/convert_element_type | solution.py:60
  44.8 18.7 %all-to-all-done = bf16[32,400,128]{2,1,0:T(8,128)(2,1)} async-done(((bf16[32,400,128]{2,1,0:T(8,128)(2,1)}), bf16[32,400,128]{2,1,0:T(8,128)(2,1)}, u32[]{:S(2)}, u32[]{:S(2)}) %all-to-all-start) | async-done | bytes 3276832 | tf_op jit(solution)/shard_map/all_to_all | solution.py:62
  63.5 7.1 %multiply_convert_fusion.2 = bf16[2048,704]{0,1:T(8,128)(2,1)} fusion(bf16[800,704]{1,0:T(8,128)(2,1)} %fusion.30, bf16[100,8,16,128]{3,2,1,0:T(8,128)(2,1)} %bitcast.29, f32[]{:T(128)S(6)} %convert_element_type.47), kind=kOutput, calls=%fused_computation.5 | convolution fusion | flops 2309750784 | bytes 7286788 | tf_op jit(solution)/shard_map/dot_general | solution.py:70
  70.6 7.4 %all-to-all-start.1 = ((bf16[32,400,128]{2,1,0:T(8,128)(2,1)}), bf16[32,400,128]{2,1,0:T(8,128)(2,1)}, u32[]{:S(2)}, u32[]{:S(2)}) async-start(bf16[32,400,128]{2,1,0:T(8,128)(2,1)} %bitcast_select_fusion), calls=%async_computation.1 | async-start | bytes 6553600 | tf_op jit(solution)/shard_map/all_to_all | solution.py:66
  78.3 6.6 %reshape.88 = bf16[32,25,2048]{2,1,0:T(8,128)(2,1)} reshape(bf16[32,400,128]{2,1,0:T(8,128)(2,1)} %all-to-all-done) | data formatting | bytes 6553600 | tf_op jit(solution)/shard_map/reshape | solution.py:77
  84.9 2.7 %copy.63 = bf16[32,25,1408]{2,0,1:T(8,128)(2,1)S(1)} copy(bf16[32,25,1408]{2,1,0:T(8,128)(2,1)} %reshape.86) | data formatting | bytes 4505600 | tf_op jit(solution)/shard_map/optimization_barrier | solution.py:63
  87.9 6.5 %fusion.27 = (bf16[32,25,704]{2,0,1:T(8,128)(2,1)S(1)}, bf16[32,25,704]{2,0,1:T(8,128)(2,1)}) fusion(bf16[32,25,1408]{2,0,1:T(8,128)(2,1)S(1)} %copy.63, bf16[1,704,2048]{2,1,0:T(8,128)(2,1)S(1)} %copy-done, bf16[32,25,2048]{2,1,0:T(8,128)(2,1)S(1)} %copy-done.5), kind=kOutput, calls=%fused_computation.33 | convolution fusion | flops 2315315200 | bytes 10665984 | tf_op jit(solution)/shard_map/dot_general | solution.py:84
  97.7 2.1 %copy.68 = bf16[32,25,704]{2,1,0:T(8,128)(2,1)S(1)} copy(bf16[32,25,704]{2,0,1:T(8,128)(2,1)} %get-tuple-element.19) | data formatting | bytes 2252800 | tf_op jit(solution)/shard_map/convert.5
  101.4 2.0 pad_maximum_fusion
  103.4 11.2 %fusion.2 = bf16[32,25,2048]{2,1,0:T(8,128)(2,1)} fusion(bf16[1,2048,1408]{2,1,0:T(8,128)(2,1)} %param.13, bf16[32,25,1408]{2,0,1:T(8,128)(2,1)S(1)} %pad_maximum_fusion), kind=kOutput, calls=%fused_computation.6 | convolution fusion | flops 4615372800 | bytes 11296768 | tf_op jit(solution)/shard_map/dot_general | solution.py:94
  114.6 4.2 %all-to-all-done.1 = bf16[32,400,128]{2,1,0:T(8,128)(2,1)} async-done(((bf16[32,400,128]{2,1,0:T(8,128)(2,1)}), bf16[32,400,128]{2,1,0:T(8,128)(2,1)}, u32[]{:S(2)}, u32[]{:S(2)}) %all-to-all-start.1) | async-done | bytes 3276832 | tf_op jit(solution)/shard_map/all_to_all | solution.py:66
  118.7 11.5 %multiply_convert_fusion = bf16[2048,1408]{0,1:T(8,128)(2,1)} fusion(f32[]{:T(128)S(6)} %convert_element_type.47, bf16[100,8,16,128]{3,2,1,0:T(8,128)(2,1)} %bitcast.33, bf16[800,704]{1,0:T(8,128)(2,1)S(1)} %copy-done.7, bf16[800,704]{1,0:T(8,128)(2,1)S(1)} %copy-done.6), kind=kOutput, calls=%fused_computation.1 | convolution fusion | flops 4624007168 | bytes 11296772 | tf_op jit(solution)/shard_map/dot_general | solution.py:103
  130.3 7.4 %all-to-all-start.2 = ((bf16[32,25,2048]{2,1,0:T(8,128)(2,1)}), bf16[32,25,2048]{2,1,0:T(8,128)(2,1)}, u32[]{:S(2)}, u32[]{:S(2)}) async-start(bf16[32,25,2048]{2,1,0:T(8,128)(2,1)} %fusion.2), calls=%async_computation.2 | async-start | bytes 8388608 | tf_op jit(solution)/shard_map/all_to_all | solution.py:99
  137.8 2.2 %pad_bitcast_fusion = bf16[1,256,2112]{1,2,0:T(8,128)(2,1)} fusion(bf16[256,704]{0,1:T(8,128)(2,1)} %reduce-scatter.3.cloned.1.call-done), kind=kLoop, calls=%fused_computation.43 | loop fusion | bytes 1441792 | tf_op jit(solution)/shard_map/broadcast_in_dim | solution.py:111
  140.0 48.2 %all-to-all-done.2 = bf16[32,25,2048]{2,1,0:T(8,128)(2,1)} async-done(((bf16[32,25,2048]{2,1,0:T(8,128)(2,1)}), bf16[32,25,2048]{2,1,0:T(8,128)(2,1)}, u32[]{:S(2)}, u32[]{:S(2)}) %all-to-all-start.2) | async-done | bytes 3276832 | tf_op jit(solution)/shard_map/all_to_all | solution.py:99
  188.1 5.2 %fusion.31 = bf16[128,2048]{1,0:T(8,128)(2,1)} fusion(bf16[32,25,2048]{2,1,0:T(8,128)(2,1)} %all-to-all-done.2, s32[32,128]{1,0:T(8,128)S(1)} %convolution_convert_fusion, pred[32,128]{1,0:T(8,128)(4,1)S(1)} %bitcast.77), kind=kOutput, calls=%fused_computation.37 | convolution fusion | flops 419897344 | bytes 3821568 | tf_op jit(solution)/shard_map/dot_general | solution.py:107
  193.3 8.0 %reduce-scatter.5.cloned.1.call-done = bf16[256,1408]{0,1:T(8,128)(2,1)} async-done(((bf16[2048,1408]{0,1:T(8,128)(2,1)}), bf16[256,1408]{0,1:T(8,128)(2,1)}) %reduce-scatter.5.cloned.1.call-update) | async-done | bytes 720912 | tf_op jit(solution)/shard_map/reduce_scatter | solution.py:105
  201.3 2.0 bitcast_dynamic-update-slice_fusion
  (40 shorter events, 10.6 us)
Async XLA Ops:
  7.2 80.4 %copy-start = (bf16[1,704,2048]{2,1,0:T(8,128)(2,1)S(1)}, bf16[1,704,2048]{2,1,0:T(8,128)(2,1)}, u32[]{:S(2)}) copy-start(bf16[1,704,2048]{2,1,0:T(8,128)(2,1)} %param.14) | copy-start | bytes 8650756
  14.2 8.8 %copy-start.8 = (s32[8]{0:T(128)S(1)}, s32[8]{0:T(128)}, u32[]{:S(2)}) copy-start(s32[8]{0:T(128)} %param.12) | copy-start | bytes 100
  14.2 49.3 %all-to-all-start = ((bf16[32,400,128]{2,1,0:T(8,128)(2,1)}), bf16[32,400,128]{2,1,0:T(8,128)(2,1)}, u32[]{:S(2)}, u32[]{:S(2)}) async-start(bf16[32,400,128]{2,1,0:T(8,128)(2,1)} %bitcast.68), calls=%async_computation | async-start | bytes 6553600 | tf_op jit(solution)/shard_map/all_to_all | solution.py:62
  23.0 114.8 %reduce-scatter.3.cloned.1.call-start = ((), (), s32[]{:S(2)}) async-start(), calls=%async_computation.5 | async-start | bytes 3244032 | tf_op jit(solution)/shard_map/reduce_scatter | solution.py:78
  35.1 7.4 %copy-start.2 = (bf16[1,1,800,1408]{3,2,1,0:T(8,128)(2,1)S(1)}, bf16[1,1,800,1408]{3,2,1,0:T(8,128)(2,1)}, u32[]{:S(2)}) copy-start(bf16[1,1,800,1408]{3,2,1,0:T(8,128)(2,1)} %param.15) | copy-start | bytes 6758404
  70.6 48.1 %all-to-all-start.1 = ((bf16[32,400,128]{2,1,0:T(8,128)(2,1)}), bf16[32,400,128]{2,1,0:T(8,128)(2,1)}, u32[]{:S(2)}, u32[]{:S(2)}) async-start(bf16[32,400,128]{2,1,0:T(8,128)(2,1)} %bitcast_select_fusion), calls=%async_computation.1 | async-start | bytes 6553600 | tf_op jit(solution)/shard_map/all_to_all | solution.py:66
  78.1 123.2 %reduce-scatter.5.cloned.1.call-start = ((), (), s32[]{:S(2)}) async-start(), calls=%async_computation.6 | async-start | bytes 6488064 | tf_op jit(solution)/shard_map/reduce_scatter | solution.py:105
  84.9 3.1 %copy-start.5 = (bf16[32,25,2048]{2,1,0:T(8,128)(2,1)S(1)}, bf16[32,25,2048]{2,1,0:T(8,128)(2,1)}, u32[]{:S(2)}) copy-start(bf16[32,25,2048]{2,1,0:T(8,128)(2,1)} %reshape.88) | copy-start | bytes 9830404
  94.5 1.0 copy-start.3
  97.7 3.6 %copy-start.4 = (bf16[32,25,704]{2,0,1:T(8,128)(2,1)S(1)}, bf16[32,25,704]{2,0,1:T(8,128)(2,1)}, u32[]{:S(2)}) copy-start(bf16[32,25,704]{2,0,1:T(8,128)(2,1)} %copy-done.3) | copy-start | bytes 3379204
  103.4 15.4 %copy-start.6 = (bf16[800,704]{1,0:T(8,128)(2,1)S(1)}, bf16[800,704]{1,0:T(8,128)(2,1)}, u32[]{:S(2)}) copy-start(bf16[800,704]{1,0:T(8,128)(2,1)} %concatenate.17) | copy-start | bytes 3379204
  103.4 15.4 %copy-start.7 = (bf16[800,704]{1,0:T(8,128)(2,1)S(1)}, bf16[800,704]{1,0:T(8,128)(2,1)}, u32[]{:S(2)}) copy-start(bf16[800,704]{1,0:T(8,128)(2,1)} %concatenate.18) | copy-start | bytes 3379204
  130.3 57.8 %all-to-all-start.2 = ((bf16[32,25,2048]{2,1,0:T(8,128)(2,1)}), bf16[32,25,2048]{2,1,0:T(8,128)(2,1)}, u32[]{:S(2)}, u32[]{:S(2)}) async-start(bf16[32,25,2048]{2,1,0:T(8,128)(2,1)} %fusion.2), calls=%async_computation.2 | async-start | bytes 8388608 | tf_op jit(solution)/shard_map/all_to_all | solution.py:99
  137.8 65.5 %copy-start.1 = (bf16[1,704,2048]{2,1,0:T(8,128)(2,1)S(1)}, bf16[1,704,2048]{2,1,0:T(8,128)(2,1)}, u32[]{:S(2)}) copy-start(bf16[1,704,2048]{2,1,0:T(8,128)(2,1)} %param.14) | copy-start | bytes 8650756
Sparse Core Ops, SparseCore 0:
  70.7 42.4 reduce-scatter.2
  130.4 70.8 reduce-scatter.4
